TPU v7x, 256 devices: a whole 4x4x8 slice. The times are simulated.
256 devices in a mesh: orb: 64 (over y, z, core), rep: 4 (over x).
Axes of the slice: x: 4, y: 4, z: 8, core: 2. Of those that a mesh axis runs over, the one named last changes fastest.
Arguments:
- blocks: bfloat16 [128, 1024, 512], P('orb', 'rep'), may hold values from -1.078125 to 1.078125
- amplitudes: bfloat16 [512, 512, 512], P('orb', 'rep'), may hold values from -3 to 3
- pair_orbitals: int32 [512, 2], P('orb'), may hold values from 0 to 127, as said below
- coupling: int32 [512, 4], P('orb'), may hold values from 0 to 511, as said below
- fock_coupling: bfloat16 [512, 4], P('orb'), may hold values from -0.5 to 0.5
- virtual_energy: float32 [512], replicated, may hold values from 0.3 to 2
- occupied_energy: float32 [128], replicated, may hold values from -1.5 to -0.1
Outputs:
- updated_amplitudes: bfloat16 [512, 512, 512], P('orb', 'rep')
Inputs may be any that keep to these rules, and one draw needn't show every extreme that they name: `pair_orbitals`: orbital o lives on owner o // 2 and pair p on owner p // 8. A pair's first orbital lies on the pair's owner; its second lies on the same owner or the next one. `coupling`: every coupled pair lies on the pair's owner or on an adjacent owner.
All inputs are finite; a program needn't handle non-finite values.
Results may differ from a plain program's by a relative error of at most 0.01.
Values may be sent and summed in bfloat16 or wider, within the bound.
No kernel may reach another device: no remote copies, remote signals or barrier semaphores. Data moves between devices by JAX's collectives and lax.ppermute only.
A program may use at most 64 MiB of HBM per device.

v0:
```python
import jax
import jax.numpy as jnp
from jax import lax
from jax.sharding import PartitionSpec as P

damping = 0.7


def passed_along(block, axis, distance):
    devices = range(lax.axis_size(axis))
    route = [(i - distance, i) for i in devices if i - distance in devices]
    return lax.ppermute(block, axis, route)


def extended_2(x, sides, width):
    for axis, dim in sides:
        peers, length = (lax.axis_size(axis), x.shape[dim])
        up = [(i, (i + 1) % peers) for i in range(peers - 1)]
        down = [(j, i) for i, j in up]
        last = lax.slice_in_dim(x, length - width, length, axis=dim)
        leading = lax.slice_in_dim(x, 0, width, axis=dim)
        before = lax.ppermute(last, axis, up)
        after = lax.ppermute(leading, axis, down)
        x = jnp.concatenate([before, x, after], axis=dim)
    return x


def per_device(
    blocks, amplitudes, pair_orbitals, coupling, fock_coupling, virtual_energy, occupied_energy
):
    orbital_count = blocks.shape[0]
    pair_count = amplitudes.shape[0]
    row_count = amplitudes.shape[1]
    owner_index = lax.axis_index("orb")
    replica_index = lax.axis_index("rep")
    first_local = pair_orbitals[:, 0] - owner_index * orbital_count
    second_local = pair_orbitals[:, 1] - owner_index * orbital_count
    next_blocks = passed_along(blocks, "orb", -1)
    extended = jnp.concatenate([blocks, next_blocks], axis=0)
    combos = jnp.einsum("iqa,jqb->ijab", blocks, extended, preferred_element_type=jnp.float32)
    partial_value = combos[first_local, second_local]
    integrals = lax.psum_scatter(
        partial_value.astype(jnp.bfloat16), "rep", scatter_dimension=1, tiled=True
    ).astype(jnp.float32)
    amp_extended = extended_2(amplitudes, (("orb", 0),), pair_count)
    coupled_local = coupling - (owner_index - 1) * pair_count
    picked = amp_extended[coupled_local]
    coupled = jnp.einsum("pc,pcab->pab", fock_coupling, picked, preferred_element_type=jnp.float32)
    row_energy = lax.dynamic_slice_in_dim(virtual_energy, replica_index * row_count, row_count)
    orbital_ids = jnp.arange(occupied_energy.shape[0], dtype=jnp.int32)
    matches = (pair_orbitals[:, :, None] == orbital_ids[None, None, :]).astype(jnp.float32)
    pair_shift = jnp.sum(matches * occupied_energy[None, None, :], axis=(1, 2))
    denominator = (
        row_energy[None, :, None] + virtual_energy[None, None, :] - pair_shift[:, None, None]
    )
    residual = integrals - coupled
    updated = (1.0 - damping) * amplitudes.astype(jnp.float32) - damping * residual / denominator
    return updated.astype(jnp.bfloat16)


def solution(mesh):
    placed = (
        P("orb", "rep", None),
        P("orb", "rep", None),
        P("orb", None),
        P("orb", None),
        P("orb", None),
        P(),
        P(),
    )
    return jax.shard_map(
        per_device, mesh=mesh, in_specs=placed, out_specs=P("orb", "rep", None), check_vma=False
    )
```

profile of v0, /device:TPU:1, one launch (start us, length us, event | category | flops | bytes accessed | tf_op | source)
XLA Modules:
  0.0 109.2 jit_solution(899589056150502864)
XLA Ops:
  6.5 0.0 reduce-scatter.4.cloned.1.call-start
  6.5 1.2 %copy.28 = bf16[2,256,512]{1,2,0:T(8,128)(2,1)S(1)} copy(bf16[2,256,512]{2,1,0:T(8,128)(2,1)} %param.7) | data formatting | bytes 1048576 | tf_op args[0]
  7.8 5.1 %collective-permute-start = (bf16[2,256,512]{1,2,0:T(8,128)(2,1)S(1)}, bf16[2,256,512]{1,2,0:T(8,128)(2,1)S(1)}, u32[]{:S(2)}, u32[]{:S(2)}) collective-permute-start(bf16[2,256,512]{1,2,0:T(8,128)(2,1)S(1)} %copy.28), channel_id=1, source_target_pairs={{4,0},{8,4},{12,8},{16,12},{20,16},{24,20},{28,24},{32,28},{36,32}... | collective-permute-start | bytes 1572872 | tf_op jit(solution)/shard_map/ppermute | solution.py:12
  12.9 0.8 fusion.8
  13.7 5.9 %collective-permute-done = bf16[2,256,512]{1,2,0:T(8,128)(2,1)S(1)} collective-permute-done((bf16[2,256,512]{1,2,0:T(8,128)(2,1)S(1)}, bf16[2,256,512]{1,2,0:T(8,128)(2,1)S(1)}, u32[]{:S(2)}, u32[]{:S(2)}) %collective-permute-start) | collective-permute-done | bytes 524320 | tf_op jit(solution)/shard_map/ppermute | solution.py:12
  19.6 4.3 %convolution_bitcast_fusion = bf16[2,4,512,512]{2,3,0,1:T(8,128)(2,1)} fusion(bf16[2,256,512]{1,2,0:T(8,128)(2,1)S(1)} %collective-permute-done, bf16[2,256,512]{1,2,0:T(8,128)(2,1)S(1)} %copy.28, bf16[2,256,512]{2,1,0:T(8,128)(2,1)} %param.7), kind=kOutput, calls=%fused_computation.3 | convolution fusion | flops 1075838976 | bytes 5767168 | tf_op jit(solution)/shard_map/iqa,jqb->ijab/dot_general | solution.py:40
  23.8 4.9 %gather_fusion = bf16[8,512,512]{1,2,0:T(8,128)(2,1)} fusion(bf16[2,4,512,512]{2,3,0,1:T(8,128)(2,1)} %convolution_bitcast_fusion, s32[8]{0:T(128)S(1)} %fusion.8), kind=kCustom, calls=%fused_computation | custom fusion | bytes 8388672 | tf_op jit(solution)/shard_map/gather | solution.py:41
  28.8 8.0 %copy.37 = bf16[8,512,512]{2,0,1:T(8,128)(2,1)} copy(bf16[8,512,512]{1,2,0:T(8,128)(2,1)} %gather_fusion) | data formatting | bytes 8388608
  36.8 6.4 %copy.40 = bf16[64,8,8,512]{3,1,2,0:T(8,128)(2,1)} copy(bf16[64,8,8,512]{3,2,1,0:T(8,128)(2,1)} %bitcast.23) | data formatting | bytes 8388608
  43.2 0.0 copy-start
  43.2 0.0 copy-start.4
  43.2 0.0 copy-start.5
  43.2 0.0 copy-start.3
  43.2 0.0 copy-start.2
  43.2 0.0 copy-start.6
  43.2 0.0 reduce-scatter.4.cloned.1.call-update
  43.2 1.2 %copy-done = bf16[8,128,512]{2,1,0:T(8,128)(2,1)S(1)} copy-done((bf16[8,128,512]{2,1,0:T(8,128)(2,1)S(1)}, bf16[8,128,512]{2,1,0:T(8,128)(2,1)}, u32[]{:S(2)}) %copy-start) | copy-done | bytes 1048600
  44.4 1.9 %collective-permute-start.1 = (bf16[8,128,512]{2,1,0:T(8,128)(2,1)S(1)}, bf16[8,128,512]{2,1,0:T(8,128)(2,1)S(1)}, u32[]{:S(2)}, u32[]{:S(2)}) collective-permute-start(bf16[8,128,512]{2,1,0:T(8,128)(2,1)S(1)} %copy-done), channel_id=1, source_target_pairs={{0,4},{4,8},{8,12},{12,16},{16,20},{20,24},{24,28},{28,32},{32,36}... | collective-permute-start | bytes 3145736 | tf_op jit(solution)/shard_map/ppermute | solution.py:22
  46.3 2.5 %collective-permute-start.2 = (bf16[8,128,512]{2,1,0:T(8,128)(2,1)S(1)}, bf16[8,128,512]{2,1,0:T(8,128)(2,1)}, u32[]{:S(2)}, u32[]{:S(2)}) collective-permute-start(bf16[8,128,512]{2,1,0:T(8,128)(2,1)S(1)} %copy-done), channel_id=1, source_target_pairs={{4,0},{8,4},{12,8},{16,12},{20,16},{24,20},{28,24},{32,28},{36,32}... | collective-permute-start | bytes 3145736 | tf_op jit(solution)/shard_map/ppermute | solution.py:23
  48.8 1.3 %copy.26 = bf16[8,128,512]{1,2,0:T(8,128)(2,1)} copy(bf16[8,128,512]{2,1,0:T(8,128)(2,1)S(1)} %copy-done) | data formatting | bytes 2097152 | tf_op args[1]
  50.1 0.0 copy-done.4
  50.1 0.1 copy.29
  50.2 0.1 reshape.43
  50.3 0.0 copy-done.5
  50.3 0.1 copy.39
  50.3 0.0 copy-done.3
  50.3 0.1 dynamic_slice.3
  50.4 0.0 copy-done.2
  50.4 0.0 copy-done.6
  50.4 0.2 select_reduce_fusion
  50.6 0.1 broadcast_add_fusion
  50.8 7.3 %collective-permute-done.1 = bf16[8,128,512]{2,1,0:T(8,128)(2,1)S(1)} collective-permute-done((bf16[8,128,512]{2,1,0:T(8,128)(2,1)S(1)}, bf16[8,128,512]{2,1,0:T(8,128)(2,1)S(1)}, u32[]{:S(2)}, u32[]{:S(2)}) %collective-permute-start.1) | collective-permute-done | bytes 1048608 | tf_op jit(solution)/shard_map/ppermute | solution.py:22
  58.0 0.0 copy-start.1
  58.0 1.0 copy-done.1
  59.0 4.1 %collective-permute-done.2 = bf16[8,128,512]{2,1,0:T(8,128)(2,1)} collective-permute-done((bf16[8,128,512]{2,1,0:T(8,128)(2,1)S(1)}, bf16[8,128,512]{2,1,0:T(8,128)(2,1)}, u32[]{:S(2)}, u32[]{:S(2)}) %collective-permute-start.2) | collective-permute-done | bytes 1048608 | tf_op jit(solution)/shard_map/ppermute | solution.py:23
  63.1 2.1 %pad_maximum_fusion = bf16[24,128,512]{2,1,0:T(8,128)(2,1)S(1)} fusion(bf16[8,128,512]{2,1,0:T(8,128)(2,1)} %collective-permute-done.2, bf16[8,128,512]{2,1,0:T(8,128)(2,1)} %param.8, bf16[8,128,512]{2,1,0:T(8,128)(2,1)} %copy-done.1), kind=kLoop, calls=%fused_computation.4 | loop fusion | flops 3145728 | bytes 6291456 | tf_op jit(solution)/shard_map/concatenate | solution.py:24
  65.2 2.8 %gather_fusion.1 = bf16[32,128,512]{2,1,0:T(8,128)(2,1)} fusion(bf16[24,128,512]{2,1,0:T(8,128)(2,1)S(1)} %pad_maximum_fusion, s32[1024]{0:T(1024)S(1)} %pad_clamp_fusion), kind=kCustom, calls=%fused_computation.1 | custom fusion | bytes 8388736 | tf_op jit(solution)/shard_map/gather | solution.py:47
  68.0 4.7 %multiply_reduce_fusion = f32[8,128,512]{2,1,0:T(8,128)} fusion(f32[8,4]{1,0:T(8,128)S(1)} %copy.39, bf16[32,128,512]{2,1,0:T(8,128)(2,1)} %gather_fusion.1), kind=kLoop, calls=%fused_computation.2 | loop fusion | flops 5767168 | bytes 6291584
  72.7 1.9 %copy.36 = f32[8,128,512]{1,2,0:T(8,128)S(1)} copy(f32[8,128,512]{2,1,0:T(8,128)} %multiply_reduce_fusion) | data formatting | bytes 4194304 | tf_op jit(solution)/shard_map/pc,pcab->pab/dot_general | solution.py:48
  74.6 20.8 %reduce-scatter.4.cloned.1.call-done = bf16[128,4096]{1,0:T(8,128)(2,1)} async-done(((bf16[512,4096]{1,0:T(8,128)(2,1)}), bf16[128,4096]{1,0:T(8,128)(2,1)}) %reduce-scatter.4.cloned.1.call-update) | async-done | bytes 1048592
  95.4 1.6 %copy.41 = bf16[16,8,8,512]{3,2,1,0:T(8,128)(2,1)S(1)} copy(bf16[16,8,8,512]{3,1,2,0:T(8,128)(2,1)} %bitcast.25) | data formatting | bytes 2097152
  97.1 1.7 %copy.38 = bf16[8,128,512]{1,2,0:T(8,128)(2,1)} copy(bf16[8,128,512]{2,0,1:T(8,128)(2,1)S(1)} %bitcast.24) | data formatting | bytes 2097152
  98.8 2.2 %subtract_convert_fusion = bf16[8,128,512]{1,2,0:T(8,128)(2,1)S(1)} fusion(f32[8,128,512]{1,2,0:T(8,128)S(1)} %copy.36, bf16[8,128,512]{1,2,0:T(8,128)(2,1)} %copy.38, bf16[8,128,512]{1,2,0:T(8,128)(2,1)} %copy.26, f32[8]{0:T(128)S(1)} %select_reduce_fusion, f32[128,512]{0,1:T(8,128)S(1)} %broadcast_add_fusion), kind=kLoop, calls=%fused_computation.5 | loop fusion | flops 4718592 | bytes 5505056 | tf_op jit(solution)/shard_map/convert_element_type | solution.py:58
  101.0 1.3 %copy.30 = bf16[8,128,512]{2,1,0:T(8,128)(2,1)} copy(bf16[8,128,512]{1,2,0:T(8,128)(2,1)S(1)} %subtract_convert_fusion) | data formatting | bytes 2097152 | tf_op jit(solution)/shard_map/convert_element_type | solution.py:58
  (2 shorter events, 0.0 us)
Async XLA Ops:
  6.5 88.9 %reduce-scatter.4.cloned.1.call-start = ((), (), s32[]{:S(2)}) async-start(), calls=%async_computation.1 | async-start | bytes 5242880
  7.8 11.8 %collective-permute-start = (bf16[2,256,512]{1,2,0:T(8,128)(2,1)S(1)}, bf16[2,256,512]{1,2,0:T(8,128)(2,1)S(1)}, u32[]{:S(2)}, u32[]{:S(2)}) collective-permute-start(bf16[2,256,512]{1,2,0:T(8,128)(2,1)S(1)} %copy.28), channel_id=1, source_target_pairs={{4,0},{8,4},{12,8},{16,12},{20,16},{24,20},{28,24},{32,28},{36,32}... | collective-permute-start | bytes 1572872 | tf_op jit(solution)/shard_map/ppermute | solution.py:12
  43.2 1.2 %copy-start = (bf16[8,128,512]{2,1,0:T(8,128)(2,1)S(1)}, bf16[8,128,512]{2,1,0:T(8,128)(2,1)}, u32[]{:S(2)}) copy-start(bf16[8,128,512]{2,1,0:T(8,128)(2,1)} %param.8) | copy-start | bytes 3145732
  43.2 6.9 %copy-start.4 = (s32[8,4]{0,1:T(4,128)S(1)}, s32[8,4]{0,1:T(4,128)}, u32[]{:S(2)}) copy-start(s32[8,4]{0,1:T(4,128)} %param.10) | copy-start | bytes 388
  43.2 7.1 %copy-start.5 = (bf16[8,4]{0,1:T(4,128)(2,1)S(1)}, bf16[8,4]{0,1:T(4,128)(2,1)}, u32[]{:S(2)}) copy-start(bf16[8,4]{0,1:T(4,128)(2,1)} %param.11) | copy-start | bytes 196
  43.2 7.2 %copy-start.3 = (f32[512]{0:T(512)S(1)}, f32[512]{0:T(512)}, u32[]{:S(2)}) copy-start(f32[512]{0:T(512)} %param.12) | copy-start | bytes 6148
  43.2 7.3 %copy-start.2 = (s32[8,2]{0,1:T(2,128)S(1)}, s32[8,2]{0,1:T(2,128)}, u32[]{:S(2)}) copy-start(s32[8,2]{0,1:T(2,128)} %param.9) | copy-start | bytes 196
  43.2 7.3 %copy-start.6 = (f32[128]{0:T(128)S(1)}, f32[128]{0:T(128)}, u32[]{:S(2)}) copy-start(f32[128]{0:T(128)} %param.13) | copy-start | bytes 1540
  44.4 13.6 %collective-permute-start.1 = (bf16[8,128,512]{2,1,0:T(8,128)(2,1)S(1)}, bf16[8,128,512]{2,1,0:T(8,128)(2,1)S(1)}, u32[]{:S(2)}, u32[]{:S(2)}) collective-permute-start(bf16[8,128,512]{2,1,0:T(8,128)(2,1)S(1)} %copy-done), channel_id=1, source_target_pairs={{0,4},{4,8},{8,12},{12,16},{16,20},{20,24},{24,28},{28,32},{32,36}... | collective-permute-start | bytes 3145736 | tf_op jit(solution)/shard_map/ppermute | solution.py:22
  46.3 16.8 %collective-permute-start.2 = (bf16[8,128,512]{2,1,0:T(8,128)(2,1)S(1)}, bf16[8,128,512]{2,1,0:T(8,128)(2,1)}, u32[]{:S(2)}, u32[]{:S(2)}) collective-permute-start(bf16[8,128,512]{2,1,0:T(8,128)(2,1)S(1)} %copy-done), channel_id=1, source_target_pairs={{4,0},{8,4},{12,8},{16,12},{20,16},{24,20},{28,24},{32,28},{36,32}... | collective-permute-start | bytes 3145736 | tf_op jit(solution)/shard_map/ppermute | solution.py:23
  58.0 1.0 copy-start.1
Sparse Core Ops, SparseCore 0:
  43.3 52.0 reduce-scatter.3
where the time goes:
time: 110 us; the launch traced here: 109 us
  waiting for transfers between devices  38.1 us (35%)
  local copies, waits for them, and re-layouts  33.7 us (31%)
  between operations  13.5 us (12%)
  other arithmetic  10.1 us (9%)
  starting transfers between devices  9.49 us (9%)
  matrix products  4.26 us (4%)
    unnamed x21, local copies, waits for them, and re-layouts  22.5 us
    unnamed x2, waiting for transfers between devices  20.8 us
    ppermute x1, waiting for transfers between devices, extended_2(): before = lax.ppermute(last, axis, up)  7.26 us
    ppermute x1, waiting for transfers between devices, passed_along(): return lax.ppermute(block, axis, route)  5.89 us
    ppermute x1, starting transfers between devices, passed_along(): return lax.ppermute(block, axis, route)  5.11 us
    gather x1, local copies, waits for them, and re-layouts, per_device(): partial_value = combos[first_local, second_local]  4.94 us
    unnamed x1, other arithmetic  4.72 us
    dot_general x1, matrix products, per_device(): jnp.einsum('iqa,jqb->ijab', blocks, extended, preferred_element_type=jnp....  4.26 us
  transfers between devices with their start and end apart: 4, of which 4 were waited for; matrix products, arithmetic and copies ran while one was open for 13% of the time, Pallas kernels for 0%

commit v1 on v0

v1 whole, which is shorter than its diff:
```python
import jax
import jax.numpy as jnp
from jax import lax
from jax.experimental import pallas as pl
from jax.experimental.pallas import tpu as pltpu
from jax.sharding import PartitionSpec as P

damping = 0.7


SMEM = pl.BlockSpec(memory_space=pltpu.SMEM)
VMEM = pl.BlockSpec(memory_space=pltpu.VMEM)
ANY = pl.BlockSpec(memory_space=pl.ANY)


def along_orb(x, distance):
    n = lax.axis_size("orb")
    return lax.ppermute(x, "orb", [(i - distance, i) for i in range(n) if 0 <= i - distance < n])


def along_rep(x, distance):
    n = lax.axis_size("rep")
    return lax.ppermute(x, "rep", [(i, (i + distance) % n) for i in range(n)])


def along_rep_odd(x, distance):
    n, m = lax.axis_size("orb"), lax.axis_size("rep")
    route = [(o * m + i, o * m + (i + distance * (o % 2)) % m) for o in range(n) for i in range(m)]
    return lax.ppermute(x, ("orb", "rep"), route)


def odd_to_even(x):
    n = lax.axis_size("orb")
    return lax.ppermute(x, "orb", [(o, o - 1) for o in range(1, n, 2)])


def call(body, out_shape, in_specs, scratch=(), limit=16, cost=10**8):
    return pl.pallas_call(
        body,
        out_shape=out_shape,
        in_specs=in_specs,
        out_specs=jax.tree.map(lambda _: VMEM, out_shape),
        scratch_shapes=list(scratch),
        compiler_params=pltpu.CompilerParams(vmem_limit_bytes=limit * 2**20),
        cost_estimate=pl.CostEstimate(flops=cost, bytes_accessed=4 * 2**20, transcendentals=0),
    )


def couple_kernel(ids, orbs, cpl, fock, occ, row_e, col_e, prev, own, nxt, pre, wgt, amps, sems):
    pair_count, rows = own.shape[:2]
    copies = [
        pltpu.make_async_copy(src, amps.at[pl.ds(k * pair_count, pair_count)], sems.at[k])
        for k, src in enumerate((prev, own, nxt))
    ]
    for c in copies:
        c.start()
    for c in copies:
        c.wait()
    base = (ids[0] - 1) * pair_count
    step = 32

    def pair(p, carry):
        shift = occ[orbs[0, p]] + occ[orbs[1, p]]
        slots = [cpl[c, p] - base for c in range(cpl.shape[0])]
        weights = [fock[c, p] for c in range(cpl.shape[0])]
        for r in range(0, rows, step):
            part = pl.ds(r, step)
            w = damping / (row_e[part, :] + (col_e[...] - shift))
            total = None
            for s, f in zip(slots, weights):
                term = f * amps[s, part, :].astype(jnp.float32)
                total = term if total is None else total + term
            mine = amps[p + pair_count, part, :].astype(jnp.float32)
            pre[p, part, :] = (1.0 - damping) * mine + w * total
            wgt[p, part, :] = w
        return carry

    lax.fori_loop(0, pair_count, pair, 0)


def coupled_terms(*args):
    own = args[-2]
    shape = jax.ShapeDtypeStruct(own.shape, jnp.float32)
    scratch = (
        pltpu.VMEM((3 * own.shape[0],) + own.shape[1:], own.dtype),
        pltpu.SemaphoreType.DMA((3,)),
    )
    specs = [SMEM] * 5 + [VMEM] * 2 + [ANY] * 3
    return call(couple_kernel, (shape, shape), specs, scratch)(*args)


def dot_t(a, b):
    return lax.dot_general(a, b, (((0,), (0,)), ((), ())), preferred_element_type=jnp.float32)


def left_of(ids, blocks, rows):
    start = pl.multiple_of(ids[1] * rows, rows)
    return jnp.concatenate(
        [
            jnp.concatenate([b[i, :, pl.ds(start, rows)] for i in range(b.shape[0])], axis=1)
            for b in blocks
        ],
        axis=0,
    )


def products(ids, left, right, out):
    orbitals, _, rows, _ = out.shape
    lhs = left_of(ids, left, rows)
    for j in range(orbitals):
        both = dot_t(lhs, jnp.concatenate([r(j) for r in right], axis=0))
        for i in range(orbitals):
            out[i, j] = both[i * rows:(i + 1) * rows]


def acc_shape(block):
    orbitals, _, width = block.shape
    return jax.ShapeDtypeStruct(
        (orbitals, orbitals, width // lax.axis_size("rep"), width), jnp.float32
    )


def whole(ref):
    return lambda j: ref[j]


def either(ids, odd_ref, even_ref):
    odd = lax.rem(ids[0], 2) == 1
    return lambda j: jnp.where(odd, odd_ref[j], even_ref[j])


def own_part(ids, b0, b1, b2):
    def body(ids, b0, b1, b2, out):
        products(ids, (b0, b1, b2), [whole(b) for b in (b0, b1, b2)], out)

    return call(body, acc_shape(b0), [SMEM] + [VMEM] * 3)(ids, b0, b1, b2)


def next_part(ids, b0, b1, b2, n0, n1, n2x, n2c):
    def body(ids, b0, b1, b2, n0, n1, n2x, n2c, out):
        products(ids, (b0, b1, b2), [whole(n0), whole(n1), either(ids, n2x, n2c)], out)

    return call(body, acc_shape(b0), [SMEM] + [VMEM] * 7)(ids, b0, b1, b2, n0, n1, n2x, n2c)


def pair_slot(ids, orbs, p, orbitals):
    base = ids[0] * orbitals
    return orbs[0, p] - base, orbs[1, p] - base


def partial_update(ids, orbs, own_acc, next_acc, pre, wgt, b3):
    def body(ids, orbs, own_acc, next_acc, pre, wgt, b3, out, acc):
        orbitals, _, rows, _ = own_acc.shape
        lhs = left_of(ids, (b3,), rows)
        for j in range(orbitals):
            both = dot_t(lhs, b3[j])
            for i in range(orbitals):
                acc[i, j] = own_acc[i, j] + both[i * rows:(i + 1) * rows]
                acc[i, orbitals + j] = next_acc[i, j]

        def pair(p, carry):
            i, j = pair_slot(ids, orbs, p, orbitals)
            out[p] = pre[p] - wgt[p] * acc[i, j]
            return carry

        lax.fori_loop(0, out.shape[0], pair, 0)

    o, _, r, w = own_acc.shape
    return call(
        body, jax.ShapeDtypeStruct(pre.shape, jnp.float32),
        [SMEM] * 2 + [VMEM] * 5, [pltpu.VMEM((o, 2 * o, r, w), jnp.float32)],
    )(ids, orbs, own_acc, next_acc, pre, wgt, b3)


def last_update(ids, orbs, part, wgt, b3, n3x, n3c):
    def body(ids, orbs, part, wgt, b3, n3x, n3c, out, acc):
        orbitals, _, _, _ = acc.shape
        products(ids, (b3,), [either(ids, n3x, n3c)], acc)

        def pair(p, carry):
            i, j = pair_slot(ids, orbs, p, orbitals)
            ahead = j >= orbitals

            @pl.when(ahead)
            def _():
                out[p] = (part[p] - wgt[p] * acc[i, j - orbitals]).astype(out.dtype)

            @pl.when(jnp.logical_not(ahead))
            def _():
                out[p] = part[p].astype(out.dtype)

            return carry

        lax.fori_loop(0, out.shape[0], pair, 0)

    acc = acc_shape(b3)
    return call(
        body, jax.ShapeDtypeStruct(part.shape, jnp.bfloat16),
        [SMEM] * 2 + [VMEM] * 5, [pltpu.VMEM(acc.shape, acc.dtype)],
    )(ids, orbs, part, wgt, b3, n3x, n3c)


def device_step(
    blocks, amplitudes, pair_orbitals, coupling, fock_coupling, virtual_energy, occupied_energy
):
    row_count = amplitudes.shape[1]
    owner = lax.axis_index("orb").astype(jnp.int32)
    replica = lax.axis_index("rep").astype(jnp.int32)
    ids = jnp.stack([owner, replica])
    orbs = pair_orbitals.T
    b0 = blocks
    n0 = along_orb(b0, -1)
    b1 = along_rep(b0, 1)
    b2 = along_rep(b0, -1)
    amps_next = along_orb(amplitudes, -1)
    amps_prev = along_orb(amplitudes, 1)
    n2x = along_rep_odd(n0, -1)
    b3 = along_rep(b1, 1)
    n1 = along_orb(b1, -1)
    n2c = odd_to_even(b2)
    n3x = along_rep_odd(n2x, -1)
    n3c = odd_to_even(b3)
    row_e = lax.dynamic_slice_in_dim(virtual_energy, replica * row_count, row_count)[:, None]
    pre, wgt = coupled_terms(
        ids, orbs, coupling.T, fock_coupling.T.astype(jnp.float32), occupied_energy,
        row_e, virtual_energy[None, :], amps_prev, amplitudes, amps_next,
    )
    own_acc = own_part(ids, b0, b1, b2)
    next_acc = next_part(ids, b0, b1, b2, n0, n1, n2x, n2c)
    part = partial_update(ids, orbs, own_acc, next_acc, pre, wgt, b3)
    return last_update(ids, orbs, part, wgt, b3, n3x, n3c)


def solution(mesh):
    placed = (
        P("orb", "rep", None),
        P("orb", "rep", None),
        P("orb", None),
        P("orb", None),
        P("orb", None),
        P(),
        P(),
    )
    return jax.shard_map(
        device_step, mesh=mesh, in_specs=placed, out_specs=P("orb", "rep", None), check_vma=False
    )
```

time: 110 us -> 61.9 us (0.56)
  the two profiles are of different devices: /device:TPU:1 before, /device:TPU:24 now
where the time goes in v1:
time: 61.9 us; the launch traced here: 61.2 us
  starting transfers between devices  34.3 us (55%)
  waiting for transfers between devices  12.6 us (20%)
  Pallas kernels  10.6 us (17%)
  local copies, waits for them, and re-layouts  2.74 us (4%)
  other arithmetic  0.76 us (1%)
    ppermute x4, starting transfers between devices, along_orb(): lax.ppermute(x, 'orb', [(i - distance, i) for i in range(n) if 0 <= i - d...  21.3 us
    ppermute x3, waiting for transfers between devices, along_rep(): return lax.ppermute(x, 'rep', [(i, (i + distance) % n) for i in range(n)])  12.5 us
    ppermute x2, starting transfers between devices, along_rep_odd(): return lax.ppermute(x, ('orb', 'rep'), route)  6.82 us
    ppermute x3, starting transfers between devices, along_rep(): return lax.ppermute(x, 'rep', [(i, (i + distance) % n) for i in range(n)])  3.67 us
    pallas_call x1, Pallas kernels, coupled_terms(): return call(couple_kernel, (shape, shape), specs, scratch)(*args)  3.37 us
    pallas_call x1, Pallas kernels, last_update(): call(body, jax.ShapeDtypeStruct(part.shape, jnp.bfloat16), [SMEM] * 2 + [...  2.89 us
    ppermute x2, starting transfers between devices, odd_to_even(): return lax.ppermute(x, 'orb', [(o, o - 1) for o in range(1, n, 2)])  2.56 us
    pallas_call x1, Pallas kernels, next_part(): call(body, acc_shape(b0), [SMEM] + [VMEM] * 7)  1.89 us
  transfers between devices with their start and end apart: 11, of which 2 were waited for; matrix products, arithmetic and copies ran while one was open for 3% of the time, Pallas kernels for 13%

profile of v1, /device:TPU:24, one launch (start us, length us, event | category | flops | bytes accessed | tf_op | source)
XLA Modules:
  0.0 61.2 jit_solution(3987330477582592923)
XLA Ops:
  0.0 1.5 %collective-permute-start = (bf16[2,256,512]{2,1,0:T(8,128)(2,1)}, bf16[2,256,512]{2,1,0:T(8,128)(2,1)S(1)}, u32[]{:S(2)}, u32[]{:S(2)}) collective-permute-start(bf16[2,256,512]{2,1,0:T(8,128)(2,1)} %b0.3), channel_id=1, source_target_pairs={{0,1},{1,2},{2,3},{3,0},{4,5},{5,6},{6,7},{7,4},{8,9},{9,10},{10,1... | collective-permute-start | bytes 1572872 | tf_op jit(solution)/shard_map/ppermute | solution.py:23
  1.5 7.1 %collective-permute-start.2 = (bf16[2,256,512]{2,1,0:T(8,128)(2,1)}, bf16[2,256,512]{2,1,0:T(8,128)(2,1)S(1)}, u32[]{:S(2)}, u32[]{:S(2)}) collective-permute-start(bf16[2,256,512]{2,1,0:T(8,128)(2,1)} %b0.3), channel_id=1, source_target_pairs={{4,0},{8,4},{12,8},{16,12},{20,16},{24,20},{28,24},{32,28},{36,32}... | collective-permute-start | bytes 1572872 | tf_op jit(solution)/shard_map/ppermute | solution.py:18
  8.6 1.8 %collective-permute-start.1 = (bf16[2,256,512]{2,1,0:T(8,128)(2,1)}, bf16[2,256,512]{2,1,0:T(8,128)(2,1)S(1)}, u32[]{:S(2)}, u32[]{:S(2)}) collective-permute-start(bf16[2,256,512]{2,1,0:T(8,128)(2,1)} %b0.3), channel_id=1, source_target_pairs={{0,3},{1,0},{2,1},{3,2},{4,7},{5,4},{6,5},{7,6},{8,11},{9,8},{10,9... | collective-permute-start | bytes 1572872 | tf_op jit(solution)/shard_map/ppermute | solution.py:23
  10.4 4.7 %collective-permute-done.b1 = bf16[2,256,512]{2,1,0:T(8,128)(2,1)S(1)} collective-permute-done((bf16[2,256,512]{2,1,0:T(8,128)(2,1)}, bf16[2,256,512]{2,1,0:T(8,128)(2,1)S(1)}, u32[]{:S(2)}, u32[]{:S(2)}) %collective-permute-start) | collective-permute-done | bytes 524320 | tf_op jit(solution)/shard_map/ppermute | solution.py:23
  15.1 6.5 %collective-permute-start.3 = (bf16[2,256,512]{2,1,0:T(8,128)(2,1)S(1)}, bf16[2,256,512]{2,1,0:T(8,128)(2,1)S(1)}, u32[]{:S(2)}, u32[]{:S(2)}) collective-permute-start(bf16[2,256,512]{2,1,0:T(8,128)(2,1)S(1)} %collective-permute-done.b1), channel_id=1, source_target_pairs={{4,0},{8,4},{12,8},{16,12},{20,16},{24,20},{28,24},{32,28},{36,32}... | collective-permute-start | bytes 1572872 | tf_op jit(solution)/shard_map/ppermute | solution.py:18
  21.6 1.9 %collective-permute-start.6 = (bf16[8,128,512]{2,1,0:T(8,128)(2,1)}, bf16[8,128,512]{2,1,0:T(8,128)(2,1)S(1)}, u32[]{:S(2)}, u32[]{:S(2)}) collective-permute-start(bf16[8,128,512]{2,1,0:T(8,128)(2,1)} %own.1), channel_id=1, source_target_pairs={{0,4},{4,8},{8,12},{12,16},{16,20},{20,24},{24,28},{28,32},{32,36}... | collective-permute-start | bytes 3145736 | tf_op jit(solution)/shard_map/ppermute | solution.py:18
  23.5 5.8 %collective-permute-start.7 = (bf16[8,128,512]{2,1,0:T(8,128)(2,1)}, bf16[8,128,512]{2,1,0:T(8,128)(2,1)}, u32[]{:S(2)}, u32[]{:S(2)}) collective-permute-start(bf16[8,128,512]{2,1,0:T(8,128)(2,1)} %own.1), channel_id=1, source_target_pairs={{4,0},{8,4},{12,8},{16,12},{20,16},{24,20},{28,24},{32,28},{36,32}... | collective-permute-start | bytes 3145736 | tf_op jit(solution)/shard_map/ppermute | solution.py:18
  29.3 0.0 collective-permute-done.2.n0
  29.3 0.4 collective-permute-start.8
  29.7 0.0 collective-permute-done.1.b2
  29.7 1.5 %collective-permute-start.4 = (bf16[2,256,512]{2,1,0:T(8,128)(2,1)S(1)}, bf16[2,256,512]{2,1,0:T(8,128)(2,1)}, u32[]{:S(2)}, u32[]{:S(2)}) collective-permute-start(bf16[2,256,512]{2,1,0:T(8,128)(2,1)S(1)} %collective-permute-done.2.n0), channel_id=1, source_target_pairs={{0,0},{1,1},{2,2},{3,3},{4,7},{5,4},{6,5},{7,6},{8,8},{9,9},{10,10... | collective-permute-start | bytes 1572872 | tf_op jit(solution)/shard_map/ppermute | solution.py:29
  31.1 0.0 collective-permute-done.3.n1
  31.1 0.0 copy-start.2
  31.1 0.8 %copy-done.2 = bf16[2,256,512]{2,1,0:T(8,128)(2,1)} copy-done((bf16[2,256,512]{2,1,0:T(8,128)(2,1)}, bf16[2,256,512]{2,1,0:T(8,128)(2,1)S(1)}, u32[]{:S(2)}) %copy-start.2) | copy-done | bytes 524312
  31.9 1.3 %collective-permute-start.5 = (bf16[2,256,512]{2,1,0:T(8,128)(2,1)S(1)}, bf16[2,256,512]{2,1,0:T(8,128)(2,1)}, u32[]{:S(2)}, u32[]{:S(2)}) collective-permute-start(bf16[2,256,512]{2,1,0:T(8,128)(2,1)S(1)} %collective-permute-done.1.b2), channel_id=1, source_target_pairs={{4,0},{12,8},{20,16},{28,24},{36,32},{44,40},{52,48},{60,56},{68,6... | collective-permute-start | bytes 1572872 | tf_op jit(solution)/shard_map/ppermute | solution.py:34
  33.2 7.9 %collective-permute-done.8.b3 = bf16[2,256,512]{2,1,0:T(8,128)(2,1)S(1)} collective-permute-done((bf16[2,256,512]{2,1,0:T(8,128)(2,1)S(1)}, bf16[2,256,512]{2,1,0:T(8,128)(2,1)S(1)}, u32[]{:S(2)}, u32[]{:S(2)}) %collective-permute-start.8) | collective-permute-done | bytes 524320 | tf_op jit(solution)/shard_map/ppermute | solution.py:23
  41.1 1.3 %collective-permute-start.10 = (bf16[2,256,512]{2,1,0:T(8,128)(2,1)S(1)}, bf16[2,256,512]{2,1,0:T(8,128)(2,1)}, u32[]{:S(2)}, u32[]{:S(2)}) collective-permute-start(bf16[2,256,512]{2,1,0:T(8,128)(2,1)S(1)} %collective-permute-done.8.b3), channel_id=1, source_target_pairs={{4,0},{12,8},{20,16},{28,24},{36,32},{44,40},{52,48},{60,56},{68,6... | collective-permute-start | bytes 1572872 | tf_op jit(solution)/shard_map/ppermute | solution.py:34
  42.4 0.0 collective-permute-done.4.n2x
  42.4 5.4 %collective-permute-start.9 = (bf16[2,256,512]{2,1,0:T(8,128)(2,1)}, bf16[2,256,512]{2,1,0:T(8,128)(2,1)}, u32[]{:S(2)}, u32[]{:S(2)}) collective-permute-start(bf16[2,256,512]{2,1,0:T(8,128)(2,1)} %collective-permute-done.4.n2x), channel_id=1, source_target_pairs={{0,0},{1,1},{2,2},{3,3},{4,7},{5,4},{6,5},{7,6},{8,8},{9,9},{10,10... | collective-permute-start | bytes 1572872 | tf_op jit(solution)/shard_map/ppermute | solution.py:29
  47.8 0.8 %dynamic-slice_bitcast_fusion = f32[128,1]{0,1:T(1,128)S(1)} fusion(f32[512]{0:T(512)} %param.12, s32[]{:T(128)S(6)} %select_n.3), kind=kLoop, calls=%fused_computation.2 | loop fusion | bytes 1028 | tf_op jit(solution)/shard_map/broadcast_in_dim | solution.py:223
  48.5 0.1 copy.8.row_e
  48.6 0.1 pad_add_fusion.ids
  48.7 0.7 %convert_bitcast_fusion.fock = f32[4,8]{1,0:T(4,128)S(1)} fusion(bf16[8,4]{0,1:T(4,128)(2,1)} %param.11), kind=kLoop, calls=%fused_computation | loop fusion | flops 32 | bytes 192 | tf_op jit(solution)/shard_map/convert_element_type | solution.py:225
  49.4 0.0 copy-start
  49.4 1.0 %copy-done = bf16[2,256,512]{2,1,0:T(8,128)(2,1)S(1)} copy-done((bf16[2,256,512]{2,1,0:T(8,128)(2,1)S(1)}, bf16[2,256,512]{2,1,0:T(8,128)(2,1)}, u32[]{:S(2)}) %copy-start) | copy-done | bytes 524312
  50.4 0.0 copy-start.3
  50.4 1.1 %shard_map.73.own_acc = f32[2,2,128,512]{3,2,1,0:T(8,128)S(1)} custom-call(s32[2]{0:T(128)S(1)} %pad_add_fusion.ids, bf16[2,256,512]{2,1,0:T(8,128)(2,1)S(1)} %copy-done, bf16[2,256,512]{2,1,0:T(8,128)(2,1)S(1)} %collective-permute-done.b1, bf16[2,256,512]{2,1,0:T(8,128)(2,1)S(1)} %collective-permute-done.1.b2), custom_call_target="tpu_custom_call" | custom-call | flops 100000000 | bytes 4194304 | tf_op jit(solution)/shard_map/pallas_call | solution.py:136
  51.6 0.0 copy-start.1
  51.6 0.0 copy-start.4
  51.6 0.0 copy-start.5
  51.6 0.0 copy-start.6
  51.6 0.0 copy-start.7
  51.6 0.0 collective-permute-done.5.n2c
  51.6 0.0 copy-done.3
  51.6 1.9 %shard_map.74.next_acc = f32[2,2,128,512]{3,2,1,0:T(8,128)S(1)} custom-call(s32[2]{0:T(128)S(1)} %pad_add_fusion.ids, bf16[2,256,512]{2,1,0:T(8,128)(2,1)S(1)} %copy-done, bf16[2,256,512]{2,1,0:T(8,128)(2,1)S(1)} %collective-permute-done.b1, bf16[2,256,512]{2,1,0:T(8,128)(2,1)S(1)} %collective-permute-done.1.b2, ...), custom_call_target="tpu_custom_call" | custom-call | flops 100000000 | bytes 4194304 | tf_op jit(solution)/shard_map/pallas_call | solution.py:143
  53.5 0.0 collective-permute-done.6.prev
  53.6 0.0 collective-permute-done.7.nxt
  53.6 0.0 copy-done.1
  53.6 0.0 copy-done.4
  53.6 0.0 copy-done.5
  53.6 0.0 copy-done.6
  53.6 0.0 copy-done.7
  53.6 3.4 %shard_map.75 = (f32[8,128,512]{2,1,0:T(8,128)S(1)}, f32[8,128,512]{2,1,0:T(8,128)S(1)}) custom-call(s32[2]{0:T(128)S(1)} %pad_add_fusion.ids, s32[2,8]{1,0:T(2,128)S(1)} %bitcast.9, s32[4,8]{1,0:T(4,128)S(1)} %bitcast.12, f32[4,8]{1,0:T(4,128)S(1)} %convert_bitcast_fusion.fock, f32[128]{0:T(128)S(1)} %copy-done.7, f32[128,1]{1,0:T(8,128)S(1)} %copy.8.row_e, ...), custom_call_target="tpu_custom_call" | custom-call | flops 100000000 | bytes 4194304 | tf_op jit(solution)/shard_map/pallas_call | solution.py:89
  57.0 1.3 %shard_map.76.part = f32[8,128,512]{2,1,0:T(8,128)S(1)} custom-call(s32[2]{0:T(128)S(1)} %pad_add_fusion.ids, s32[2,8]{1,0:T(2,128)S(1)} %bitcast.10, f32[2,2,128,512]{3,2,1,0:T(8,128)S(1)} %shard_map.73.own_acc, f32[2,2,128,512]{3,2,1,0:T(8,128)S(1)} %shard_map.74.next_acc, f32[8,128,512]{2,1,0:T(8,128)S(1)} %get-tuple-element.7.pre, ...), custom_call_target="tpu_custom_call" | custom-call | flops 100000000 | bytes 4194304 | tf_op jit(solution)/shard_map/pallas_call | solution.py:169
  58.3 0.0 collective-permute-done.10.n3c
  58.3 0.0 collective-permute-done.9.n3x
  58.3 2.9 %shard_map.77 = bf16[8,128,512]{2,1,0:T(8,128)(2,1)} custom-call(s32[2]{0:T(128)S(1)} %pad_add_fusion.ids, s32[2,8]{1,0:T(2,128)S(1)} %bitcast.11, f32[8,128,512]{2,1,0:T(8,128)S(1)} %shard_map.76.part, f32[8,128,512]{2,1,0:T(8,128)S(1)} %get-tuple-element.8.wgt, bf16[2,256,512]{2,1,0:T(8,128)(2,1)S(1)} %collective-permute-done.8.b3, ...), custom_call_target="tpu_custom_call" | custom-call | flops 100000000 | bytes 4194304 | tf_op jit(solution)/shard_map/pallas_call | solution.py:197
Async XLA Ops:
  0.0 15.1 %collective-permute-start = (bf16[2,256,512]{2,1,0:T(8,128)(2,1)}, bf16[2,256,512]{2,1,0:T(8,128)(2,1)S(1)}, u32[]{:S(2)}, u32[]{:S(2)}) collective-permute-start(bf16[2,256,512]{2,1,0:T(8,128)(2,1)} %b0.3), channel_id=1, source_target_pairs={{0,1},{1,2},{2,3},{3,0},{4,5},{5,6},{6,7},{7,4},{8,9},{9,10},{10,1... | collective-permute-start | bytes 1572872 | tf_op jit(solution)/shard_map/ppermute | solution.py:23
  1.5 27.8 %collective-permute-start.2 = (bf16[2,256,512]{2,1,0:T(8,128)(2,1)}, bf16[2,256,512]{2,1,0:T(8,128)(2,1)S(1)}, u32[]{:S(2)}, u32[]{:S(2)}) collective-permute-start(bf16[2,256,512]{2,1,0:T(8,128)(2,1)} %b0.3), channel_id=1, source_target_pairs={{4,0},{8,4},{12,8},{16,12},{20,16},{24,20},{28,24},{32,28},{36,32}... | collective-permute-start | bytes 1572872 | tf_op jit(solution)/shard_map/ppermute | solution.py:18
  8.6 21.1 %collective-permute-start.1 = (bf16[2,256,512]{2,1,0:T(8,128)(2,1)}, bf16[2,256,512]{2,1,0:T(8,128)(2,1)S(1)}, u32[]{:S(2)}, u32[]{:S(2)}) collective-permute-start(bf16[2,256,512]{2,1,0:T(8,128)(2,1)} %b0.3), channel_id=1, source_target_pairs={{0,3},{1,0},{2,1},{3,2},{4,7},{5,4},{6,5},{7,6},{8,11},{9,8},{10,9... | collective-permute-start | bytes 1572872 | tf_op jit(solution)/shard_map/ppermute | solution.py:23
  15.1 16.1 %collective-permute-start.3 = (bf16[2,256,512]{2,1,0:T(8,128)(2,1)S(1)}, bf16[2,256,512]{2,1,0:T(8,128)(2,1)S(1)}, u32[]{:S(2)}, u32[]{:S(2)}) collective-permute-start(bf16[2,256,512]{2,1,0:T(8,128)(2,1)S(1)} %collective-permute-done.b1), channel_id=1, source_target_pairs={{4,0},{8,4},{12,8},{16,12},{20,16},{24,20},{28,24},{32,28},{36,32}... | collective-permute-start | bytes 1572872 | tf_op jit(solution)/shard_map/ppermute | solution.py:18
  21.6 31.9 %collective-permute-start.6 = (bf16[8,128,512]{2,1,0:T(8,128)(2,1)}, bf16[8,128,512]{2,1,0:T(8,128)(2,1)S(1)}, u32[]{:S(2)}, u32[]{:S(2)}) collective-permute-start(bf16[8,128,512]{2,1,0:T(8,128)(2,1)} %own.1), channel_id=1, source_target_pairs={{0,4},{4,8},{8,12},{12,16},{16,20},{20,24},{24,28},{28,32},{32,36}... | collective-permute-start | bytes 3145736 | tf_op jit(solution)/shard_map/ppermute | solution.py:18
  23.5 30.0 %collective-permute-start.7 = (bf16[8,128,512]{2,1,0:T(8,128)(2,1)}, bf16[8,128,512]{2,1,0:T(8,128)(2,1)}, u32[]{:S(2)}, u32[]{:S(2)}) collective-permute-start(bf16[8,128,512]{2,1,0:T(8,128)(2,1)} %own.1), channel_id=1, source_target_pairs={{4,0},{8,4},{12,8},{16,12},{20,16},{24,20},{28,24},{32,28},{36,32}... | collective-permute-start | bytes 3145736 | tf_op jit(solution)/shard_map/ppermute | solution.py:18
  29.3 11.8 %collective-permute-start.8 = (bf16[2,256,512]{2,1,0:T(8,128)(2,1)S(1)}, bf16[2,256,512]{2,1,0:T(8,128)(2,1)S(1)}, u32[]{:S(2)}, u32[]{:S(2)}) collective-permute-start(bf16[2,256,512]{2,1,0:T(8,128)(2,1)S(1)} %collective-permute-done.b1), channel_id=1, source_target_pairs={{0,1},{1,2},{2,3},{3,0},{4,5},{5,6},{6,7},{7,4},{8,9},{9,10},{10,1... | collective-permute-start | bytes 1572872 | tf_op jit(solution)/shard_map/ppermute | solution.py:23
  29.7 12.7 %collective-permute-start.4 = (bf16[2,256,512]{2,1,0:T(8,128)(2,1)S(1)}, bf16[2,256,512]{2,1,0:T(8,128)(2,1)}, u32[]{:S(2)}, u32[]{:S(2)}) collective-permute-start(bf16[2,256,512]{2,1,0:T(8,128)(2,1)S(1)} %collective-permute-done.2.n0), channel_id=1, source_target_pairs={{0,0},{1,1},{2,2},{3,3},{4,7},{5,4},{6,5},{7,6},{8,8},{9,9},{10,10... | collective-permute-start | bytes 1572872 | tf_op jit(solution)/shard_map/ppermute | solution.py:29
  31.1 0.8 %copy-start.2 = (bf16[2,256,512]{2,1,0:T(8,128)(2,1)}, bf16[2,256,512]{2,1,0:T(8,128)(2,1)S(1)}, u32[]{:S(2)}) copy-start(bf16[2,256,512]{2,1,0:T(8,128)(2,1)S(1)} %collective-permute-done.3.n1) | copy-start | bytes 1572868
  31.9 19.7 %collective-permute-start.5 = (bf16[2,256,512]{2,1,0:T(8,128)(2,1)S(1)}, bf16[2,256,512]{2,1,0:T(8,128)(2,1)}, u32[]{:S(2)}, u32[]{:S(2)}) collective-permute-start(bf16[2,256,512]{2,1,0:T(8,128)(2,1)S(1)} %collective-permute-done.1.b2), channel_id=1, source_target_pairs={{4,0},{12,8},{20,16},{28,24},{36,32},{44,40},{52,48},{60,56},{68,6... | collective-permute-start | bytes 1572872 | tf_op jit(solution)/shard_map/ppermute | solution.py:34
  41.1 17.2 %collective-permute-start.10 = (bf16[2,256,512]{2,1,0:T(8,128)(2,1)S(1)}, bf16[2,256,512]{2,1,0:T(8,128)(2,1)}, u32[]{:S(2)}, u32[]{:S(2)}) collective-permute-start(bf16[2,256,512]{2,1,0:T(8,128)(2,1)S(1)} %collective-permute-done.8.b3), channel_id=1, source_target_pairs={{4,0},{12,8},{20,16},{28,24},{36,32},{44,40},{52,48},{60,56},{68,6... | collective-permute-start | bytes 1572872 | tf_op jit(solution)/shard_map/ppermute | solution.py:34
  42.4 15.9 %collective-permute-start.9 = (bf16[2,256,512]{2,1,0:T(8,128)(2,1)}, bf16[2,256,512]{2,1,0:T(8,128)(2,1)}, u32[]{:S(2)}, u32[]{:S(2)}) collective-permute-start(bf16[2,256,512]{2,1,0:T(8,128)(2,1)} %collective-permute-done.4.n2x), channel_id=1, source_target_pairs={{0,0},{1,1},{2,2},{3,3},{4,7},{5,4},{6,5},{7,6},{8,8},{9,9},{10,10... | collective-permute-start | bytes 1572872 | tf_op jit(solution)/shard_map/ppermute | solution.py:29
  49.4 1.0 %copy-start = (bf16[2,256,512]{2,1,0:T(8,128)(2,1)S(1)}, bf16[2,256,512]{2,1,0:T(8,128)(2,1)}, u32[]{:S(2)}) copy-start(bf16[2,256,512]{2,1,0:T(8,128)(2,1)} %b0.3) | copy-start | bytes 1572868
  50.4 1.2 %copy-start.3 = (bf16[2,256,512]{2,1,0:T(8,128)(2,1)S(1)}, bf16[2,256,512]{2,1,0:T(8,128)(2,1)}, u32[]{:S(2)}) copy-start(bf16[2,256,512]{2,1,0:T(8,128)(2,1)} %copy-done.2) | copy-start | bytes 1572868
  51.6 2.0 %copy-start.1 = (bf16[8,128,512]{2,1,0:T(8,128)(2,1)S(1)}, bf16[8,128,512]{2,1,0:T(8,128)(2,1)}, u32[]{:S(2)}) copy-start(bf16[8,128,512]{2,1,0:T(8,128)(2,1)} %own.1) | copy-start | bytes 3145732
  51.6 2.0 %copy-start.4 = (s32[8,2]{0,1:T(2,128)S(1)}, s32[8,2]{0,1:T(2,128)}, u32[]{:S(2)}) copy-start(s32[8,2]{0,1:T(2,128)} %param.9) | copy-start | bytes 196
  51.6 2.0 %copy-start.5 = (s32[8,4]{0,1:T(4,128)S(1)}, s32[8,4]{0,1:T(4,128)}, u32[]{:S(2)}) copy-start(s32[8,4]{0,1:T(4,128)} %param.10) | copy-start | bytes 388
  51.6 2.0 %copy-start.6 = (f32[512]{0:T(512)S(1)}, f32[512]{0:T(512)}, u32[]{:S(2)}) copy-start(f32[512]{0:T(512)} %param.12) | copy-start | bytes 6148
  51.6 2.0 %copy-start.7 = (f32[128]{0:T(128)S(1)}, f32[128]{0:T(128)}, u32[]{:S(2)}) copy-start(f32[128]{0:T(128)} %occ.1) | copy-start | bytes 1540

commit v2 on v1

--- a/solution.py
+++ b/solution.py
@@ -34,19 +34,19 @@
     return lax.ppermute(x, "orb", [(o, o - 1) for o in range(1, n, 2)])
 
 
-def call(body, out_shape, in_specs, scratch=(), limit=16, cost=10**8):
+def call(body, out_shape, in_specs, scratch=(), out_specs=None, limit=16):
     return pl.pallas_call(
         body,
         out_shape=out_shape,
         in_specs=in_specs,
-        out_specs=jax.tree.map(lambda _: VMEM, out_shape),
+        out_specs=out_specs or jax.tree.map(lambda _: VMEM, out_shape),
         scratch_shapes=list(scratch),
         compiler_params=pltpu.CompilerParams(vmem_limit_bytes=limit * 2**20),
-        cost_estimate=pl.CostEstimate(flops=cost, bytes_accessed=4 * 2**20, transcendentals=0),
-    )
-
-
-def couple_kernel(ids, orbs, cpl, fock, occ, row_e, col_e, prev, own, nxt, pre, wgt, amps, sems):
+        cost_estimate=pl.CostEstimate(flops=10**8, bytes_accessed=4 * 2**20, transcendentals=0),
+    )
+
+
+def couple_kernel(ids, orbs, cpl, fock, occ, mine, energy, prev, own, nxt, pre, wgt, amps, sems):
     pair_count, rows = own.shape[:2]
     copies = [
         pltpu.make_async_copy(src, amps.at[pl.ds(k * pair_count, pair_count)], sems.at[k])
@@ -54,25 +54,32 @@
     ]
     for c in copies:
         c.start()
+    tile = jnp.broadcast_to(mine[...], (rows, rows))
+
+    def denominators(p, carry):
+        shift = occ[orbs[0, p]] + occ[orbs[1, p]]
+        for c in range(0, energy.shape[1], rows):
+            part = slice(c, c + rows)
+            wgt[p, :, part] = damping / (tile + (energy[:, part] - shift))
+        return carry
+
+    lax.fori_loop(0, pair_count, denominators, 0)
     for c in copies:
         c.wait()
     base = (ids[0] - 1) * pair_count
     step = 32
 
     def pair(p, carry):
-        shift = occ[orbs[0, p]] + occ[orbs[1, p]]
         slots = [cpl[c, p] - base for c in range(cpl.shape[0])]
-        weights = [fock[c, p] for c in range(cpl.shape[0])]
+        scales = [fock[c, p] for c in range(cpl.shape[0])]
         for r in range(0, rows, step):
             part = pl.ds(r, step)
-            w = damping / (row_e[part, :] + (col_e[...] - shift))
             total = None
-            for s, f in zip(slots, weights):
+            for s, f in zip(slots, scales):
                 term = f * amps[s, part, :].astype(jnp.float32)
                 total = term if total is None else total + term
             mine = amps[p + pair_count, part, :].astype(jnp.float32)
-            pre[p, part, :] = (1.0 - damping) * mine + w * total
-            wgt[p, part, :] = w
+            pre[p, part, :] = (1.0 - damping) * mine + wgt[p, part, :] * total
         return carry
 
     lax.fori_loop(0, pair_count, pair, 0)
@@ -156,54 +163,69 @@
             both = dot_t(lhs, b3[j])
             for i in range(orbitals):
                 acc[i, j] = own_acc[i, j] + both[i * rows:(i + 1) * rows]
-                acc[i, orbitals + j] = next_acc[i, j]
 
         def pair(p, carry):
             i, j = pair_slot(ids, orbs, p, orbitals)
-            out[p] = pre[p] - wgt[p] * acc[i, j]
+
+            @pl.when(j < orbitals)
+            def _():
+                out[p] = pre[p] - wgt[p] * acc[i, j]
+
+            @pl.when(j >= orbitals)
+            def _():
+                out[p] = pre[p] - wgt[p] * next_acc[i, j - orbitals]
+
             return carry
 
         lax.fori_loop(0, out.shape[0], pair, 0)
 
-    o, _, r, w = own_acc.shape
     return call(
         body, jax.ShapeDtypeStruct(pre.shape, jnp.float32),
-        [SMEM] * 2 + [VMEM] * 5, [pltpu.VMEM((o, 2 * o, r, w), jnp.float32)],
+        [SMEM] * 2 + [VMEM] * 5, [pltpu.VMEM(own_acc.shape, own_acc.dtype)],
     )(ids, orbs, own_acc, next_acc, pre, wgt, b3)
 
 
-def last_update(ids, orbs, part, wgt, b3, n3x, n3c):
-    def body(ids, orbs, part, wgt, b3, n3x, n3c, out, acc):
-        orbitals, _, _, _ = acc.shape
-        products(ids, (b3,), [either(ids, n3x, n3c)], acc)
+def last_update(ids, orbs, part, wgt, left, n3x, n3c):
+    def body(ids, orbs, part, wgt, left, n3x, n3c, out, acc, done, sem):
+        orbitals = acc.shape[0]
+        products(ids, (left,), [either(ids, n3x, n3c)], acc)
 
         def pair(p, carry):
             i, j = pair_slot(ids, orbs, p, orbitals)
-            ahead = j >= orbitals
-
-            @pl.when(ahead)
-            def _():
-                out[p] = (part[p] - wgt[p] * acc[i, j - orbitals]).astype(out.dtype)
-
-            @pl.when(jnp.logical_not(ahead))
-            def _():
-                out[p] = part[p].astype(out.dtype)
-
+
+            @pl.when(j >= orbitals)
+            def _():
+                done[p] = (part[p] - wgt[p] * acc[i, j - orbitals]).astype(done.dtype)
+
+            @pl.when(j < orbitals)
+            def _():
+                done[p] = part[p].astype(done.dtype)
+
+            pltpu.make_async_copy(done.at[p], out.at[p], sem.at[p]).start()
             return carry
 
-        lax.fori_loop(0, out.shape[0], pair, 0)
-
-    acc = acc_shape(b3)
+        def wait(p, carry):
+            pltpu.make_async_copy(done.at[p], out.at[p], sem.at[p]).wait()
+            return carry
+
+        lax.fori_loop(0, done.shape[0], pair, 0)
+        lax.fori_loop(0, done.shape[0], wait, 0)
+
+    acc = acc_shape(n3x)
+    scratch = [
+        pltpu.VMEM(acc.shape, acc.dtype),
+        pltpu.VMEM(part.shape, jnp.bfloat16),
+        pltpu.SemaphoreType.DMA((part.shape[0],)),
+    ]
     return call(
         body, jax.ShapeDtypeStruct(part.shape, jnp.bfloat16),
-        [SMEM] * 2 + [VMEM] * 5, [pltpu.VMEM(acc.shape, acc.dtype)],
-    )(ids, orbs, part, wgt, b3, n3x, n3c)
+        [SMEM] * 2 + [VMEM] * 5, scratch, out_specs=ANY,
+    )(ids, orbs, part, wgt, left, n3x, n3c)
 
 
 def device_step(
     blocks, amplitudes, pair_orbitals, coupling, fock_coupling, virtual_energy, occupied_energy
 ):
-    row_count = amplitudes.shape[1]
     owner = lax.axis_index("orb").astype(jnp.int32)
     replica = lax.axis_index("rep").astype(jnp.int32)
     ids = jnp.stack([owner, replica])
@@ -220,10 +242,12 @@
     n2c = odd_to_even(b2)
     n3x = along_rep_odd(n2x, -1)
     n3c = odd_to_even(b3)
-    row_e = lax.dynamic_slice_in_dim(virtual_energy, replica * row_count, row_count)[:, None]
+    rows = amplitudes.shape[1]
+    row_e = lax.dynamic_slice_in_dim(virtual_energy, replica * rows, rows)[:, None]
+    fock = fock_coupling.T.astype(jnp.float32)
     pre, wgt = coupled_terms(
-        ids, orbs, coupling.T, fock_coupling.T.astype(jnp.float32), occupied_energy,
-        row_e, virtual_energy[None, :], amps_prev, amplitudes, amps_next,
+        ids, orbs, coupling.T, fock, occupied_energy, row_e, virtual_energy[None, :],
+        amps_prev, amplitudes, amps_next,
     )
     own_acc = own_part(ids, b0, b1, b2)
     next_acc = next_part(ids, b0, b1, b2, n0, n1, n2x, n2c)

time: 61.9 us -> 61.5 us (level)
  transfers between devices with their start and end apart: 11 -> 11, of which waited for: 2 -> 2; matrix products, arithmetic and copies ran while one was open for 3% -> 3% of each run, Pallas kernels for 13% -> 12%
where the time goes in v2:
time: 61.5 us; the launch traced here: 60.8 us
  starting transfers between devices  34.3 us (56%)
  waiting for transfers between devices  12.6 us (20%)
  Pallas kernels  10.2 us (17%)
  local copies, waits for them, and re-layouts  2.74 us (4%)
  other arithmetic  0.76 us (1%)
    ppermute x4, starting transfers between devices, along_orb(): lax.ppermute(x, 'orb', [(i - distance, i) for i in range(n) if 0 <= i - d...  21.3 us
    ppermute x3, waiting for transfers between devices, along_rep(): return lax.ppermute(x, 'rep', [(i, (i + distance) % n) for i in range(n)])  12.5 us
    ppermute x2, starting transfers between devices, along_rep_odd(): return lax.ppermute(x, ('orb', 'rep'), route)  6.82 us
    ppermute x3, starting transfers between devices, along_rep(): return lax.ppermute(x, 'rep', [(i, (i + distance) % n) for i in range(n)])  3.67 us
    pallas_call x1, Pallas kernels, coupled_terms(): return call(couple_kernel, (shape, shape), specs, scratch)(*args)  3.12 us
    pallas_call x1, Pallas kernels, last_update(): call(body, jax.ShapeDtypeStruct(part.shape, jnp.bfloat16), [SMEM] * 2 + [...  2.66 us
    ppermute x2, starting transfers between devices, odd_to_even(): return lax.ppermute(x, 'orb', [(o, o - 1) for o in range(1, n, 2)])  2.56 us
    pallas_call x1, Pallas kernels, next_part(): call(body, acc_shape(b0), [SMEM] + [VMEM] * 7)  1.89 us
  transfers between devices with their start and end apart: 11, of which 2 were waited for; matrix products, arithmetic and copies ran while one was open for 3% of the time, Pallas kernels for 12%

profile of v2, /device:TPU:24, one launch (start us, length us, event | category | flops | bytes accessed | tf_op | source)
XLA Modules:
  0.0 60.8 jit_solution(6866019676323182379)
XLA Ops:
  0.0 1.5 %collective-permute-start = (bf16[2,256,512]{2,1,0:T(8,128)(2,1)}, bf16[2,256,512]{2,1,0:T(8,128)(2,1)S(1)}, u32[]{:S(2)}, u32[]{:S(2)}) collective-permute-start(bf16[2,256,512]{2,1,0:T(8,128)(2,1)} %b0.3), channel_id=1, source_target_pairs={{0,1},{1,2},{2,3},{3,0},{4,5},{5,6},{6,7},{7,4},{8,9},{9,10},{10,1... | collective-permute-start | bytes 1572872 | tf_op jit(solution)/shard_map/ppermute | solution.py:23
  1.5 7.1 %collective-permute-start.2 = (bf16[2,256,512]{2,1,0:T(8,128)(2,1)}, bf16[2,256,512]{2,1,0:T(8,128)(2,1)S(1)}, u32[]{:S(2)}, u32[]{:S(2)}) collective-permute-start(bf16[2,256,512]{2,1,0:T(8,128)(2,1)} %b0.3), channel_id=1, source_target_pairs={{4,0},{8,4},{12,8},{16,12},{20,16},{24,20},{28,24},{32,28},{36,32}... | collective-permute-start | bytes 1572872 | tf_op jit(solution)/shard_map/ppermute | solution.py:18
  8.6 1.8 %collective-permute-start.1 = (bf16[2,256,512]{2,1,0:T(8,128)(2,1)}, bf16[2,256,512]{2,1,0:T(8,128)(2,1)S(1)}, u32[]{:S(2)}, u32[]{:S(2)}) collective-permute-start(bf16[2,256,512]{2,1,0:T(8,128)(2,1)} %b0.3), channel_id=1, source_target_pairs={{0,3},{1,0},{2,1},{3,2},{4,7},{5,4},{6,5},{7,6},{8,11},{9,8},{10,9... | collective-permute-start | bytes 1572872 | tf_op jit(solution)/shard_map/ppermute | solution.py:23
  10.4 4.7 %collective-permute-done.b1 = bf16[2,256,512]{2,1,0:T(8,128)(2,1)S(1)} collective-permute-done((bf16[2,256,512]{2,1,0:T(8,128)(2,1)}, bf16[2,256,512]{2,1,0:T(8,128)(2,1)S(1)}, u32[]{:S(2)}, u32[]{:S(2)}) %collective-permute-start) | collective-permute-done | bytes 524320 | tf_op jit(solution)/shard_map/ppermute | solution.py:23
  15.1 6.5 %collective-permute-start.3 = (bf16[2,256,512]{2,1,0:T(8,128)(2,1)S(1)}, bf16[2,256,512]{2,1,0:T(8,128)(2,1)S(1)}, u32[]{:S(2)}, u32[]{:S(2)}) collective-permute-start(bf16[2,256,512]{2,1,0:T(8,128)(2,1)S(1)} %collective-permute-done.b1), channel_id=1, source_target_pairs={{4,0},{8,4},{12,8},{16,12},{20,16},{24,20},{28,24},{32,28},{36,32}... | collective-permute-start | bytes 1572872 | tf_op jit(solution)/shard_map/ppermute | solution.py:18
  21.6 1.9 %collective-permute-start.6 = (bf16[8,128,512]{2,1,0:T(8,128)(2,1)}, bf16[8,128,512]{2,1,0:T(8,128)(2,1)S(1)}, u32[]{:S(2)}, u32[]{:S(2)}) collective-permute-start(bf16[8,128,512]{2,1,0:T(8,128)(2,1)} %own.1), channel_id=1, source_target_pairs={{0,4},{4,8},{8,12},{12,16},{16,20},{20,24},{24,28},{28,32},{32,36}... | collective-permute-start | bytes 3145736 | tf_op jit(solution)/shard_map/ppermute | solution.py:18
  23.5 5.8 %collective-permute-start.7 = (bf16[8,128,512]{2,1,0:T(8,128)(2,1)}, bf16[8,128,512]{2,1,0:T(8,128)(2,1)}, u32[]{:S(2)}, u32[]{:S(2)}) collective-permute-start(bf16[8,128,512]{2,1,0:T(8,128)(2,1)} %own.1), channel_id=1, source_target_pairs={{4,0},{8,4},{12,8},{16,12},{20,16},{24,20},{28,24},{32,28},{36,32}... | collective-permute-start | bytes 3145736 | tf_op jit(solution)/shard_map/ppermute | solution.py:18
  29.3 0.0 collective-permute-done.2.n0
  29.3 0.4 collective-permute-start.8
  29.7 0.0 collective-permute-done.1.b2
  29.7 1.5 %collective-permute-start.4 = (bf16[2,256,512]{2,1,0:T(8,128)(2,1)S(1)}, bf16[2,256,512]{2,1,0:T(8,128)(2,1)}, u32[]{:S(2)}, u32[]{:S(2)}) collective-permute-start(bf16[2,256,512]{2,1,0:T(8,128)(2,1)S(1)} %collective-permute-done.2.n0), channel_id=1, source_target_pairs={{0,0},{1,1},{2,2},{3,3},{4,7},{5,4},{6,5},{7,6},{8,8},{9,9},{10,10... | collective-permute-start | bytes 1572872 | tf_op jit(solution)/shard_map/ppermute | solution.py:29
  31.1 0.0 collective-permute-done.3.n1
  31.1 0.0 copy-start.2
  31.1 0.8 %copy-done.2 = bf16[2,256,512]{2,1,0:T(8,128)(2,1)} copy-done((bf16[2,256,512]{2,1,0:T(8,128)(2,1)}, bf16[2,256,512]{2,1,0:T(8,128)(2,1)S(1)}, u32[]{:S(2)}) %copy-start.2) | copy-done | bytes 524312
  31.9 1.3 %collective-permute-start.5 = (bf16[2,256,512]{2,1,0:T(8,128)(2,1)S(1)}, bf16[2,256,512]{2,1,0:T(8,128)(2,1)}, u32[]{:S(2)}, u32[]{:S(2)}) collective-permute-start(bf16[2,256,512]{2,1,0:T(8,128)(2,1)S(1)} %collective-permute-done.1.b2), channel_id=1, source_target_pairs={{4,0},{12,8},{20,16},{28,24},{36,32},{44,40},{52,48},{60,56},{68,6... | collective-permute-start | bytes 1572872 | tf_op jit(solution)/shard_map/ppermute | solution.py:34
  33.2 7.9 %collective-permute-done.8.b3.left = bf16[2,256,512]{2,1,0:T(8,128)(2,1)S(1)} collective-permute-done((bf16[2,256,512]{2,1,0:T(8,128)(2,1)S(1)}, bf16[2,256,512]{2,1,0:T(8,128)(2,1)S(1)}, u32[]{:S(2)}, u32[]{:S(2)}) %collective-permute-start.8) | collective-permute-done | bytes 524320 | tf_op jit(solution)/shard_map/ppermute | solution.py:23
  41.1 1.3 %collective-permute-start.10 = (bf16[2,256,512]{2,1,0:T(8,128)(2,1)S(1)}, bf16[2,256,512]{2,1,0:T(8,128)(2,1)}, u32[]{:S(2)}, u32[]{:S(2)}) collective-permute-start(bf16[2,256,512]{2,1,0:T(8,128)(2,1)S(1)} %collective-permute-done.8.b3.left), channel_id=1, source_target_pairs={{4,0},{12,8},{20,16},{28,24},{36,32},{44,40},{52,48},{60,56},{68,6... | collective-permute-start | bytes 1572872 | tf_op jit(solution)/shard_map/ppermute | solution.py:34
  42.4 0.0 collective-permute-done.4.n2x
  42.4 5.4 %collective-permute-start.9 = (bf16[2,256,512]{2,1,0:T(8,128)(2,1)}, bf16[2,256,512]{2,1,0:T(8,128)(2,1)}, u32[]{:S(2)}, u32[]{:S(2)}) collective-permute-start(bf16[2,256,512]{2,1,0:T(8,128)(2,1)} %collective-permute-done.4.n2x), channel_id=1, source_target_pairs={{0,0},{1,1},{2,2},{3,3},{4,7},{5,4},{6,5},{7,6},{8,8},{9,9},{10,10... | collective-permute-start | bytes 1572872 | tf_op jit(solution)/shard_map/ppermute | solution.py:29
  47.8 0.8 %dynamic-slice_bitcast_fusion = f32[128,1]{0,1:T(1,128)S(1)} fusion(f32[512]{0:T(512)} %param.12, s32[]{:T(128)S(6)} %select_n.3), kind=kLoop, calls=%fused_computation.2 | loop fusion | bytes 1028 | tf_op jit(solution)/shard_map/broadcast_in_dim | solution.py:246
  48.5 0.1 copy.8.mine
  48.6 0.1 pad_add_fusion.ids
  48.7 0.7 %convert_bitcast_fusion.fock = f32[4,8]{1,0:T(4,128)S(1)} fusion(bf16[8,4]{0,1:T(4,128)(2,1)} %param.11), kind=kLoop, calls=%fused_computation | loop fusion | flops 32 | bytes 192 | tf_op jit(solution)/shard_map/convert_element_type | solution.py:247
  49.4 0.0 copy-start
  49.4 1.0 %copy-done = bf16[2,256,512]{2,1,0:T(8,128)(2,1)S(1)} copy-done((bf16[2,256,512]{2,1,0:T(8,128)(2,1)S(1)}, bf16[2,256,512]{2,1,0:T(8,128)(2,1)}, u32[]{:S(2)}) %copy-start) | copy-done | bytes 524312
  50.4 0.0 copy-start.3
  50.4 1.1 %shard_map.73.own_acc = f32[2,2,128,512]{3,2,1,0:T(8,128)S(1)} custom-call(s32[2]{0:T(128)S(1)} %pad_add_fusion.ids, bf16[2,256,512]{2,1,0:T(8,128)(2,1)S(1)} %copy-done, bf16[2,256,512]{2,1,0:T(8,128)(2,1)S(1)} %collective-permute-done.b1, bf16[2,256,512]{2,1,0:T(8,128)(2,1)S(1)} %collective-permute-done.1.b2), custom_call_target="tpu_custom_call" | custom-call | flops 100000000 | bytes 4194304 | tf_op jit(solution)/shard_map/pallas_call | solution.py:143
  51.6 0.0 copy-start.1
  51.6 0.0 copy-start.4
  51.6 0.0 copy-start.5
  51.6 0.0 copy-start.6
  51.6 0.0 copy-start.7
  51.6 0.0 collective-permute-done.5.n2c
  51.6 0.0 copy-done.3
  51.6 1.9 %shard_map.74.next_acc = f32[2,2,128,512]{3,2,1,0:T(8,128)S(1)} custom-call(s32[2]{0:T(128)S(1)} %pad_add_fusion.ids, bf16[2,256,512]{2,1,0:T(8,128)(2,1)S(1)} %copy-done, bf16[2,256,512]{2,1,0:T(8,128)(2,1)S(1)} %collective-permute-done.b1, bf16[2,256,512]{2,1,0:T(8,128)(2,1)S(1)} %collective-permute-done.1.b2, ...), custom_call_target="tpu_custom_call" | custom-call | flops 100000000 | bytes 4194304 | tf_op jit(solution)/shard_map/pallas_call | solution.py:150
  53.5 0.0 collective-permute-done.6.prev
  53.6 0.0 collective-permute-done.7.nxt
  53.6 0.0 copy-done.1
  53.6 0.0 copy-done.4
  53.6 0.0 copy-done.5
  53.6 0.0 copy-done.6
  53.6 0.0 copy-done.7
  53.6 3.1 %shard_map.75 = (f32[8,128,512]{2,1,0:T(8,128)S(1)}, f32[8,128,512]{2,1,0:T(8,128)S(1)}) custom-call(s32[2]{0:T(128)S(1)} %pad_add_fusion.ids, s32[2,8]{1,0:T(2,128)S(1)} %bitcast.9, s32[4,8]{1,0:T(4,128)S(1)} %bitcast.12, f32[4,8]{1,0:T(4,128)S(1)} %convert_bitcast_fusion.fock, f32[128]{0:T(128)S(1)} %copy-done.7, f32[128,1]{1,0:T(8,128)S(1)} %copy.8.mine, ...), custom_call_target="tpu_custom_call" | custom-call | flops 100000000 | bytes 4194304 | tf_op jit(solution)/shard_map/pallas_call | solution.py:96
  56.7 1.4 %shard_map.76.part = f32[8,128,512]{2,1,0:T(8,128)S(1)} custom-call(s32[2]{0:T(128)S(1)} %pad_add_fusion.ids, s32[2,8]{1,0:T(2,128)S(1)} %bitcast.10, f32[2,2,128,512]{3,2,1,0:T(8,128)S(1)} %shard_map.73.own_acc, f32[2,2,128,512]{3,2,1,0:T(8,128)S(1)} %shard_map.74.next_acc, f32[8,128,512]{2,1,0:T(8,128)S(1)} %get-tuple-element.7.pre, ...), custom_call_target="tpu_custom_call" | custom-call | flops 100000000 | bytes 4194304 | tf_op jit(solution)/shard_map/pallas_call | solution.py:182
  58.1 0.0 collective-permute-done.10.n3c
  58.1 0.0 collective-permute-done.9.n3x
  58.1 2.7 %shard_map.77 = bf16[8,128,512]{2,1,0:T(8,128)(2,1)} custom-call(s32[2]{0:T(128)S(1)} %pad_add_fusion.ids, s32[2,8]{1,0:T(2,128)S(1)} %bitcast.11, f32[8,128,512]{2,1,0:T(8,128)S(1)} %shard_map.76.part, f32[8,128,512]{2,1,0:T(8,128)S(1)} %get-tuple-element.8.wgt, bf16[2,256,512]{2,1,0:T(8,128)(2,1)S(1)} %collective-permute-done.8.b3.left, ...), custom_call_target="tpu_custom_call" | custom-call | flops 100000000 | bytes 4194304 | tf_op jit(solution)/shard_map/pallas_call | solution.py:220
Async XLA Ops:
  0.0 15.1 %collective-permute-start = (bf16[2,256,512]{2,1,0:T(8,128)(2,1)}, bf16[2,256,512]{2,1,0:T(8,128)(2,1)S(1)}, u32[]{:S(2)}, u32[]{:S(2)}) collective-permute-start(bf16[2,256,512]{2,1,0:T(8,128)(2,1)} %b0.3), channel_id=1, source_target_pairs={{0,1},{1,2},{2,3},{3,0},{4,5},{5,6},{6,7},{7,4},{8,9},{9,10},{10,1... | collective-permute-start | bytes 1572872 | tf_op jit(solution)/shard_map/ppermute | solution.py:23
  1.5 27.8 %collective-permute-start.2 = (bf16[2,256,512]{2,1,0:T(8,128)(2,1)}, bf16[2,256,512]{2,1,0:T(8,128)(2,1)S(1)}, u32[]{:S(2)}, u32[]{:S(2)}) collective-permute-start(bf16[2,256,512]{2,1,0:T(8,128)(2,1)} %b0.3), channel_id=1, source_target_pairs={{4,0},{8,4},{12,8},{16,12},{20,16},{24,20},{28,24},{32,28},{36,32}... | collective-permute-start | bytes 1572872 | tf_op jit(solution)/shard_map/ppermute | solution.py:18
  8.6 21.1 %collective-permute-start.1 = (bf16[2,256,512]{2,1,0:T(8,128)(2,1)}, bf16[2,256,512]{2,1,0:T(8,128)(2,1)S(1)}, u32[]{:S(2)}, u32[]{:S(2)}) collective-permute-start(bf16[2,256,512]{2,1,0:T(8,128)(2,1)} %b0.3), channel_id=1, source_target_pairs={{0,3},{1,0},{2,1},{3,2},{4,7},{5,4},{6,5},{7,6},{8,11},{9,8},{10,9... | collective-permute-start | bytes 1572872 | tf_op jit(solution)/shard_map/ppermute | solution.py:23
  15.1 16.1 %collective-permute-start.3 = (bf16[2,256,512]{2,1,0:T(8,128)(2,1)S(1)}, bf16[2,256,512]{2,1,0:T(8,128)(2,1)S(1)}, u32[]{:S(2)}, u32[]{:S(2)}) collective-permute-start(bf16[2,256,512]{2,1,0:T(8,128)(2,1)S(1)} %collective-permute-done.b1), channel_id=1, source_target_pairs={{4,0},{8,4},{12,8},{16,12},{20,16},{24,20},{28,24},{32,28},{36,32}... | collective-permute-start | bytes 1572872 | tf_op jit(solution)/shard_map/ppermute | solution.py:18
  21.6 31.9 %collective-permute-start.6 = (bf16[8,128,512]{2,1,0:T(8,128)(2,1)}, bf16[8,128,512]{2,1,0:T(8,128)(2,1)S(1)}, u32[]{:S(2)}, u32[]{:S(2)}) collective-permute-start(bf16[8,128,512]{2,1,0:T(8,128)(2,1)} %own.1), channel_id=1, source_target_pairs={{0,4},{4,8},{8,12},{12,16},{16,20},{20,24},{24,28},{28,32},{32,36}... | collective-permute-start | bytes 3145736 | tf_op jit(solution)/shard_map/ppermute | solution.py:18
  23.5 30.0 %collective-permute-start.7 = (bf16[8,128,512]{2,1,0:T(8,128)(2,1)}, bf16[8,128,512]{2,1,0:T(8,128)(2,1)}, u32[]{:S(2)}, u32[]{:S(2)}) collective-permute-start(bf16[8,128,512]{2,1,0:T(8,128)(2,1)} %own.1), channel_id=1, source_target_pairs={{4,0},{8,4},{12,8},{16,12},{20,16},{24,20},{28,24},{32,28},{36,32}... | collective-permute-start | bytes 3145736 | tf_op jit(solution)/shard_map/ppermute | solution.py:18
  29.3 11.8 %collective-permute-start.8 = (bf16[2,256,512]{2,1,0:T(8,128)(2,1)S(1)}, bf16[2,256,512]{2,1,0:T(8,128)(2,1)S(1)}, u32[]{:S(2)}, u32[]{:S(2)}) collective-permute-start(bf16[2,256,512]{2,1,0:T(8,128)(2,1)S(1)} %collective-permute-done.b1), channel_id=1, source_target_pairs={{0,1},{1,2},{2,3},{3,0},{4,5},{5,6},{6,7},{7,4},{8,9},{9,10},{10,1... | collective-permute-start | bytes 1572872 | tf_op jit(solution)/shard_map/ppermute | solution.py:23
  29.7 12.7 %collective-permute-start.4 = (bf16[2,256,512]{2,1,0:T(8,128)(2,1)S(1)}, bf16[2,256,512]{2,1,0:T(8,128)(2,1)}, u32[]{:S(2)}, u32[]{:S(2)}) collective-permute-start(bf16[2,256,512]{2,1,0:T(8,128)(2,1)S(1)} %collective-permute-done.2.n0), channel_id=1, source_target_pairs={{0,0},{1,1},{2,2},{3,3},{4,7},{5,4},{6,5},{7,6},{8,8},{9,9},{10,10... | collective-permute-start | bytes 1572872 | tf_op jit(solution)/shard_map/ppermute | solution.py:29
  31.1 0.8 %copy-start.2 = (bf16[2,256,512]{2,1,0:T(8,128)(2,1)}, bf16[2,256,512]{2,1,0:T(8,128)(2,1)S(1)}, u32[]{:S(2)}) copy-start(bf16[2,256,512]{2,1,0:T(8,128)(2,1)S(1)} %collective-permute-done.3.n1) | copy-start | bytes 1572868
  31.9 19.7 %collective-permute-start.5 = (bf16[2,256,512]{2,1,0:T(8,128)(2,1)S(1)}, bf16[2,256,512]{2,1,0:T(8,128)(2,1)}, u32[]{:S(2)}, u32[]{:S(2)}) collective-permute-start(bf16[2,256,512]{2,1,0:T(8,128)(2,1)S(1)} %collective-permute-done.1.b2), channel_id=1, source_target_pairs={{4,0},{12,8},{20,16},{28,24},{36,32},{44,40},{52,48},{60,56},{68,6... | collective-permute-start | bytes 1572872 | tf_op jit(solution)/shard_map/ppermute | solution.py:34
  41.1 17.0 %collective-permute-start.10 = (bf16[2,256,512]{2,1,0:T(8,128)(2,1)S(1)}, bf16[2,256,512]{2,1,0:T(8,128)(2,1)}, u32[]{:S(2)}, u32[]{:S(2)}) collective-permute-start(bf16[2,256,512]{2,1,0:T(8,128)(2,1)S(1)} %collective-permute-done.8.b3.left), channel_id=1, source_target_pairs={{4,0},{12,8},{20,16},{28,24},{36,32},{44,40},{52,48},{60,56},{68,6... | collective-permute-start | bytes 1572872 | tf_op jit(solution)/shard_map/ppermute | solution.py:34
  42.4 15.7 %collective-permute-start.9 = (bf16[2,256,512]{2,1,0:T(8,128)(2,1)}, bf16[2,256,512]{2,1,0:T(8,128)(2,1)}, u32[]{:S(2)}, u32[]{:S(2)}) collective-permute-start(bf16[2,256,512]{2,1,0:T(8,128)(2,1)} %collective-permute-done.4.n2x), channel_id=1, source_target_pairs={{0,0},{1,1},{2,2},{3,3},{4,7},{5,4},{6,5},{7,6},{8,8},{9,9},{10,10... | collective-permute-start | bytes 1572872 | tf_op jit(solution)/shard_map/ppermute | solution.py:29
  49.4 1.0 %copy-start = (bf16[2,256,512]{2,1,0:T(8,128)(2,1)S(1)}, bf16[2,256,512]{2,1,0:T(8,128)(2,1)}, u32[]{:S(2)}) copy-start(bf16[2,256,512]{2,1,0:T(8,128)(2,1)} %b0.3) | copy-start | bytes 1572868
  50.4 1.2 %copy-start.3 = (bf16[2,256,512]{2,1,0:T(8,128)(2,1)S(1)}, bf16[2,256,512]{2,1,0:T(8,128)(2,1)}, u32[]{:S(2)}) copy-start(bf16[2,256,512]{2,1,0:T(8,128)(2,1)} %copy-done.2) | copy-start | bytes 1572868
  51.6 2.0 %copy-start.1 = (bf16[8,128,512]{2,1,0:T(8,128)(2,1)S(1)}, bf16[8,128,512]{2,1,0:T(8,128)(2,1)}, u32[]{:S(2)}) copy-start(bf16[8,128,512]{2,1,0:T(8,128)(2,1)} %own.1) | copy-start | bytes 3145732
  51.6 2.0 %copy-start.4 = (s32[8,2]{0,1:T(2,128)S(1)}, s32[8,2]{0,1:T(2,128)}, u32[]{:S(2)}) copy-start(s32[8,2]{0,1:T(2,128)} %param.9) | copy-start | bytes 196
  51.6 2.0 %copy-start.5 = (s32[8,4]{0,1:T(4,128)S(1)}, s32[8,4]{0,1:T(4,128)}, u32[]{:S(2)}) copy-start(s32[8,4]{0,1:T(4,128)} %param.10) | copy-start | bytes 388
  51.6 2.0 %copy-start.6 = (f32[512]{0:T(512)S(1)}, f32[512]{0:T(512)}, u32[]{:S(2)}) copy-start(f32[512]{0:T(512)} %param.12) | copy-start | bytes 6148
  51.6 2.0 %copy-start.7 = (f32[128]{0:T(128)S(1)}, f32[128]{0:T(128)}, u32[]{:S(2)}) copy-start(f32[128]{0:T(128)} %occ.1) | copy-start | bytes 1540

commit v3 on v2

--- a/solution.py
+++ b/solution.py
@@ -29,9 +29,23 @@
     return lax.ppermute(x, ("orb", "rep"), route)
 
 
+def diagonal(x, distance):
+    n, m = lax.axis_size("orb"), lax.axis_size("rep")
+    route = [(o * m + i, (o - 1) * m + i) for o in range(1, n, 2) for i in range(m)]
+    route += [
+        (o * m + i, (o - 1) * m + (i + distance) % m) for o in range(2, n, 2) for i in range(m)
+    ]
+    return lax.ppermute(x, ("orb", "rep"), route)
+
+
 def odd_to_even(x):
     n = lax.axis_size("orb")
     return lax.ppermute(x, "orb", [(o, o - 1) for o in range(1, n, 2)])
+
+
+def swapped(x):
+    n = lax.axis_size("orb")
+    return lax.ppermute(x, "orb", [(o, o ^ 1) for o in range(n)])
 
 
 def call(body, out_shape, in_specs, scratch=(), out_specs=None, limit=16):
@@ -46,7 +60,10 @@
     )
 
 
-def couple_kernel(ids, orbs, cpl, fock, occ, mine, energy, prev, own, nxt, pre, wgt, amps, sems):
+def couple_kernel(
+    orb, rep, ints, fock, occ, energies, prev, own, nxt, pre, wgt, amps, sems
+):
+    first = energies.shape[1] - own.shape[2]
     pair_count, rows = own.shape[:2]
     copies = [
         pltpu.make_async_copy(src, amps.at[pl.ds(k * pair_count, pair_count)], sems.at[k])
@@ -54,24 +71,25 @@
     ]
     for c in copies:
         c.start()
-    tile = jnp.broadcast_to(mine[...], (rows, rows))
+    mine = energies[:, pl.ds(pl.multiple_of(first + rep[0] * rows, rows), rows)]
+    tile = jnp.transpose(jnp.broadcast_to(mine, (rows, rows)))
 
     def denominators(p, carry):
-        shift = occ[orbs[0, p]] + occ[orbs[1, p]]
-        for c in range(0, energy.shape[1], rows):
-            part = slice(c, c + rows)
-            wgt[p, :, part] = damping / (tile + (energy[:, part] - shift))
+        shift = occ[0, ints[0, p]] + occ[0, ints[1, p]]
+        for c in range(0, own.shape[2], rows):
+            row = energies[:, first + c:first + c + rows]
+            wgt[p, :, c:c + rows] = damping / (tile + (row - shift))
         return carry
 
     lax.fori_loop(0, pair_count, denominators, 0)
     for c in copies:
         c.wait()
-    base = (ids[0] - 1) * pair_count
+    base = (orb[0] - 1) * pair_count
     step = 32
 
     def pair(p, carry):
-        slots = [cpl[c, p] - base for c in range(cpl.shape[0])]
-        scales = [fock[c, p] for c in range(cpl.shape[0])]
+        slots = [ints[2 + c, p] - base for c in range(fock.shape[0])]
+        scales = [fock[c, p] for c in range(fock.shape[0])]
         for r in range(0, rows, step):
             part = pl.ds(r, step)
             total = None
@@ -92,7 +110,7 @@
         pltpu.VMEM((3 * own.shape[0],) + own.shape[1:], own.dtype),
         pltpu.SemaphoreType.DMA((3,)),
     )
-    specs = [SMEM] * 5 + [VMEM] * 2 + [ANY] * 3
+    specs = [SMEM] * 5 + [VMEM] + [ANY] * 3
     return call(couple_kernel, (shape, shape), specs, scratch)(*args)
 
 
@@ -100,8 +118,8 @@
     return lax.dot_general(a, b, (((0,), (0,)), ((), ())), preferred_element_type=jnp.float32)
 
 
-def left_of(ids, blocks, rows):
-    start = pl.multiple_of(ids[1] * rows, rows)
+def left_of(rep, blocks, rows):
+    start = pl.multiple_of(rep[0] * rows, rows)
     return jnp.concatenate(
         [
             jnp.concatenate([b[i, :, pl.ds(start, rows)] for i in range(b.shape[0])], axis=1)
@@ -111,9 +129,9 @@
     )
 
 
-def products(ids, left, right, out):
+def products(rep, left, right, out):
     orbitals, _, rows, _ = out.shape
-    lhs = left_of(ids, left, rows)
+    lhs = left_of(rep, left, rows)
     for j in range(orbitals):
         both = dot_t(lhs, jnp.concatenate([r(j) for r in right], axis=0))
         for i in range(orbitals):
@@ -131,41 +149,59 @@
     return lambda j: ref[j]
 
 
-def either(ids, odd_ref, even_ref):
-    odd = lax.rem(ids[0], 2) == 1
+def either(orb, odd_ref, even_ref):
+    odd = lax.rem(orb[0], 2) == 1
     return lambda j: jnp.where(odd, odd_ref[j], even_ref[j])
 
 
-def own_part(ids, b0, b1, b2):
-    def body(ids, b0, b1, b2, out):
-        products(ids, (b0, b1, b2), [whole(b) for b in (b0, b1, b2)], out)
-
-    return call(body, acc_shape(b0), [SMEM] + [VMEM] * 3)(ids, b0, b1, b2)
-
-
-def next_part(ids, b0, b1, b2, n0, n1, n2x, n2c):
-    def body(ids, b0, b1, b2, n0, n1, n2x, n2c, out):
-        products(ids, (b0, b1, b2), [whole(n0), whole(n1), either(ids, n2x, n2c)], out)
-
-    return call(body, acc_shape(b0), [SMEM] + [VMEM] * 7)(ids, b0, b1, b2, n0, n1, n2x, n2c)
-
-
-def pair_slot(ids, orbs, p, orbitals):
-    base = ids[0] * orbitals
+def own_part(rep, b0, b1, b2):
+    def body(rep, b0, b1, b2, out, pack, sems):
+        orbitals = b0.shape[0]
+        copies = [
+            pltpu.make_async_copy(b, pack.at[pl.ds(k * orbitals, orbitals)], sems.at[k])
+            for k, b in enumerate((b1, b2))
+        ]
+        for c in copies:
+            c.start()
+        products(rep, (b0, b1, b2), [whole(b) for b in (b0, b1, b2)], out)
+        for c in copies:
+            c.wait()
+
+    pack = jax.ShapeDtypeStruct((2 * b0.shape[0],) + b0.shape[1:], b0.dtype)
+    return call(
+        body, (acc_shape(b0), pack), [SMEM] + [VMEM] * 3,
+        [pltpu.SemaphoreType.DMA((2,))], (VMEM, ANY),
+    )(rep, b0, b1, b2)
+
+
+def next_part(orb, rep, b0, b1, b2, n0, n1x, n2d, n12c):
+    def body(orb, rep, b0, b1, b2, n0, n1x, n2d, n12c, out):
+        orbitals = b0.shape[0]
+        lft = either(orb, n1x, n12c)
+        rgt = either(orb, n2d, n12c.at[orbitals:])
+        products(rep, (b0, b1, b2), [whole(n0), lft, rgt], out)
+
+    return call(body, acc_shape(b0), [SMEM] * 2 + [VMEM] * 7)(
+        orb, rep, b0, b1, b2, n0, n1x, n2d, n12c
+    )
+
+
+def pair_slot(orb, orbs, p, orbitals):
+    base = orb[0] * orbitals
     return orbs[0, p] - base, orbs[1, p] - base
 
 
-def partial_update(ids, orbs, own_acc, next_acc, pre, wgt, b3):
-    def body(ids, orbs, own_acc, next_acc, pre, wgt, b3, out, acc):
+def partial_update(orb, rep, orbs, own_acc, next_acc, pre, wgt, b3):
+    def body(orb, rep, orbs, own_acc, next_acc, pre, wgt, b3, out, acc):
         orbitals, _, rows, _ = own_acc.shape
-        lhs = left_of(ids, (b3,), rows)
+        lhs = left_of(rep, (b3,), rows)
         for j in range(orbitals):
             both = dot_t(lhs, b3[j])
             for i in range(orbitals):
                 acc[i, j] = own_acc[i, j] + both[i * rows:(i + 1) * rows]
 
         def pair(p, carry):
-            i, j = pair_slot(ids, orbs, p, orbitals)
+            i, j = pair_slot(orb, orbs, p, orbitals)
 
             @pl.when(j < orbitals)
             def _():
@@ -181,17 +217,17 @@
 
     return call(
         body, jax.ShapeDtypeStruct(pre.shape, jnp.float32),
-        [SMEM] * 2 + [VMEM] * 5, [pltpu.VMEM(own_acc.shape, own_acc.dtype)],
-    )(ids, orbs, own_acc, next_acc, pre, wgt, b3)
-
-
-def last_update(ids, orbs, part, wgt, left, n3x, n3c):
-    def body(ids, orbs, part, wgt, left, n3x, n3c, out, acc, done, sem):
+        [SMEM] * 3 + [VMEM] * 5, [pltpu.VMEM(own_acc.shape, own_acc.dtype)],
+    )(orb, rep, orbs, own_acc, next_acc, pre, wgt, b3)
+
+
+def last_update(orb, rep, orbs, part, wgt, left, n3x, n3c):
+    def body(orb, rep, orbs, part, wgt, left, n3x, n3c, out, acc, done, sem):
         orbitals = acc.shape[0]
-        products(ids, (left,), [either(ids, n3x, n3c)], acc)
+        products(rep, (left,), [either(orb, n3x, n3c)], acc)
 
         def pair(p, carry):
-            i, j = pair_slot(ids, orbs, p, orbitals)
+            i, j = pair_slot(orb, orbs, p, orbitals)
 
             @pl.when(j >= orbitals)
             def _():
@@ -219,40 +255,38 @@
     ]
     return call(
         body, jax.ShapeDtypeStruct(part.shape, jnp.bfloat16),
-        [SMEM] * 2 + [VMEM] * 5, scratch, out_specs=ANY,
-    )(ids, orbs, part, wgt, left, n3x, n3c)
+        [SMEM] * 3 + [VMEM] * 5, scratch, out_specs=ANY,
+    )(orb, rep, orbs, part, wgt, left, n3x, n3c)
 
 
 def device_step(
     blocks, amplitudes, pair_orbitals, coupling, fock_coupling, virtual_energy, occupied_energy
 ):
-    owner = lax.axis_index("orb").astype(jnp.int32)
-    replica = lax.axis_index("rep").astype(jnp.int32)
-    ids = jnp.stack([owner, replica])
-    orbs = pair_orbitals.T
+    orb = lax.axis_index("orb").astype(jnp.int32).reshape(1)
+    rep = lax.axis_index("rep").astype(jnp.int32).reshape(1)
     b0 = blocks
-    n0 = along_orb(b0, -1)
     b1 = along_rep(b0, 1)
     b2 = along_rep(b0, -1)
+    n2d = diagonal(b0, -1)
+    n0 = along_orb(b0, -1)
+    amps_prev = along_orb(amplitudes, 1)
     amps_next = along_orb(amplitudes, -1)
-    amps_prev = along_orb(amplitudes, 1)
-    n2x = along_rep_odd(n0, -1)
     b3 = along_rep(b1, 1)
-    n1 = along_orb(b1, -1)
-    n2c = odd_to_even(b2)
-    n3x = along_rep_odd(n2x, -1)
+    n3x = along_rep_odd(n2d, -1)
+    n1x = along_rep_odd(n0, 1)
+    own_acc, pack = own_part(rep, b0, b1, b2)
+    n12c = swapped(pack)
     n3c = odd_to_even(b3)
-    rows = amplitudes.shape[1]
-    row_e = lax.dynamic_slice_in_dim(virtual_energy, replica * rows, rows)[:, None]
     fock = fock_coupling.T.astype(jnp.float32)
+    ints = jnp.concatenate([pair_orbitals.T, coupling.T], axis=0)
+    energies = jnp.concatenate([occupied_energy[None, :], virtual_energy[None, :]], axis=1)
     pre, wgt = coupled_terms(
-        ids, orbs, coupling.T, fock, occupied_energy, row_e, virtual_energy[None, :],
+        orb, rep, ints, fock, energies, energies,
         amps_prev, amplitudes, amps_next,
     )
-    own_acc = own_part(ids, b0, b1, b2)
-    next_acc = next_part(ids, b0, b1, b2, n0, n1, n2x, n2c)
-    part = partial_update(ids, orbs, own_acc, next_acc, pre, wgt, b3)
-    return last_update(ids, orbs, part, wgt, b3, n3x, n3c)
+    next_acc = next_part(orb, rep, b0, b1, b2, n0, n1x, n2d, n12c)
+    part = partial_update(orb, rep, ints, own_acc, next_acc, pre, wgt, b3)
+    return last_update(orb, rep, ints, part, wgt, b3, n3x, n3c)
 
 
 def solution(mesh):

time: 61.5 us -> 57.5 us (0.935)
  the two profiles are of different devices: /device:TPU:24 before, /device:TPU:25 now
where the time goes in v3:
time: 57.5 us; the launch traced here: 56.5 us
  starting transfers between devices  33.1 us (58%)
  Pallas kernels  10.8 us (19%)
  waiting for transfers between devices  8 us (14%)
  local copies, waits for them, and re-layouts  2.26 us (4%)
  other arithmetic  2.07 us (4%)
    ppermute x3, starting transfers between devices, along_orb(): lax.ppermute(x, 'orb', [(i - distance, i) for i in range(n) if 0 <= i - d...  10.7 us
    ppermute x3, waiting for transfers between devices, along_rep(): return lax.ppermute(x, 'rep', [(i, (i + distance) % n) for i in range(n)])  7.97 us
    ppermute x2, starting transfers between devices, along_rep_odd(): return lax.ppermute(x, ('orb', 'rep'), route)  6.48 us
    ppermute x1, starting transfers between devices, diagonal(): return lax.ppermute(x, ('orb', 'rep'), route)  5.3 us
    ppermute x1, starting transfers between devices, odd_to_even(): return lax.ppermute(x, 'orb', [(o, o - 1) for o in range(1, n, 2)])  4.21 us
    ppermute x1, starting transfers between devices, swapped(): return lax.ppermute(x, 'orb', [(o, o ^ 1) for o in range(n)])  3.65 us
    pallas_call x1, Pallas kernels, coupled_terms(): return call(couple_kernel, (shape, shape), specs, scratch)(*args)  3.39 us
    ppermute x3, starting transfers between devices, along_rep(): return lax.ppermute(x, 'rep', [(i, (i + distance) % n) for i in range(n)])  2.79 us
  transfers between devices with their start and end apart: 11, of which 1 were waited for; matrix products, arithmetic and copies ran while one was open for 4% of the time, Pallas kernels for 15%

profile of v3, /device:TPU:25, one launch (start us, length us, event | category | flops | bytes accessed | tf_op | source)
XLA Modules:
  0.0 56.5 jit_solution(17268747784020616700)
XLA Ops:
  0.0 1.2 %collective-permute-start = (bf16[2,256,512]{2,1,0:T(8,128)(2,1)}, bf16[2,256,512]{2,1,0:T(8,128)(2,1)S(1)}, u32[]{:S(2)}, u32[]{:S(2)}) collective-permute-start(bf16[2,256,512]{2,1,0:T(8,128)(2,1)} %b0.3), channel_id=1, source_target_pairs={{0,1},{1,2},{2,3},{3,0},{4,5},{5,6},{6,7},{7,4},{8,9},{9,10},{10,1... | collective-permute-start | bytes 1572872 | tf_op jit(solution)/shard_map/ppermute | solution.py:23
  1.2 1.5 %collective-permute-start.1 = (bf16[2,256,512]{2,1,0:T(8,128)(2,1)}, bf16[2,256,512]{2,1,0:T(8,128)(2,1)S(1)}, u32[]{:S(2)}, u32[]{:S(2)}) collective-permute-start(bf16[2,256,512]{2,1,0:T(8,128)(2,1)} %b0.3), channel_id=1, source_target_pairs={{0,3},{1,0},{2,1},{3,2},{4,7},{5,4},{6,5},{7,6},{8,11},{9,8},{10,9... | collective-permute-start | bytes 1572872 | tf_op jit(solution)/shard_map/ppermute | solution.py:23
  2.7 4.7 %collective-permute-start.6 = (bf16[8,128,512]{2,1,0:T(8,128)(2,1)}, bf16[8,128,512]{2,1,0:T(8,128)(2,1)}, u32[]{:S(2)}, u32[]{:S(2)}) collective-permute-start(bf16[8,128,512]{2,1,0:T(8,128)(2,1)} %own.1), channel_id=1, source_target_pairs={{0,4},{4,8},{8,12},{12,16},{16,20},{20,24},{24,28},{28,32},{32,36}... | collective-permute-start | bytes 3145736 | tf_op jit(solution)/shard_map/ppermute | solution.py:18
  7.3 1.9 %collective-permute-start.2 = (bf16[2,256,512]{2,1,0:T(8,128)(2,1)}, bf16[2,256,512]{2,1,0:T(8,128)(2,1)}, u32[]{:S(2)}, u32[]{:S(2)}) collective-permute-start(bf16[2,256,512]{2,1,0:T(8,128)(2,1)} %b0.3), channel_id=1, source_target_pairs={{4,0},{8,4},{12,8},{16,12},{20,16},{24,20},{28,24},{32,28},{36,32}... | collective-permute-start | bytes 1572872 | tf_op jit(solution)/shard_map/ppermute | solution.py:18
  9.3 5.3 %collective-permute-start.4 = (bf16[2,256,512]{2,1,0:T(8,128)(2,1)}, bf16[2,256,512]{2,1,0:T(8,128)(2,1)}, u32[]{:S(2)}, u32[]{:S(2)}) collective-permute-start(bf16[2,256,512]{2,1,0:T(8,128)(2,1)} %b0.3), channel_id=1, source_target_pairs={{4,0},{5,1},{6,2},{7,3},{12,8},{13,9},{14,10},{15,11},{20,16},{21,... | collective-permute-start | bytes 1572872 | tf_op jit(solution)/shard_map/ppermute | solution.py:38
  14.6 0.0 collective-permute-done.b1
  14.6 4.1 %collective-permute-start.7 = (bf16[8,128,512]{2,1,0:T(8,128)(2,1)}, bf16[8,128,512]{2,1,0:T(8,128)(2,1)}, u32[]{:S(2)}, u32[]{:S(2)}) collective-permute-start(bf16[8,128,512]{2,1,0:T(8,128)(2,1)} %own.1), channel_id=1, source_target_pairs={{4,0},{8,4},{12,8},{16,12},{20,16},{24,20},{28,24},{32,28},{36,32}... | collective-permute-start | bytes 3145736 | tf_op jit(solution)/shard_map/ppermute | solution.py:18
  18.7 0.0 collective-permute-done.1.b2
  18.7 0.0 copy-start
  18.8 1.0 %copy-done = bf16[2,256,512]{2,1,0:T(8,128)(2,1)S(1)} copy-done((bf16[2,256,512]{2,1,0:T(8,128)(2,1)S(1)}, bf16[2,256,512]{2,1,0:T(8,128)(2,1)}, u32[]{:S(2)}) %copy-start) | copy-done | bytes 524312
  19.8 0.0 copy-start.1
  19.8 1.1 %shard_map.73 = (f32[2,2,128,512]{3,2,1,0:T(8,128)S(1)}, bf16[4,256,512]{2,1,0:T(8,128)(2,1)}) custom-call(s32[1]{0:T(128)} %bitcast.1.rep, bf16[2,256,512]{2,1,0:T(8,128)(2,1)S(1)} %copy-done, bf16[2,256,512]{2,1,0:T(8,128)(2,1)S(1)} %collective-permute-done.b1, bf16[2,256,512]{2,1,0:T(8,128)(2,1)S(1)} %collective-permute-done.1.b2), custom_call_target="tpu_custom_call" | custom-call | flops 100000000 | bytes 4194304 | tf_op jit(solution)/shard_map/pallas_call | solution.py:171
  20.9 3.6 %collective-permute-start.5 = (bf16[4,256,512]{2,1,0:T(8,128)(2,1)}, bf16[4,256,512]{2,1,0:T(8,128)(2,1)}, u32[]{:S(2)}, u32[]{:S(2)}) collective-permute-start(bf16[4,256,512]{2,1,0:T(8,128)(2,1)} %get-tuple-element.10), channel_id=1, source_target_pairs={{0,4},{4,0},{8,12},{12,8},{16,20},{20,16},{24,28},{28,24},{32,36},... | collective-permute-start | bytes 3145736 | tf_op jit(solution)/shard_map/ppermute | solution.py:48
  24.5 0.0 collective-permute-done.2.n0
  24.5 0.1 collective-permute-start.8
  24.6 0.0 collective-permute-done.4.n2d
  24.6 3.1 %collective-permute-start.3 = (bf16[2,256,512]{2,1,0:T(8,128)(2,1)}, bf16[2,256,512]{2,1,0:T(8,128)(2,1)}, u32[]{:S(2)}, u32[]{:S(2)}) collective-permute-start(bf16[2,256,512]{2,1,0:T(8,128)(2,1)} %collective-permute-done.2.n0), channel_id=1, source_target_pairs={{0,0},{1,1},{2,2},{3,3},{4,5},{5,6},{6,7},{7,4},{8,8},{9,9},{10,10... | collective-permute-start | bytes 1572872 | tf_op jit(solution)/shard_map/ppermute | solution.py:29
  27.7 0.0 collective-permute-done.6.prev
  27.7 3.4 %collective-permute-start.9 = (bf16[2,256,512]{2,1,0:T(8,128)(2,1)}, bf16[2,256,512]{2,1,0:T(8,128)(2,1)}, u32[]{:S(2)}, u32[]{:S(2)}) collective-permute-start(bf16[2,256,512]{2,1,0:T(8,128)(2,1)} %collective-permute-done.4.n2d), channel_id=1, source_target_pairs={{0,0},{1,1},{2,2},{3,3},{4,7},{5,4},{6,5},{7,6},{8,8},{9,9},{10,10... | collective-permute-start | bytes 1572872 | tf_op jit(solution)/shard_map/ppermute | solution.py:29
  31.1 8.0 %collective-permute-done.8.b3.left = bf16[2,256,512]{2,1,0:T(8,128)(2,1)S(1)} collective-permute-done((bf16[2,256,512]{2,1,0:T(8,128)(2,1)S(1)}, bf16[2,256,512]{2,1,0:T(8,128)(2,1)S(1)}, u32[]{:S(2)}, u32[]{:S(2)}) %collective-permute-start.8) | collective-permute-done | bytes 524320 | tf_op jit(solution)/shard_map/ppermute | solution.py:23
  39.1 4.2 %collective-permute-start.10 = (bf16[2,256,512]{2,1,0:T(8,128)(2,1)S(1)}, bf16[2,256,512]{2,1,0:T(8,128)(2,1)}, u32[]{:S(2)}, u32[]{:S(2)}) collective-permute-start(bf16[2,256,512]{2,1,0:T(8,128)(2,1)S(1)} %collective-permute-done.8.b3.left), channel_id=1, source_target_pairs={{4,0},{12,8},{20,16},{28,24},{36,32},{44,40},{52,48},{60,56},{68,6... | collective-permute-start | bytes 1572872 | tf_op jit(solution)/shard_map/ppermute | solution.py:43
  43.3 0.7 %pad_maximum_fusion.occ.energies = f32[1,640]{1,0:T(1,128)S(1)} fusion(f32[1,512]{1,0:T(1,128)} %bitcast.9, f32[1,128]{1,0:T(1,128)} %bitcast.11), kind=kLoop, calls=%fused_computation.1 | loop fusion | flops 640 | bytes 5120 | tf_op jit(solution)/shard_map/concatenate | solution.py:282
  44.0 0.7 %pad_add_fusion.ints.orbs = s32[6,8]{1,0:T(8,128)S(1)} fusion(s32[4,8]{1,0:T(4,128)} %bitcast.8, s32[2,8]{1,0:T(2,128)} %bitcast.10), kind=kLoop, calls=%fused_computation | loop fusion | flops 48 | bytes 384 | tf_op jit(solution)/shard_map/concatenate | solution.py:281
  44.7 0.7 %convert_bitcast_fusion.fock = f32[4,8]{1,0:T(4,128)S(1)} fusion(bf16[8,4]{0,1:T(4,128)(2,1)} %param.11), kind=kLoop, calls=%fused_computation.2 | loop fusion | flops 32 | bytes 192 | tf_op jit(solution)/shard_map/convert_element_type | solution.py:280
  45.4 0.0 collective-permute-done.7.nxt
  45.4 0.0 copy-start.2
  45.4 1.2 %copy-done.2 = bf16[8,128,512]{2,1,0:T(8,128)(2,1)S(1)} copy-done((bf16[8,128,512]{2,1,0:T(8,128)(2,1)S(1)}, bf16[8,128,512]{2,1,0:T(8,128)(2,1)}, u32[]{:S(2)}) %copy-start.2) | copy-done | bytes 1048600
  46.6 3.4 %shard_map.75 = (f32[8,128,512]{2,1,0:T(8,128)S(1)}, f32[8,128,512]{2,1,0:T(8,128)S(1)}) custom-call(s32[1]{0:T(128)} %bitcast.orb, s32[1]{0:T(128)} %bitcast.1.rep, s32[6,8]{1,0:T(8,128)S(1)} %pad_add_fusion.ints.orbs, f32[4,8]{1,0:T(4,128)S(1)} %convert_bitcast_fusion.fock, f32[1,640]{1,0:T(1,128)S(1)} %pad_maximum_fusion.occ.energies, ...), custom_call_target="tpu_custom_call" | custom-call | flops 100000000 | bytes 4194304 | tf_op jit(solution)/shard_map/pallas_call | solution.py:114
  50.0 0.0 collective-permute-done.3.n1x
  50.0 0.0 collective-permute-done.5.n12c
  50.0 0.0 copy-done.1
  50.0 2.3 %shard_map.74.next_acc = f32[2,2,128,512]{3,2,1,0:T(8,128)S(1)} custom-call(s32[1]{0:T(128)} %bitcast.orb, s32[1]{0:T(128)} %bitcast.1.rep, bf16[2,256,512]{2,1,0:T(8,128)(2,1)S(1)} %copy-done.1, bf16[2,256,512]{2,1,0:T(8,128)(2,1)S(1)} %collective-permute-done.b1, bf16[2,256,512]{2,1,0:T(8,128)(2,1)S(1)} %collective-permute-done.1.b2, ...), custom_call_target="tpu_custom_call" | custom-call | flops 100000000 | bytes 4194304 | tf_op jit(solution)/shard_map/pallas_call | solution.py:184
  52.4 1.4 %shard_map.76.part = f32[8,128,512]{2,1,0:T(8,128)S(1)} custom-call(s32[1]{0:T(128)} %bitcast.orb, s32[1]{0:T(128)} %bitcast.1.rep, s32[6,8]{1,0:T(8,128)S(1)} %pad_add_fusion.ints.orbs, f32[2,2,128,512]{3,2,1,0:T(8,128)S(1)} %get-tuple-element.9.own_acc, f32[2,2,128,512]{3,2,1,0:T(8,128)S(1)} %shard_map.74.next_acc, ...), custom_call_target="tpu_custom_call" | custom-call | flops 100000000 | bytes 4194304 | tf_op jit(solution)/shard_map/pallas_call | solution.py:218
  53.8 0.0 collective-permute-done.9.n3x
  53.8 0.0 collective-permute-done.10.n3c
  53.8 2.6 %shard_map.77 = bf16[8,128,512]{2,1,0:T(8,128)(2,1)} custom-call(s32[1]{0:T(128)} %bitcast.orb, s32[1]{0:T(128)} %bitcast.1.rep, s32[6,8]{1,0:T(8,128)S(1)} %pad_add_fusion.ints.orbs, f32[8,128,512]{2,1,0:T(8,128)S(1)} %shard_map.76.part, f32[8,128,512]{2,1,0:T(8,128)S(1)} %get-tuple-element.12.wgt, bf16[2,256,512]{2,1,0:T(8,128)(2,1)S(1)} %collective-permute-done.8.b3.left, ...), custom_call_target="tpu_custom_call" | custom-call | flops 100000000 | bytes 4194304 | tf_op jit(solution)/shard_map/pallas_call | solution.py:256
Async XLA Ops:
  0.0 14.6 %collective-permute-start = (bf16[2,256,512]{2,1,0:T(8,128)(2,1)}, bf16[2,256,512]{2,1,0:T(8,128)(2,1)S(1)}, u32[]{:S(2)}, u32[]{:S(2)}) collective-permute-start(bf16[2,256,512]{2,1,0:T(8,128)(2,1)} %b0.3), channel_id=1, source_target_pairs={{0,1},{1,2},{2,3},{3,0},{4,5},{5,6},{6,7},{7,4},{8,9},{9,10},{10,1... | collective-permute-start | bytes 1572872 | tf_op jit(solution)/shard_map/ppermute | solution.py:23
  1.2 17.5 %collective-permute-start.1 = (bf16[2,256,512]{2,1,0:T(8,128)(2,1)}, bf16[2,256,512]{2,1,0:T(8,128)(2,1)S(1)}, u32[]{:S(2)}, u32[]{:S(2)}) collective-permute-start(bf16[2,256,512]{2,1,0:T(8,128)(2,1)} %b0.3), channel_id=1, source_target_pairs={{0,3},{1,0},{2,1},{3,2},{4,7},{5,4},{6,5},{7,6},{8,11},{9,8},{10,9... | collective-permute-start | bytes 1572872 | tf_op jit(solution)/shard_map/ppermute | solution.py:23
  2.7 25.1 %collective-permute-start.6 = (bf16[8,128,512]{2,1,0:T(8,128)(2,1)}, bf16[8,128,512]{2,1,0:T(8,128)(2,1)}, u32[]{:S(2)}, u32[]{:S(2)}) collective-permute-start(bf16[8,128,512]{2,1,0:T(8,128)(2,1)} %own.1), channel_id=1, source_target_pairs={{0,4},{4,8},{8,12},{12,16},{16,20},{20,24},{24,28},{28,32},{32,36}... | collective-permute-start | bytes 3145736 | tf_op jit(solution)/shard_map/ppermute | solution.py:18
  7.3 17.2 %collective-permute-start.2 = (bf16[2,256,512]{2,1,0:T(8,128)(2,1)}, bf16[2,256,512]{2,1,0:T(8,128)(2,1)}, u32[]{:S(2)}, u32[]{:S(2)}) collective-permute-start(bf16[2,256,512]{2,1,0:T(8,128)(2,1)} %b0.3), channel_id=1, source_target_pairs={{4,0},{8,4},{12,8},{16,12},{20,16},{24,20},{28,24},{32,28},{36,32}... | collective-permute-start | bytes 1572872 | tf_op jit(solution)/shard_map/ppermute | solution.py:18
  9.3 15.3 %collective-permute-start.4 = (bf16[2,256,512]{2,1,0:T(8,128)(2,1)}, bf16[2,256,512]{2,1,0:T(8,128)(2,1)}, u32[]{:S(2)}, u32[]{:S(2)}) collective-permute-start(bf16[2,256,512]{2,1,0:T(8,128)(2,1)} %b0.3), channel_id=1, source_target_pairs={{4,0},{5,1},{6,2},{7,3},{12,8},{13,9},{14,10},{15,11},{20,16},{21,... | collective-permute-start | bytes 1572872 | tf_op jit(solution)/shard_map/ppermute | solution.py:38
  14.6 30.8 %collective-permute-start.7 = (bf16[8,128,512]{2,1,0:T(8,128)(2,1)}, bf16[8,128,512]{2,1,0:T(8,128)(2,1)}, u32[]{:S(2)}, u32[]{:S(2)}) collective-permute-start(bf16[8,128,512]{2,1,0:T(8,128)(2,1)} %own.1), channel_id=1, source_target_pairs={{4,0},{8,4},{12,8},{16,12},{20,16},{24,20},{28,24},{32,28},{36,32}... | collective-permute-start | bytes 3145736 | tf_op jit(solution)/shard_map/ppermute | solution.py:18
  18.7 1.0 %copy-start = (bf16[2,256,512]{2,1,0:T(8,128)(2,1)S(1)}, bf16[2,256,512]{2,1,0:T(8,128)(2,1)}, u32[]{:S(2)}) copy-start(bf16[2,256,512]{2,1,0:T(8,128)(2,1)} %b0.3) | copy-start | bytes 1572868
  19.8 30.2 %copy-start.1 = (bf16[2,256,512]{2,1,0:T(8,128)(2,1)S(1)}, bf16[2,256,512]{2,1,0:T(8,128)(2,1)}, u32[]{:S(2)}) copy-start(bf16[2,256,512]{2,1,0:T(8,128)(2,1)} %b0.3) | copy-start | bytes 1572868
  20.9 29.2 %collective-permute-start.5 = (bf16[4,256,512]{2,1,0:T(8,128)(2,1)}, bf16[4,256,512]{2,1,0:T(8,128)(2,1)}, u32[]{:S(2)}, u32[]{:S(2)}) collective-permute-start(bf16[4,256,512]{2,1,0:T(8,128)(2,1)} %get-tuple-element.10), channel_id=1, source_target_pairs={{0,4},{4,0},{8,12},{12,8},{16,20},{20,16},{24,28},{28,24},{32,36},... | collective-permute-start | bytes 3145736 | tf_op jit(solution)/shard_map/ppermute | solution.py:48
  24.5 14.6 %collective-permute-start.8 = (bf16[2,256,512]{2,1,0:T(8,128)(2,1)S(1)}, bf16[2,256,512]{2,1,0:T(8,128)(2,1)S(1)}, u32[]{:S(2)}, u32[]{:S(2)}) collective-permute-start(bf16[2,256,512]{2,1,0:T(8,128)(2,1)S(1)} %collective-permute-done.b1), channel_id=1, source_target_pairs={{0,1},{1,2},{2,3},{3,0},{4,5},{5,6},{6,7},{7,4},{8,9},{9,10},{10,1... | collective-permute-start | bytes 1572872 | tf_op jit(solution)/shard_map/ppermute | solution.py:23
  24.6 25.4 %collective-permute-start.3 = (bf16[2,256,512]{2,1,0:T(8,128)(2,1)}, bf16[2,256,512]{2,1,0:T(8,128)(2,1)}, u32[]{:S(2)}, u32[]{:S(2)}) collective-permute-start(bf16[2,256,512]{2,1,0:T(8,128)(2,1)} %collective-permute-done.2.n0), channel_id=1, source_target_pairs={{0,0},{1,1},{2,2},{3,3},{4,5},{5,6},{6,7},{7,4},{8,8},{9,9},{10,10... | collective-permute-start | bytes 1572872 | tf_op jit(solution)/shard_map/ppermute | solution.py:29
  27.7 26.1 %collective-permute-start.9 = (bf16[2,256,512]{2,1,0:T(8,128)(2,1)}, bf16[2,256,512]{2,1,0:T(8,128)(2,1)}, u32[]{:S(2)}, u32[]{:S(2)}) collective-permute-start(bf16[2,256,512]{2,1,0:T(8,128)(2,1)} %collective-permute-done.4.n2d), channel_id=1, source_target_pairs={{0,0},{1,1},{2,2},{3,3},{4,7},{5,4},{6,5},{7,6},{8,8},{9,9},{10,10... | collective-permute-start | bytes 1572872 | tf_op jit(solution)/shard_map/ppermute | solution.py:29
  39.1 14.7 %collective-permute-start.10 = (bf16[2,256,512]{2,1,0:T(8,128)(2,1)S(1)}, bf16[2,256,512]{2,1,0:T(8,128)(2,1)}, u32[]{:S(2)}, u32[]{:S(2)}) collective-permute-start(bf16[2,256,512]{2,1,0:T(8,128)(2,1)S(1)} %collective-permute-done.8.b3.left), channel_id=1, source_target_pairs={{4,0},{12,8},{20,16},{28,24},{36,32},{44,40},{52,48},{60,56},{68,6... | collective-permute-start | bytes 1572872 | tf_op jit(solution)/shard_map/ppermute | solution.py:43
  45.4 1.2 %copy-start.2 = (bf16[8,128,512]{2,1,0:T(8,128)(2,1)S(1)}, bf16[8,128,512]{2,1,0:T(8,128)(2,1)}, u32[]{:S(2)}) copy-start(bf16[8,128,512]{2,1,0:T(8,128)(2,1)} %own.1) | copy-start | bytes 3145732

commit v4 on v2

--- a/solution.py
+++ b/solution.py
@@ -25,7 +25,7 @@
 
 def along_rep_odd(x, distance):
     n, m = lax.axis_size("orb"), lax.axis_size("rep")
-    route = [(o * m + i, o * m + (i + distance * (o % 2)) % m) for o in range(n) for i in range(m)]
+    route = [(o * m + i, o * m + (i + distance) % m) for o in range(1, n, 2) for i in range(m)]
     return lax.ppermute(x, ("orb", "rep"), route)
 
 
@@ -111,20 +111,20 @@
     )
 
 
-def products(ids, left, right, out):
+def products(ids, left, right, out, offset=0, base=None):
     orbitals, _, rows, _ = out.shape
     lhs = left_of(ids, left, rows)
-    for j in range(orbitals):
+    for j in range(left[0].shape[0]):
         both = dot_t(lhs, jnp.concatenate([r(j) for r in right], axis=0))
         for i in range(orbitals):
-            out[i, j] = both[i * rows:(i + 1) * rows]
-
-
-def acc_shape(block):
+            part = both[i * rows:(i + 1) * rows]
+            out[i, offset + j] = part if base is None else base[i, orbitals + j] + part
+
+
+def acc_shape(block, columns=1):
     orbitals, _, width = block.shape
-    return jax.ShapeDtypeStruct(
-        (orbitals, orbitals, width // lax.axis_size("rep"), width), jnp.float32
-    )
+    rows = width // lax.axis_size("rep")
+    return jax.ShapeDtypeStruct((orbitals, columns * orbitals, rows, width), jnp.float32)
 
 
 def whole(ref):
@@ -136,18 +136,19 @@
     return lambda j: jnp.where(odd, odd_ref[j], even_ref[j])
 
 
-def own_part(ids, b0, b1, b2):
-    def body(ids, b0, b1, b2, out):
+def own_part(ids, b0, b1, b2, n0):
+    def body(ids, b0, b1, b2, n0, out):
         products(ids, (b0, b1, b2), [whole(b) for b in (b0, b1, b2)], out)
-
-    return call(body, acc_shape(b0), [SMEM] + [VMEM] * 3)(ids, b0, b1, b2)
-
-
-def next_part(ids, b0, b1, b2, n0, n1, n2x, n2c):
-    def body(ids, b0, b1, b2, n0, n1, n2x, n2c, out):
-        products(ids, (b0, b1, b2), [whole(n0), whole(n1), either(ids, n2x, n2c)], out)
-
-    return call(body, acc_shape(b0), [SMEM] + [VMEM] * 7)(ids, b0, b1, b2, n0, n1, n2x, n2c)
+        products(ids, (b0,), [whole(n0)], out, b0.shape[0])
+
+    return call(body, acc_shape(b0, 2), [SMEM] + [VMEM] * 4)(ids, b0, b1, b2, n0)
+
+
+def next_part(ids, acc, b1, b2, n1, n2x, n2c):
+    def body(ids, acc, b1, b2, n1, n2x, n2c, out):
+        products(ids, (b1, b2), [whole(n1), either(ids, n2x, n2c)], out, 0, acc)
+
+    return call(body, acc_shape(b1), [SMEM] + [VMEM] * 6)(ids, acc, b1, b2, n1, n2x, n2c)
 
 
 def pair_slot(ids, orbs, p, orbitals):
@@ -157,7 +158,7 @@
 
 def partial_update(ids, orbs, own_acc, next_acc, pre, wgt, b3):
     def body(ids, orbs, own_acc, next_acc, pre, wgt, b3, out, acc):
-        orbitals, _, rows, _ = own_acc.shape
+        orbitals, _, rows, _ = next_acc.shape
         lhs = left_of(ids, (b3,), rows)
         for j in range(orbitals):
             both = dot_t(lhs, b3[j])
@@ -181,7 +182,7 @@
 
     return call(
         body, jax.ShapeDtypeStruct(pre.shape, jnp.float32),
-        [SMEM] * 2 + [VMEM] * 5, [pltpu.VMEM(own_acc.shape, own_acc.dtype)],
+        [SMEM] * 2 + [VMEM] * 5, [pltpu.VMEM(next_acc.shape, next_acc.dtype)],
     )(ids, orbs, own_acc, next_acc, pre, wgt, b3)
 
 
@@ -249,8 +250,8 @@
         ids, orbs, coupling.T, fock, occupied_energy, row_e, virtual_energy[None, :],
         amps_prev, amplitudes, amps_next,
     )
-    own_acc = own_part(ids, b0, b1, b2)
-    next_acc = next_part(ids, b0, b1, b2, n0, n1, n2x, n2c)
+    own_acc = own_part(ids, b0, b1, b2, n0)
+    next_acc = next_part(ids, own_acc, b1, b2, n1, n2x, n2c)
     part = partial_update(ids, orbs, own_acc, next_acc, pre, wgt, b3)
     return last_update(ids, orbs, part, wgt, b3, n3x, n3c)
 

time: 61.5 us -> 61.1 us (level)
  the two profiles are of different devices: /device:TPU:24 before, /device:TPU:27 now
where the time goes in v4:
time: 61.1 us; the launch traced here: 60.6 us
  starting transfers between devices  36.6 us (60%)
  Pallas kernels  10 us (16%)
  waiting for transfers between devices  8.44 us (14%)
  local copies, waits for them, and re-layouts  4.57 us (7%)
  other arithmetic  0.76 us (1%)
    ppermute x4, starting transfers between devices, along_orb(): lax.ppermute(x, 'orb', [(i - distance, i) for i in range(n) if 0 <= i - d...  15 us
    ppermute x2, starting transfers between devices, odd_to_even(): return lax.ppermute(x, 'orb', [(o, o - 1) for o in range(1, n, 2)])  12.1 us
    ppermute x3, waiting for transfers between devices, along_rep(): return lax.ppermute(x, 'rep', [(i, (i + distance) % n) for i in range(n)])  8.42 us
    ppermute x2, starting transfers between devices, along_rep_odd(): return lax.ppermute(x, ('orb', 'rep'), route)  6.75 us
    unnamed x20, local copies, waits for them, and re-layouts  3.69 us
    pallas_call x1, Pallas kernels, coupled_terms(): return call(couple_kernel, (shape, shape), specs, scratch)(*args)  3.12 us
    ppermute x3, starting transfers between devices, along_rep(): return lax.ppermute(x, 'rep', [(i, (i + distance) % n) for i in range(n)])  2.75 us
    pallas_call x1, Pallas kernels, last_update(): call(body, jax.ShapeDtypeStruct(part.shape, jnp.bfloat16), [SMEM] * 2 + [...  2.64 us
  transfers between devices with their start and end apart: 11, of which 1 were waited for; matrix products, arithmetic and copies ran while one was open for 3% of the time, Pallas kernels for 12%

profile of v4, /device:TPU:27, one launch (start us, length us, event | category | flops | bytes accessed | tf_op | source)
XLA Modules:
  0.0 60.6 jit_solution(13343937578329524547)
XLA Ops:
  0.0 1.2 %collective-permute-start = (bf16[2,256,512]{2,1,0:T(8,128)(2,1)}, bf16[2,256,512]{2,1,0:T(8,128)(2,1)S(1)}, u32[]{:S(2)}, u32[]{:S(2)}) collective-permute-start(bf16[2,256,512]{2,1,0:T(8,128)(2,1)} %b0.1), channel_id=1, source_target_pairs={{0,1},{1,2},{2,3},{3,0},{4,5},{5,6},{6,7},{7,4},{8,9},{9,10},{10,1... | collective-permute-start | bytes 1572872 | tf_op jit(solution)/shard_map/ppermute | solution.py:23
  1.2 0.3 collective-permute-start.1
  1.5 3.1 %collective-permute-start.2 = (bf16[2,256,512]{2,1,0:T(8,128)(2,1)}, bf16[2,256,512]{2,1,0:T(8,128)(2,1)S(1)}, u32[]{:S(2)}, u32[]{:S(2)}) collective-permute-start(bf16[2,256,512]{2,1,0:T(8,128)(2,1)} %b0.1), channel_id=1, source_target_pairs={{4,0},{8,4},{12,8},{16,12},{20,16},{24,20},{28,24},{32,28},{36,32}... | collective-permute-start | bytes 1572872 | tf_op jit(solution)/shard_map/ppermute | solution.py:18
  4.6 8.4 %collective-permute-done.b1 = bf16[2,256,512]{2,1,0:T(8,128)(2,1)S(1)} collective-permute-done((bf16[2,256,512]{2,1,0:T(8,128)(2,1)}, bf16[2,256,512]{2,1,0:T(8,128)(2,1)S(1)}, u32[]{:S(2)}, u32[]{:S(2)}) %collective-permute-start) | collective-permute-done | bytes 524320 | tf_op jit(solution)/shard_map/ppermute | solution.py:23
  13.0 3.4 %collective-permute-start.3 = (bf16[2,256,512]{2,1,0:T(8,128)(2,1)S(1)}, bf16[2,256,512]{2,1,0:T(8,128)(2,1)S(1)}, u32[]{:S(2)}, u32[]{:S(2)}) collective-permute-start(bf16[2,256,512]{2,1,0:T(8,128)(2,1)S(1)} %collective-permute-done.b1), channel_id=1, source_target_pairs={{4,0},{8,4},{12,8},{16,12},{20,16},{24,20},{28,24},{32,28},{36,32}... | collective-permute-start | bytes 1572872 | tf_op jit(solution)/shard_map/ppermute | solution.py:18
  16.5 3.4 %collective-permute-start.6 = (bf16[8,128,512]{2,1,0:T(8,128)(2,1)}, bf16[8,128,512]{2,1,0:T(8,128)(2,1)S(1)}, u32[]{:S(2)}, u32[]{:S(2)}) collective-permute-start(bf16[8,128,512]{2,1,0:T(8,128)(2,1)} %own.1), channel_id=1, source_target_pairs={{0,4},{4,8},{8,12},{12,16},{16,20},{20,24},{24,28},{28,32},{32,36}... | collective-permute-start | bytes 3145736 | tf_op jit(solution)/shard_map/ppermute | solution.py:18
  19.9 5.0 %collective-permute-start.7 = (bf16[8,128,512]{2,1,0:T(8,128)(2,1)}, bf16[8,128,512]{2,1,0:T(8,128)(2,1)}, u32[]{:S(2)}, u32[]{:S(2)}) collective-permute-start(bf16[8,128,512]{2,1,0:T(8,128)(2,1)} %own.1), channel_id=1, source_target_pairs={{4,0},{8,4},{12,8},{16,12},{20,16},{24,20},{28,24},{32,28},{36,32}... | collective-permute-start | bytes 3145736 | tf_op jit(solution)/shard_map/ppermute | solution.py:18
  24.9 0.0 collective-permute-done.1.b2
  24.9 1.3 %collective-permute-start.8 = (bf16[2,256,512]{2,1,0:T(8,128)(2,1)S(1)}, bf16[2,256,512]{2,1,0:T(8,128)(2,1)S(1)}, u32[]{:S(2)}, u32[]{:S(2)}) collective-permute-start(bf16[2,256,512]{2,1,0:T(8,128)(2,1)S(1)} %collective-permute-done.b1), channel_id=1, source_target_pairs={{0,1},{1,2},{2,3},{3,0},{4,5},{5,6},{6,7},{7,4},{8,9},{9,10},{10,1... | collective-permute-start | bytes 1572872 | tf_op jit(solution)/shard_map/ppermute | solution.py:23
  26.2 0.0 collective-permute-done.2.n0
  26.2 2.2 %collective-permute-start.4 = (bf16[2,256,512]{2,1,0:T(8,128)(2,1)S(1)}, bf16[2,256,512]{2,1,0:T(8,128)(2,1)S(1)}, u32[]{:S(2)}, u32[]{:S(2)}) collective-permute-start(bf16[2,256,512]{2,1,0:T(8,128)(2,1)S(1)} %collective-permute-done.2.n0), channel_id=1, source_target_pairs={{4,7},{5,4},{6,5},{7,6},{12,15},{13,12},{14,13},{15,14},{20,23},{2... | collective-permute-start | bytes 1572872 | tf_op jit(solution)/shard_map/ppermute | solution.py:29
  28.4 0.0 copy-start.2
  28.4 0.8 %copy-done.2 = bf16[2,256,512]{2,1,0:T(8,128)(2,1)} copy-done((bf16[2,256,512]{2,1,0:T(8,128)(2,1)}, bf16[2,256,512]{2,1,0:T(8,128)(2,1)S(1)}, u32[]{:S(2)}) %copy-start.2) | copy-done | bytes 524312
  29.2 0.0 collective-permute-done.3.n1
  29.2 0.0 copy-start.4
  29.2 0.8 %copy-done.4 = bf16[2,256,512]{2,1,0:T(8,128)(2,1)} copy-done((bf16[2,256,512]{2,1,0:T(8,128)(2,1)}, bf16[2,256,512]{2,1,0:T(8,128)(2,1)S(1)}, u32[]{:S(2)}) %copy-start.4) | copy-done | bytes 524312
  30.0 5.3 %collective-permute-start.5 = (bf16[2,256,512]{2,1,0:T(8,128)(2,1)S(1)}, bf16[2,256,512]{2,1,0:T(8,128)(2,1)}, u32[]{:S(2)}, u32[]{:S(2)}) collective-permute-start(bf16[2,256,512]{2,1,0:T(8,128)(2,1)S(1)} %collective-permute-done.1.b2), channel_id=1, source_target_pairs={{4,0},{12,8},{20,16},{28,24},{36,32},{44,40},{52,48},{60,56},{68,6... | collective-permute-start | bytes 1572872 | tf_op jit(solution)/shard_map/ppermute | solution.py:34
  35.3 0.0 collective-permute-done.8.b3.left
  35.3 6.7 %collective-permute-start.10 = (bf16[2,256,512]{2,1,0:T(8,128)(2,1)S(1)}, bf16[2,256,512]{2,1,0:T(8,128)(2,1)}, u32[]{:S(2)}, u32[]{:S(2)}) collective-permute-start(bf16[2,256,512]{2,1,0:T(8,128)(2,1)S(1)} %collective-permute-done.8.b3.left), channel_id=1, source_target_pairs={{4,0},{12,8},{20,16},{28,24},{36,32},{44,40},{52,48},{60,56},{68,6... | collective-permute-start | bytes 1572872 | tf_op jit(solution)/shard_map/ppermute | solution.py:34
  42.1 0.0 collective-permute-done.4.n2x
  42.1 4.6 %collective-permute-start.9 = (bf16[2,256,512]{2,1,0:T(8,128)(2,1)S(1)}, bf16[2,256,512]{2,1,0:T(8,128)(2,1)}, u32[]{:S(2)}, u32[]{:S(2)}) collective-permute-start(bf16[2,256,512]{2,1,0:T(8,128)(2,1)S(1)} %collective-permute-done.4.n2x), channel_id=1, source_target_pairs={{4,7},{5,4},{6,5},{7,6},{12,15},{13,12},{14,13},{15,14},{20,23},{2... | collective-permute-start | bytes 1572872 | tf_op jit(solution)/shard_map/ppermute | solution.py:29
  46.7 0.8 %dynamic-slice_bitcast_fusion = f32[128,1]{0,1:T(1,128)S(1)} fusion(f32[512]{0:T(512)} %param.12, s32[]{:T(128)S(6)} %select_n.3), kind=kLoop, calls=%fused_computation.2 | loop fusion | bytes 1028 | tf_op jit(solution)/shard_map/broadcast_in_dim | solution.py:247
  47.4 0.1 copy.8.mine
  47.5 0.1 pad_add_fusion.ids
  47.6 0.7 %convert_bitcast_fusion.fock = f32[4,8]{1,0:T(4,128)S(1)} fusion(bf16[8,4]{0,1:T(4,128)(2,1)} %param.11), kind=kLoop, calls=%fused_computation | loop fusion | flops 32 | bytes 192 | tf_op jit(solution)/shard_map/convert_element_type | solution.py:248
  48.3 1.0 %copy-done.1 = bf16[2,256,512]{2,1,0:T(8,128)(2,1)S(1)} copy-done((bf16[2,256,512]{2,1,0:T(8,128)(2,1)S(1)}, bf16[2,256,512]{2,1,0:T(8,128)(2,1)}, u32[]{:S(2)}) %copy-start.1) | copy-done | bytes 524312
  49.3 1.0 %copy-done.3 = bf16[2,256,512]{2,1,0:T(8,128)(2,1)S(1)} copy-done((bf16[2,256,512]{2,1,0:T(8,128)(2,1)S(1)}, bf16[2,256,512]{2,1,0:T(8,128)(2,1)}, u32[]{:S(2)}) %copy-start.3) | copy-done | bytes 524312
  50.4 1.3 %shard_map.73.acc.own_acc = f32[2,4,128,512]{3,2,1,0:T(8,128)S(1)} custom-call(s32[2]{0:T(128)S(1)} %pad_add_fusion.ids, bf16[2,256,512]{2,1,0:T(8,128)(2,1)S(1)} %copy-done.1, bf16[2,256,512]{2,1,0:T(8,128)(2,1)S(1)} %collective-permute-done.b1, bf16[2,256,512]{2,1,0:T(8,128)(2,1)S(1)} %collective-permute-done.1.b2, bf16[2,256,512]{2,1,0:T(8,128)(2,1)S(1)} %copy-done.3), custom_call_target="tpu_custom_call" | custom-call | flops 100000000 | bytes 4194304 | tf_op jit(solution)/shard_map/pallas_call | solution.py:144
  51.7 0.0 copy-start
  51.7 0.0 copy-start.6
  51.7 0.0 copy-start.7
  51.7 0.0 copy-start.8
  51.7 0.0 copy-start.9
  51.7 0.0 collective-permute-done.5.n2c
  51.8 0.0 copy-done.5
  51.8 1.6 %shard_map.74.next_acc = f32[2,2,128,512]{3,2,1,0:T(8,128)S(1)} custom-call(s32[2]{0:T(128)S(1)} %pad_add_fusion.ids, f32[2,4,128,512]{3,2,1,0:T(8,128)S(1)} %shard_map.73.acc.own_acc, bf16[2,256,512]{2,1,0:T(8,128)(2,1)S(1)} %collective-permute-done.b1, bf16[2,256,512]{2,1,0:T(8,128)(2,1)S(1)} %collective-permute-done.1.b2, ...), custom_call_target="tpu_custom_call" | custom-call | flops 100000000 | bytes 4194304 | tf_op jit(solution)/shard_map/pallas_call | solution.py:151
  53.4 0.0 collective-permute-done.6.prev
  53.4 0.0 collective-permute-done.7.nxt
  53.4 0.0 copy-done
  53.4 0.0 copy-done.6
  53.4 0.0 copy-done.7
  53.4 0.0 copy-done.8
  53.4 0.0 copy-done.9
  53.4 3.1 %shard_map.75 = (f32[8,128,512]{2,1,0:T(8,128)S(1)}, f32[8,128,512]{2,1,0:T(8,128)S(1)}) custom-call(s32[2]{0:T(128)S(1)} %pad_add_fusion.ids, s32[2,8]{1,0:T(2,128)S(1)} %bitcast.9, s32[4,8]{1,0:T(4,128)S(1)} %bitcast.12, f32[4,8]{1,0:T(4,128)S(1)} %convert_bitcast_fusion.fock, f32[128]{0:T(128)S(1)} %copy-done.9, f32[128,1]{1,0:T(8,128)S(1)} %copy.8.mine, ...), custom_call_target="tpu_custom_call" | custom-call | flops 100000000 | bytes 4194304 | tf_op jit(solution)/shard_map/pallas_call | solution.py:96
  56.6 1.4 %shard_map.76.part = f32[8,128,512]{2,1,0:T(8,128)S(1)} custom-call(s32[2]{0:T(128)S(1)} %pad_add_fusion.ids, s32[2,8]{1,0:T(2,128)S(1)} %bitcast.10, f32[2,4,128,512]{3,2,1,0:T(8,128)S(1)} %shard_map.73.acc.own_acc, f32[2,2,128,512]{3,2,1,0:T(8,128)S(1)} %shard_map.74.next_acc, f32[8,128,512]{2,1,0:T(8,128)S(1)} %get-tuple-element.7.pre, ...), custom_call_target="tpu_custom_call" | custom-call | flops 100000000 | bytes 4194304 | tf_op jit(solution)/shard_map/pallas_call | solution.py:183
  58.0 0.0 collective-permute-done.10.n3c
  58.0 0.0 collective-permute-done.9.n3x
  58.0 2.6 %shard_map.77 = bf16[8,128,512]{2,1,0:T(8,128)(2,1)} custom-call(s32[2]{0:T(128)S(1)} %pad_add_fusion.ids, s32[2,8]{1,0:T(2,128)S(1)} %bitcast.11, f32[8,128,512]{2,1,0:T(8,128)S(1)} %shard_map.76.part, f32[8,128,512]{2,1,0:T(8,128)S(1)} %get-tuple-element.8.wgt, bf16[2,256,512]{2,1,0:T(8,128)(2,1)S(1)} %collective-permute-done.8.b3.left, ...), custom_call_target="tpu_custom_call" | custom-call | flops 100000000 | bytes 4194304 | tf_op jit(solution)/shard_map/pallas_call | solution.py:221
  (3 shorter events, 0.0 us)
Async XLA Ops:
  0.0 13.0 %collective-permute-start = (bf16[2,256,512]{2,1,0:T(8,128)(2,1)}, bf16[2,256,512]{2,1,0:T(8,128)(2,1)S(1)}, u32[]{:S(2)}, u32[]{:S(2)}) collective-permute-start(bf16[2,256,512]{2,1,0:T(8,128)(2,1)} %b0.1), channel_id=1, source_target_pairs={{0,1},{1,2},{2,3},{3,0},{4,5},{5,6},{6,7},{7,4},{8,9},{9,10},{10,1... | collective-permute-start | bytes 1572872 | tf_op jit(solution)/shard_map/ppermute | solution.py:23
  1.2 23.7 %collective-permute-start.1 = (bf16[2,256,512]{2,1,0:T(8,128)(2,1)}, bf16[2,256,512]{2,1,0:T(8,128)(2,1)S(1)}, u32[]{:S(2)}, u32[]{:S(2)}) collective-permute-start(bf16[2,256,512]{2,1,0:T(8,128)(2,1)} %b0.1), channel_id=1, source_target_pairs={{0,3},{1,0},{2,1},{3,2},{4,7},{5,4},{6,5},{7,6},{8,11},{9,8},{10,9... | collective-permute-start | bytes 1572872 | tf_op jit(solution)/shard_map/ppermute | solution.py:23
  1.5 24.8 %collective-permute-start.2 = (bf16[2,256,512]{2,1,0:T(8,128)(2,1)}, bf16[2,256,512]{2,1,0:T(8,128)(2,1)S(1)}, u32[]{:S(2)}, u32[]{:S(2)}) collective-permute-start(bf16[2,256,512]{2,1,0:T(8,128)(2,1)} %b0.1), channel_id=1, source_target_pairs={{4,0},{8,4},{12,8},{16,12},{20,16},{24,20},{28,24},{32,28},{36,32}... | collective-permute-start | bytes 1572872 | tf_op jit(solution)/shard_map/ppermute | solution.py:18
  13.0 16.2 %collective-permute-start.3 = (bf16[2,256,512]{2,1,0:T(8,128)(2,1)S(1)}, bf16[2,256,512]{2,1,0:T(8,128)(2,1)S(1)}, u32[]{:S(2)}, u32[]{:S(2)}) collective-permute-start(bf16[2,256,512]{2,1,0:T(8,128)(2,1)S(1)} %collective-permute-done.b1), channel_id=1, source_target_pairs={{4,0},{8,4},{12,8},{16,12},{20,16},{24,20},{28,24},{32,28},{36,32}... | collective-permute-start | bytes 1572872 | tf_op jit(solution)/shard_map/ppermute | solution.py:18
  16.5 36.9 %collective-permute-start.6 = (bf16[8,128,512]{2,1,0:T(8,128)(2,1)}, bf16[8,128,512]{2,1,0:T(8,128)(2,1)S(1)}, u32[]{:S(2)}, u32[]{:S(2)}) collective-permute-start(bf16[8,128,512]{2,1,0:T(8,128)(2,1)} %own.1), channel_id=1, source_target_pairs={{0,4},{4,8},{8,12},{12,16},{16,20},{20,24},{24,28},{28,32},{32,36}... | collective-permute-start | bytes 3145736 | tf_op jit(solution)/shard_map/ppermute | solution.py:18
  19.9 33.5 %collective-permute-start.7 = (bf16[8,128,512]{2,1,0:T(8,128)(2,1)}, bf16[8,128,512]{2,1,0:T(8,128)(2,1)}, u32[]{:S(2)}, u32[]{:S(2)}) collective-permute-start(bf16[8,128,512]{2,1,0:T(8,128)(2,1)} %own.1), channel_id=1, source_target_pairs={{4,0},{8,4},{12,8},{16,12},{20,16},{24,20},{28,24},{32,28},{36,32}... | collective-permute-start | bytes 3145736 | tf_op jit(solution)/shard_map/ppermute | solution.py:18
  24.9 10.4 %collective-permute-start.8 = (bf16[2,256,512]{2,1,0:T(8,128)(2,1)S(1)}, bf16[2,256,512]{2,1,0:T(8,128)(2,1)S(1)}, u32[]{:S(2)}, u32[]{:S(2)}) collective-permute-start(bf16[2,256,512]{2,1,0:T(8,128)(2,1)S(1)} %collective-permute-done.b1), channel_id=1, source_target_pairs={{0,1},{1,2},{2,3},{3,0},{4,5},{5,6},{6,7},{7,4},{8,9},{9,10},{10,1... | collective-permute-start | bytes 1572872 | tf_op jit(solution)/shard_map/ppermute | solution.py:23
  26.2 15.9 %collective-permute-start.4 = (bf16[2,256,512]{2,1,0:T(8,128)(2,1)S(1)}, bf16[2,256,512]{2,1,0:T(8,128)(2,1)S(1)}, u32[]{:S(2)}, u32[]{:S(2)}) collective-permute-start(bf16[2,256,512]{2,1,0:T(8,128)(2,1)S(1)} %collective-permute-done.2.n0), channel_id=1, source_target_pairs={{4,7},{5,4},{6,5},{7,6},{12,15},{13,12},{14,13},{15,14},{20,23},{2... | collective-permute-start | bytes 1572872 | tf_op jit(solution)/shard_map/ppermute | solution.py:29
  28.4 0.8 %copy-start.2 = (bf16[2,256,512]{2,1,0:T(8,128)(2,1)}, bf16[2,256,512]{2,1,0:T(8,128)(2,1)S(1)}, u32[]{:S(2)}) copy-start(bf16[2,256,512]{2,1,0:T(8,128)(2,1)S(1)} %collective-permute-done.2.n0) | copy-start | bytes 1572868
  29.2 0.8 %copy-start.4 = (bf16[2,256,512]{2,1,0:T(8,128)(2,1)}, bf16[2,256,512]{2,1,0:T(8,128)(2,1)S(1)}, u32[]{:S(2)}) copy-start(bf16[2,256,512]{2,1,0:T(8,128)(2,1)S(1)} %collective-permute-done.3.n1) | copy-start | bytes 1572868
  30.0 21.7 %collective-permute-start.5 = (bf16[2,256,512]{2,1,0:T(8,128)(2,1)S(1)}, bf16[2,256,512]{2,1,0:T(8,128)(2,1)}, u32[]{:S(2)}, u32[]{:S(2)}) collective-permute-start(bf16[2,256,512]{2,1,0:T(8,128)(2,1)S(1)} %collective-permute-done.1.b2), channel_id=1, source_target_pairs={{4,0},{12,8},{20,16},{28,24},{36,32},{44,40},{52,48},{60,56},{68,6... | collective-permute-start | bytes 1572872 | tf_op jit(solution)/shard_map/ppermute | solution.py:34
  35.3 22.6 %collective-permute-start.10 = (bf16[2,256,512]{2,1,0:T(8,128)(2,1)S(1)}, bf16[2,256,512]{2,1,0:T(8,128)(2,1)}, u32[]{:S(2)}, u32[]{:S(2)}) collective-permute-start(bf16[2,256,512]{2,1,0:T(8,128)(2,1)S(1)} %collective-permute-done.8.b3.left), channel_id=1, source_target_pairs={{4,0},{12,8},{20,16},{28,24},{36,32},{44,40},{52,48},{60,56},{68,6... | collective-permute-start | bytes 1572872 | tf_op jit(solution)/shard_map/ppermute | solution.py:34
  42.1 15.9 %collective-permute-start.9 = (bf16[2,256,512]{2,1,0:T(8,128)(2,1)S(1)}, bf16[2,256,512]{2,1,0:T(8,128)(2,1)}, u32[]{:S(2)}, u32[]{:S(2)}) collective-permute-start(bf16[2,256,512]{2,1,0:T(8,128)(2,1)S(1)} %collective-permute-done.4.n2x), channel_id=1, source_target_pairs={{4,7},{5,4},{6,5},{7,6},{12,15},{13,12},{14,13},{15,14},{20,23},{2... | collective-permute-start | bytes 1572872 | tf_op jit(solution)/shard_map/ppermute | solution.py:29
  48.3 1.0 %copy-start.1 = (bf16[2,256,512]{2,1,0:T(8,128)(2,1)S(1)}, bf16[2,256,512]{2,1,0:T(8,128)(2,1)}, u32[]{:S(2)}) copy-start(bf16[2,256,512]{2,1,0:T(8,128)(2,1)} %b0.1) | copy-start | bytes 1572868
  49.3 1.0 %copy-start.3 = (bf16[2,256,512]{2,1,0:T(8,128)(2,1)S(1)}, bf16[2,256,512]{2,1,0:T(8,128)(2,1)}, u32[]{:S(2)}) copy-start(bf16[2,256,512]{2,1,0:T(8,128)(2,1)} %copy-done.2) | copy-start | bytes 1572868
  50.4 1.4 %copy-start.5 = (bf16[2,256,512]{2,1,0:T(8,128)(2,1)S(1)}, bf16[2,256,512]{2,1,0:T(8,128)(2,1)}, u32[]{:S(2)}) copy-start(bf16[2,256,512]{2,1,0:T(8,128)(2,1)} %copy-done.4) | copy-start | bytes 1572868
  51.7 1.7 %copy-start = (bf16[8,128,512]{2,1,0:T(8,128)(2,1)S(1)}, bf16[8,128,512]{2,1,0:T(8,128)(2,1)}, u32[]{:S(2)}) copy-start(bf16[8,128,512]{2,1,0:T(8,128)(2,1)} %own.1) | copy-start | bytes 3145732
  51.7 1.7 %copy-start.6 = (s32[8,2]{0,1:T(2,128)S(1)}, s32[8,2]{0,1:T(2,128)}, u32[]{:S(2)}) copy-start(s32[8,2]{0,1:T(2,128)} %param.9) | copy-start | bytes 196
  51.7 1.7 %copy-start.7 = (s32[8,4]{0,1:T(4,128)S(1)}, s32[8,4]{0,1:T(4,128)}, u32[]{:S(2)}) copy-start(s32[8,4]{0,1:T(4,128)} %param.10) | copy-start | bytes 388
  51.7 1.7 %copy-start.8 = (f32[512]{0:T(512)S(1)}, f32[512]{0:T(512)}, u32[]{:S(2)}) copy-start(f32[512]{0:T(512)} %param.12) | copy-start | bytes 6148
  51.7 1.7 %copy-start.9 = (f32[128]{0:T(128)S(1)}, f32[128]{0:T(128)}, u32[]{:S(2)}) copy-start(f32[128]{0:T(128)} %occ.1) | copy-start | bytes 1540

commit v5 on v4

v5 whole, which is shorter than its diff:
```python
import jax
import jax.numpy as jnp
from jax import lax
from jax.experimental import pallas as pl
from jax.experimental.pallas import tpu as pltpu
from jax.sharding import PartitionSpec as P

damping = 0.7


SMEM = pl.BlockSpec(memory_space=pltpu.SMEM)
VMEM = pl.BlockSpec(memory_space=pltpu.VMEM)
ANY = pl.BlockSpec(memory_space=pl.ANY)


def along_orb(x, distance):
    n = lax.axis_size("orb")
    return lax.ppermute(x, "orb", [(i - distance, i) for i in range(n) if 0 <= i - distance < n])


def along_rep(x, distance):
    n = lax.axis_size("rep")
    return lax.ppermute(x, "rep", [(i, (i + distance) % n) for i in range(n)])


def along_rep_odd(x, distance):
    n, m = lax.axis_size("orb"), lax.axis_size("rep")
    route = [(o * m + i, o * m + (i + distance) % m) for o in range(1, n, 2) for i in range(m)]
    return lax.ppermute(x, ("orb", "rep"), route)


def odd_to_even(x):
    n = lax.axis_size("orb")
    return lax.ppermute(x, "orb", [(o, o - 1) for o in range(1, n, 2)])


def call(body, out_shape, in_specs, scratch=(), out_specs=None, limit=16):
    return pl.pallas_call(
        body,
        out_shape=out_shape,
        in_specs=in_specs,
        out_specs=out_specs or jax.tree.map(lambda _: VMEM, out_shape),
        scratch_shapes=list(scratch),
        compiler_params=pltpu.CompilerParams(vmem_limit_bytes=limit * 2**20),
        cost_estimate=pl.CostEstimate(flops=10**8, bytes_accessed=4 * 2**20, transcendentals=0),
    )


def dot_t(a, b):
    return lax.dot_general(a, b, (((0,), (0,)), ((), ())), preferred_element_type=jnp.float32)


def left_of(rep, blocks, rows):
    start = pl.multiple_of(rep[0] * rows, rows)
    return jnp.concatenate(
        [
            jnp.concatenate([b[i, :, pl.ds(start, rows)] for i in range(b.shape[0])], axis=1)
            for b in blocks
        ],
        axis=0,
    )


def products(rep, left, right, out, offset=0, base=None):
    orbitals, _, rows, _ = out.shape
    lhs = left_of(rep, left, rows)
    for j in range(left[0].shape[0]):
        both = dot_t(lhs, jnp.concatenate([r(j) for r in right], axis=0))
        for i in range(orbitals):
            part = both[i * rows:(i + 1) * rows]
            out[i, offset + j] = part if base is None else base[i, offset + j] + part


def acc_shape(block, columns=1):
    orbitals, _, width = block.shape
    rows = width // lax.axis_size("rep")
    return jax.ShapeDtypeStruct((orbitals, columns * orbitals, rows, width), jnp.float32)


def whole(ref):
    return lambda j: ref[j]


def either(orb, odd_ref, even_ref):
    odd = lax.rem(orb[0], 2) == 1
    return lambda j: jnp.where(odd, odd_ref[j], even_ref[j])


def own_part(rep, b0, b1, b2, n0):
    def body(rep, b0, b1, b2, n0, out):
        products(rep, (b0, b1, b2), [whole(b) for b in (b0, b1, b2)], out)
        products(rep, (b0,), [whole(n0)], out, b0.shape[0])

    return call(body, acc_shape(b0, 2), [SMEM] + [VMEM] * 4)(rep, b0, b1, b2, n0)


def pair_slot(orb, ints, p, orbitals):
    base = orb[0] * orbitals
    return ints[0, p] - base, ints[1, p] - base


def middle_kernel(
    orb, rep, ints, fock, occ, energies, base, b1, b2, b3, n1, n2x, n2c, prev, own, nxt,
    part, wgt, acc, amps, sems,
):
    pair_count, rows, width = part.shape
    orbitals = b1.shape[0]
    copies = [
        pltpu.make_async_copy(src, amps.at[pl.ds(k * pair_count, pair_count)], sems.at[k])
        for k, src in enumerate((prev, own, nxt))
    ]
    for c in copies:
        c.start()
    first = energies.shape[1] - width
    mine = energies[:, pl.ds(pl.multiple_of(first + rep[0] * rows, rows), rows)]
    tile = jnp.transpose(jnp.broadcast_to(mine, (rows, rows)))

    def denominators(p, carry):
        shift = occ[0, ints[0, p]] + occ[0, ints[1, p]]
        for c in range(0, width, rows):
            row = energies[:, first + c:first + c + rows]
            wgt[p, :, c:c + rows] = damping / (tile + (row - shift))
        return carry

    lax.fori_loop(0, pair_count, denominators, 0)
    products(rep, (b3,), [whole(b3)], acc, 0, base)
    products(rep, (b1, b2), [whole(n1), either(orb, n2x, n2c)], acc, orbitals, base)
    for c in copies:
        c.wait()
    before = (orb[0] - 1) * pair_count
    step = 32

    def pair(p, carry):
        i, j = pair_slot(orb, ints, p, orbitals)
        slots = [ints[2 + c, p] - before for c in range(fock.shape[0])]
        scales = [fock[c, p] for c in range(fock.shape[0])]
        for r in range(0, rows, step):
            rs = pl.ds(r, step)
            total = -acc[i, j, rs, :]
            for s, f in zip(slots, scales):
                total = total + f * amps[s, rs, :].astype(jnp.float32)
            mine = amps[p + pair_count, rs, :].astype(jnp.float32)
            part[p, rs, :] = (1.0 - damping) * mine + wgt[p, rs, :] * total
        return carry

    lax.fori_loop(0, pair_count, pair, 0)


def middle(*args):
    base, own = args[6], args[-2]
    shape = jax.ShapeDtypeStruct(own.shape, jnp.float32)
    scratch = (
        pltpu.VMEM(base.shape, jnp.float32),
        pltpu.VMEM((3 * own.shape[0],) + own.shape[1:], own.dtype),
        pltpu.SemaphoreType.DMA((3,)),
    )
    specs = [SMEM] * 5 + [VMEM] * 8 + [ANY] * 3
    return call(middle_kernel, (shape, shape), specs, scratch)(*args)


def last_update(orb, rep, ints, part, wgt, b3, n3x, n3c):
    def body(orb, rep, ints, part, wgt, b3, n3x, n3c, out, acc, done, sem):
        orbitals = acc.shape[0]
        products(rep, (b3,), [either(orb, n3x, n3c)], acc)

        def pair(p, carry):
            i, j = pair_slot(orb, ints, p, orbitals)

            @pl.when(j >= orbitals)
            def _():
                done[p] = (part[p] - wgt[p] * acc[i, j - orbitals]).astype(done.dtype)

            @pl.when(j < orbitals)
            def _():
                done[p] = part[p].astype(done.dtype)

            pltpu.make_async_copy(done.at[p], out.at[p], sem.at[p]).start()
            return carry

        def wait(p, carry):
            pltpu.make_async_copy(done.at[p], out.at[p], sem.at[p]).wait()
            return carry

        lax.fori_loop(0, done.shape[0], pair, 0)
        lax.fori_loop(0, done.shape[0], wait, 0)

    acc = acc_shape(b3)
    scratch = [
        pltpu.VMEM(acc.shape, acc.dtype),
        pltpu.VMEM(part.shape, jnp.bfloat16),
        pltpu.SemaphoreType.DMA((part.shape[0],)),
    ]
    return call(
        body, jax.ShapeDtypeStruct(part.shape, jnp.bfloat16),
        [SMEM] * 3 + [VMEM] * 5, scratch, out_specs=ANY,
    )(orb, rep, ints, part, wgt, b3, n3x, n3c)


def device_step(
    blocks, amplitudes, pair_orbitals, coupling, fock_coupling, virtual_energy, occupied_energy
):
    orb = lax.axis_index("orb").astype(jnp.int32).reshape(1)
    rep = lax.axis_index("rep").astype(jnp.int32).reshape(1)
    b0 = blocks
    n0 = along_orb(b0, -1)
    b1 = along_rep(b0, 1)
    b2 = along_rep(b0, -1)
    amps_next = along_orb(amplitudes, -1)
    amps_prev = along_orb(amplitudes, 1)
    n2x = along_rep_odd(n0, -1)
    b3 = along_rep(b1, 1)
    n1 = along_orb(b1, -1)
    n2c = odd_to_even(b2)
    n3x = along_rep_odd(n2x, -1)
    n3c = odd_to_even(b3)
    fock = fock_coupling.T.astype(jnp.float32)
    ints = jnp.concatenate([pair_orbitals.T, coupling.T], axis=0)
    energies = jnp.concatenate([occupied_energy[None, :], virtual_energy[None, :]], axis=1)
    base = own_part(rep, b0, b1, b2, n0)
    part, wgt = middle(
        orb, rep, ints, fock, energies, energies, base, b1, b2, b3, n1, n2x, n2c,
        amps_prev, amplitudes, amps_next,
    )
    return last_update(orb, rep, ints, part, wgt, b3, n3x, n3c)


def solution(mesh):
    placed = (
        P("orb", "rep", None),
        P("orb", "rep", None),
        P("orb", None),
        P("orb", None),
        P("orb", None),
        P(),
        P(),
    )
    return jax.shard_map(
        device_step, mesh=mesh, in_specs=placed, out_specs=P("orb", "rep", None), check_vma=False
    )
```

time: 61.1 us -> 62.9 us (1.029)
  the two profiles are of different devices: /device:TPU:27 before, /device:TPU:97 now
where the time goes in v5:
time: 62.9 us; the launch traced here: 62.4 us
  starting transfers between devices  30.7 us (49%)
  waiting for transfers between devices  19.8 us (31%)
  Pallas kernels  7.27 us (12%)
  local copies, waits for them, and re-layouts  2.42 us (4%)
  other arithmetic  2.07 us (3%)
    ppermute x4, starting transfers between devices, along_orb(): lax.ppermute(x, 'orb', [(i - distance, i) for i in range(n) if 0 <= i - d...  13.4 us
    ppermute x4, waiting for transfers between devices, along_orb(): lax.ppermute(x, 'orb', [(i - distance, i) for i in range(n) if 0 <= i - d...  11.4 us
    ppermute x2, starting transfers between devices, along_rep_odd(): return lax.ppermute(x, ('orb', 'rep'), route)  9.16 us
    ppermute x3, waiting for transfers between devices, along_rep(): return lax.ppermute(x, 'rep', [(i, (i + distance) % n) for i in range(n)])  8.42 us
    ppermute x2, starting transfers between devices, odd_to_even(): return lax.ppermute(x, 'orb', [(o, o - 1) for o in range(1, n, 2)])  5.42 us
    pallas_call x1, Pallas kernels, middle(): return call(middle_kernel, (shape, shape), specs, scratch)(*args)  3.88 us
    ppermute x3, starting transfers between devices, along_rep(): return lax.ppermute(x, 'rep', [(i, (i + distance) % n) for i in range(n)])  2.68 us
    pallas_call x1, Pallas kernels, last_update(): call(body, jax.ShapeDtypeStruct(part.shape, jnp.bfloat16), [SMEM] * 3 + [...  2.66 us
  transfers between devices with their start and end apart: 11, of which 2 were waited for; matrix products, arithmetic and copies ran while one was open for 3% of the time, Pallas kernels for 7%

profile of v5, /device:TPU:97, one launch (start us, length us, event | category | flops | bytes accessed | tf_op | source)
XLA Modules:
  0.0 62.4 jit_solution(6285576105697034568)
XLA Ops:
  0.0 1.2 %collective-permute-start = (bf16[2,256,512]{2,1,0:T(8,128)(2,1)}, bf16[2,256,512]{2,1,0:T(8,128)(2,1)S(1)}, u32[]{:S(2)}, u32[]{:S(2)}) collective-permute-start(bf16[2,256,512]{2,1,0:T(8,128)(2,1)} %b0.1), channel_id=1, source_target_pairs={{0,1},{1,2},{2,3},{3,0},{4,5},{5,6},{6,7},{7,4},{8,9},{9,10},{10,1... | collective-permute-start | bytes 1572872 | tf_op jit(solution)/shard_map/ppermute | solution.py:23
  1.2 1.5 %collective-permute-start.1 = (bf16[2,256,512]{2,1,0:T(8,128)(2,1)}, bf16[2,256,512]{2,1,0:T(8,128)(2,1)S(1)}, u32[]{:S(2)}, u32[]{:S(2)}) collective-permute-start(bf16[2,256,512]{2,1,0:T(8,128)(2,1)} %b0.1), channel_id=1, source_target_pairs={{0,3},{1,0},{2,1},{3,2},{4,7},{5,4},{6,5},{7,6},{8,11},{9,8},{10,9... | collective-permute-start | bytes 1572872 | tf_op jit(solution)/shard_map/ppermute | solution.py:23
  2.7 3.1 %collective-permute-start.2 = (bf16[2,256,512]{2,1,0:T(8,128)(2,1)}, bf16[2,256,512]{2,1,0:T(8,128)(2,1)S(1)}, u32[]{:S(2)}, u32[]{:S(2)}) collective-permute-start(bf16[2,256,512]{2,1,0:T(8,128)(2,1)} %b0.1), channel_id=1, source_target_pairs={{4,0},{8,4},{12,8},{16,12},{20,16},{24,20},{28,24},{32,28},{36,32}... | collective-permute-start | bytes 1572872 | tf_op jit(solution)/shard_map/ppermute | solution.py:18
  5.8 8.4 %collective-permute-done.b1 = bf16[2,256,512]{2,1,0:T(8,128)(2,1)S(1)} collective-permute-done((bf16[2,256,512]{2,1,0:T(8,128)(2,1)}, bf16[2,256,512]{2,1,0:T(8,128)(2,1)S(1)}, u32[]{:S(2)}, u32[]{:S(2)}) %collective-permute-start) | collective-permute-done | bytes 524320 | tf_op jit(solution)/shard_map/ppermute | solution.py:23
  14.2 0.0 collective-permute-start.3
  14.2 6.4 %collective-permute-start.7 = (bf16[8,128,512]{2,1,0:T(8,128)(2,1)}, bf16[8,128,512]{2,1,0:T(8,128)(2,1)S(1)}, u32[]{:S(2)}, u32[]{:S(2)}) collective-permute-start(bf16[8,128,512]{2,1,0:T(8,128)(2,1)} %own.1), channel_id=1, source_target_pairs={{0,4},{4,8},{8,12},{12,16},{16,20},{20,24},{24,28},{28,32},{32,36}... | collective-permute-start | bytes 3145736 | tf_op jit(solution)/shard_map/ppermute | solution.py:18
  20.7 1.9 %collective-permute-start.8 = (bf16[8,128,512]{2,1,0:T(8,128)(2,1)}, bf16[8,128,512]{2,1,0:T(8,128)(2,1)}, u32[]{:S(2)}, u32[]{:S(2)}) collective-permute-start(bf16[8,128,512]{2,1,0:T(8,128)(2,1)} %own.1), channel_id=1, source_target_pairs={{4,0},{8,4},{12,8},{16,12},{20,16},{24,20},{28,24},{32,28},{36,32}... | collective-permute-start | bytes 3145736 | tf_op jit(solution)/shard_map/ppermute | solution.py:18
  22.6 0.0 collective-permute-done.1.b2
  22.6 1.9 %collective-permute-start.4 = (bf16[2,256,512]{2,1,0:T(8,128)(2,1)S(1)}, bf16[2,256,512]{2,1,0:T(8,128)(2,1)S(1)}, u32[]{:S(2)}, u32[]{:S(2)}) collective-permute-start(bf16[2,256,512]{2,1,0:T(8,128)(2,1)S(1)} %collective-permute-done.b1), channel_id=1, source_target_pairs={{4,0},{8,4},{12,8},{16,12},{20,16},{24,20},{28,24},{32,28},{36,32}... | collective-permute-start | bytes 1572872 | tf_op jit(solution)/shard_map/ppermute | solution.py:18
  24.6 0.0 collective-permute-done.2.n0
  24.6 4.6 %collective-permute-start.5 = (bf16[2,256,512]{2,1,0:T(8,128)(2,1)S(1)}, bf16[2,256,512]{2,1,0:T(8,128)(2,1)}, u32[]{:S(2)}, u32[]{:S(2)}) collective-permute-start(bf16[2,256,512]{2,1,0:T(8,128)(2,1)S(1)} %collective-permute-done.2.n0), channel_id=1, source_target_pairs={{4,7},{5,4},{6,5},{7,6},{12,15},{13,12},{14,13},{15,14},{20,23},{2... | collective-permute-start | bytes 1572872 | tf_op jit(solution)/shard_map/ppermute | solution.py:29
  29.2 0.0 collective-permute-done.3.b3
  29.2 3.3 %collective-permute-start.6 = (bf16[2,256,512]{2,1,0:T(8,128)(2,1)S(1)}, bf16[2,256,512]{2,1,0:T(8,128)(2,1)}, u32[]{:S(2)}, u32[]{:S(2)}) collective-permute-start(bf16[2,256,512]{2,1,0:T(8,128)(2,1)S(1)} %collective-permute-done.1.b2), channel_id=1, source_target_pairs={{4,0},{12,8},{20,16},{28,24},{36,32},{44,40},{52,48},{60,56},{68,6... | collective-permute-start | bytes 1572872 | tf_op jit(solution)/shard_map/ppermute | solution.py:34
  32.5 11.3 %collective-permute-done.4.n1 = bf16[2,256,512]{2,1,0:T(8,128)(2,1)S(1)} collective-permute-done((bf16[2,256,512]{2,1,0:T(8,128)(2,1)S(1)}, bf16[2,256,512]{2,1,0:T(8,128)(2,1)S(1)}, u32[]{:S(2)}, u32[]{:S(2)}) %collective-permute-start.4) | collective-permute-done | bytes 524320 | tf_op jit(solution)/shard_map/ppermute | solution.py:18
  43.8 0.0 copy-start.2
  43.8 0.8 %copy-done.2 = bf16[2,256,512]{2,1,0:T(8,128)(2,1)} copy-done((bf16[2,256,512]{2,1,0:T(8,128)(2,1)}, bf16[2,256,512]{2,1,0:T(8,128)(2,1)S(1)}, u32[]{:S(2)}) %copy-start.2) | copy-done | bytes 524312
  44.6 2.1 %collective-permute-start.10 = (bf16[2,256,512]{2,1,0:T(8,128)(2,1)S(1)}, bf16[2,256,512]{2,1,0:T(8,128)(2,1)}, u32[]{:S(2)}, u32[]{:S(2)}) collective-permute-start(bf16[2,256,512]{2,1,0:T(8,128)(2,1)S(1)} %collective-permute-done.3.b3), channel_id=1, source_target_pairs={{4,0},{12,8},{20,16},{28,24},{36,32},{44,40},{52,48},{60,56},{68,6... | collective-permute-start | bytes 1572872 | tf_op jit(solution)/shard_map/ppermute | solution.py:34
  46.7 0.0 collective-permute-done.5.n2x
  46.7 4.6 %collective-permute-start.9 = (bf16[2,256,512]{2,1,0:T(8,128)(2,1)}, bf16[2,256,512]{2,1,0:T(8,128)(2,1)}, u32[]{:S(2)}, u32[]{:S(2)}) collective-permute-start(bf16[2,256,512]{2,1,0:T(8,128)(2,1)} %collective-permute-done.5.n2x), channel_id=1, source_target_pairs={{4,7},{5,4},{6,5},{7,6},{12,15},{13,12},{14,13},{15,14},{20,23},{2... | collective-permute-start | bytes 1572872 | tf_op jit(solution)/shard_map/ppermute | solution.py:29
  51.3 0.7 %pad_maximum_fusion.occ.energies = f32[1,640]{1,0:T(1,128)S(1)} fusion(f32[1,512]{1,0:T(1,128)} %bitcast.9, f32[1,128]{1,0:T(1,128)} %bitcast.11), kind=kLoop, calls=%fused_computation.1 | loop fusion | flops 640 | bytes 5120 | tf_op jit(solution)/shard_map/concatenate | solution.py:218
  52.0 0.7 %pad_add_fusion.ints = s32[6,8]{1,0:T(8,128)S(1)} fusion(s32[4,8]{1,0:T(4,128)} %bitcast.8, s32[2,8]{1,0:T(2,128)} %bitcast.10), kind=kLoop, calls=%fused_computation | loop fusion | flops 48 | bytes 384 | tf_op jit(solution)/shard_map/concatenate | solution.py:217
  52.7 0.7 %convert_bitcast_fusion.fock = f32[4,8]{1,0:T(4,128)S(1)} fusion(bf16[8,4]{0,1:T(4,128)(2,1)} %param.11), kind=kLoop, calls=%fused_computation.2 | loop fusion | flops 32 | bytes 192 | tf_op jit(solution)/shard_map/convert_element_type | solution.py:216
  53.4 0.0 copy-start.1
  53.4 1.0 %copy-done.1 = bf16[2,256,512]{2,1,0:T(8,128)(2,1)S(1)} copy-done((bf16[2,256,512]{2,1,0:T(8,128)(2,1)S(1)}, bf16[2,256,512]{2,1,0:T(8,128)(2,1)}, u32[]{:S(2)}) %copy-start.1) | copy-done | bytes 524312
  54.4 0.0 copy-start
  54.4 0.0 copy-start.3
  54.4 0.7 %shard_map.73.base = f32[2,4,128,512]{3,2,1,0:T(8,128)S(1)} custom-call(s32[1]{0:T(128)} %bitcast.1.rep, bf16[2,256,512]{2,1,0:T(8,128)(2,1)S(1)} %copy-done.1, bf16[2,256,512]{2,1,0:T(8,128)(2,1)S(1)} %collective-permute-done.b1, bf16[2,256,512]{2,1,0:T(8,128)(2,1)S(1)} %collective-permute-done.1.b2, bf16[2,256,512]{2,1,0:T(8,128)(2,1)S(1)} %collective-permute-done.2.n0), custom_call_target="tpu_custom_call" | custom-call | flops 100000000 | bytes 4194304 | tf_op jit(solution)/shard_map/pallas_call | solution.py:94
  55.2 0.0 collective-permute-done.6.n2c
  55.2 0.0 collective-permute-done.7.prev
  55.2 0.0 collective-permute-done.8.nxt
  55.2 0.5 copy-done
  55.7 0.1 copy-done.3
  55.8 3.9 %shard_map.74 = (f32[8,128,512]{2,1,0:T(8,128)S(1)}, f32[8,128,512]{2,1,0:T(8,128)S(1)}) custom-call(s32[1]{0:T(128)} %bitcast.orb, s32[1]{0:T(128)} %bitcast.1.rep, s32[6,8]{1,0:T(8,128)S(1)} %pad_add_fusion.ints, f32[4,8]{1,0:T(4,128)S(1)} %convert_bitcast_fusion.fock, f32[1,640]{1,0:T(1,128)S(1)} %pad_maximum_fusion.occ.energies, ...), custom_call_target="tpu_custom_call" | custom-call | flops 100000000 | bytes 4194304 | tf_op jit(solution)/shard_map/pallas_call | solution.py:158
  59.7 0.0 collective-permute-done.10.n3c
  59.7 0.0 collective-permute-done.9.n3x
  59.7 2.7 %shard_map.75 = bf16[8,128,512]{2,1,0:T(8,128)(2,1)} custom-call(s32[1]{0:T(128)} %bitcast.orb, s32[1]{0:T(128)} %bitcast.1.rep, s32[6,8]{1,0:T(8,128)S(1)} %pad_add_fusion.ints, f32[8,128,512]{2,1,0:T(8,128)S(1)} %get-tuple-element.7.part, f32[8,128,512]{2,1,0:T(8,128)S(1)} %get-tuple-element.8.wgt, bf16[2,256,512]{2,1,0:T(8,128)(2,1)S(1)} %collective-permute-done.3.b3, ...), custom_call_target="tpu_custom_call" | custom-call | flops 100000000 | bytes 4194304 | tf_op jit(solution)/shard_map/pallas_call | solution.py:193
Async XLA Ops:
  0.0 14.2 %collective-permute-start = (bf16[2,256,512]{2,1,0:T(8,128)(2,1)}, bf16[2,256,512]{2,1,0:T(8,128)(2,1)S(1)}, u32[]{:S(2)}, u32[]{:S(2)}) collective-permute-start(bf16[2,256,512]{2,1,0:T(8,128)(2,1)} %b0.1), channel_id=1, source_target_pairs={{0,1},{1,2},{2,3},{3,0},{4,5},{5,6},{6,7},{7,4},{8,9},{9,10},{10,1... | collective-permute-start | bytes 1572872 | tf_op jit(solution)/shard_map/ppermute | solution.py:23
  1.2 21.4 %collective-permute-start.1 = (bf16[2,256,512]{2,1,0:T(8,128)(2,1)}, bf16[2,256,512]{2,1,0:T(8,128)(2,1)S(1)}, u32[]{:S(2)}, u32[]{:S(2)}) collective-permute-start(bf16[2,256,512]{2,1,0:T(8,128)(2,1)} %b0.1), channel_id=1, source_target_pairs={{0,3},{1,0},{2,1},{3,2},{4,7},{5,4},{6,5},{7,6},{8,11},{9,8},{10,9... | collective-permute-start | bytes 1572872 | tf_op jit(solution)/shard_map/ppermute | solution.py:23
  2.7 21.9 %collective-permute-start.2 = (bf16[2,256,512]{2,1,0:T(8,128)(2,1)}, bf16[2,256,512]{2,1,0:T(8,128)(2,1)S(1)}, u32[]{:S(2)}, u32[]{:S(2)}) collective-permute-start(bf16[2,256,512]{2,1,0:T(8,128)(2,1)} %b0.1), channel_id=1, source_target_pairs={{4,0},{8,4},{12,8},{16,12},{20,16},{24,20},{28,24},{32,28},{36,32}... | collective-permute-start | bytes 1572872 | tf_op jit(solution)/shard_map/ppermute | solution.py:18
  14.2 14.9 %collective-permute-start.3 = (bf16[2,256,512]{2,1,0:T(8,128)(2,1)S(1)}, bf16[2,256,512]{2,1,0:T(8,128)(2,1)S(1)}, u32[]{:S(2)}, u32[]{:S(2)}) collective-permute-start(bf16[2,256,512]{2,1,0:T(8,128)(2,1)S(1)} %collective-permute-done.b1), channel_id=1, source_target_pairs={{0,1},{1,2},{2,3},{3,0},{4,5},{5,6},{6,7},{7,4},{8,9},{9,10},{10,1... | collective-permute-start | bytes 1572872 | tf_op jit(solution)/shard_map/ppermute | solution.py:23
  14.2 41.0 %collective-permute-start.7 = (bf16[8,128,512]{2,1,0:T(8,128)(2,1)}, bf16[8,128,512]{2,1,0:T(8,128)(2,1)S(1)}, u32[]{:S(2)}, u32[]{:S(2)}) collective-permute-start(bf16[8,128,512]{2,1,0:T(8,128)(2,1)} %own.1), channel_id=1, source_target_pairs={{0,4},{4,8},{8,12},{12,16},{16,20},{20,24},{24,28},{28,32},{32,36}... | collective-permute-start | bytes 3145736 | tf_op jit(solution)/shard_map/ppermute | solution.py:18
  20.7 34.5 %collective-permute-start.8 = (bf16[8,128,512]{2,1,0:T(8,128)(2,1)}, bf16[8,128,512]{2,1,0:T(8,128)(2,1)}, u32[]{:S(2)}, u32[]{:S(2)}) collective-permute-start(bf16[8,128,512]{2,1,0:T(8,128)(2,1)} %own.1), channel_id=1, source_target_pairs={{4,0},{8,4},{12,8},{16,12},{20,16},{24,20},{28,24},{32,28},{36,32}... | collective-permute-start | bytes 3145736 | tf_op jit(solution)/shard_map/ppermute | solution.py:18
  22.6 21.2 %collective-permute-start.4 = (bf16[2,256,512]{2,1,0:T(8,128)(2,1)S(1)}, bf16[2,256,512]{2,1,0:T(8,128)(2,1)S(1)}, u32[]{:S(2)}, u32[]{:S(2)}) collective-permute-start(bf16[2,256,512]{2,1,0:T(8,128)(2,1)S(1)} %collective-permute-done.b1), channel_id=1, source_target_pairs={{4,0},{8,4},{12,8},{16,12},{20,16},{24,20},{28,24},{32,28},{36,32}... | collective-permute-start | bytes 1572872 | tf_op jit(solution)/shard_map/ppermute | solution.py:18
  24.6 22.2 %collective-permute-start.5 = (bf16[2,256,512]{2,1,0:T(8,128)(2,1)S(1)}, bf16[2,256,512]{2,1,0:T(8,128)(2,1)}, u32[]{:S(2)}, u32[]{:S(2)}) collective-permute-start(bf16[2,256,512]{2,1,0:T(8,128)(2,1)S(1)} %collective-permute-done.2.n0), channel_id=1, source_target_pairs={{4,7},{5,4},{6,5},{7,6},{12,15},{13,12},{14,13},{15,14},{20,23},{2... | collective-permute-start | bytes 1572872 | tf_op jit(solution)/shard_map/ppermute | solution.py:29
  29.2 26.0 %collective-permute-start.6 = (bf16[2,256,512]{2,1,0:T(8,128)(2,1)S(1)}, bf16[2,256,512]{2,1,0:T(8,128)(2,1)}, u32[]{:S(2)}, u32[]{:S(2)}) collective-permute-start(bf16[2,256,512]{2,1,0:T(8,128)(2,1)S(1)} %collective-permute-done.1.b2), channel_id=1, source_target_pairs={{4,0},{12,8},{20,16},{28,24},{36,32},{44,40},{52,48},{60,56},{68,6... | collective-permute-start | bytes 1572872 | tf_op jit(solution)/shard_map/ppermute | solution.py:34
  43.8 0.8 %copy-start.2 = (bf16[2,256,512]{2,1,0:T(8,128)(2,1)}, bf16[2,256,512]{2,1,0:T(8,128)(2,1)S(1)}, u32[]{:S(2)}) copy-start(bf16[2,256,512]{2,1,0:T(8,128)(2,1)S(1)} %collective-permute-done.4.n1) | copy-start | bytes 1572868
  44.6 15.0 %collective-permute-start.10 = (bf16[2,256,512]{2,1,0:T(8,128)(2,1)S(1)}, bf16[2,256,512]{2,1,0:T(8,128)(2,1)}, u32[]{:S(2)}, u32[]{:S(2)}) collective-permute-start(bf16[2,256,512]{2,1,0:T(8,128)(2,1)S(1)} %collective-permute-done.3.b3), channel_id=1, source_target_pairs={{4,0},{12,8},{20,16},{28,24},{36,32},{44,40},{52,48},{60,56},{68,6... | collective-permute-start | bytes 1572872 | tf_op jit(solution)/shard_map/ppermute | solution.py:34
  46.7 13.0 %collective-permute-start.9 = (bf16[2,256,512]{2,1,0:T(8,128)(2,1)}, bf16[2,256,512]{2,1,0:T(8,128)(2,1)}, u32[]{:S(2)}, u32[]{:S(2)}) collective-permute-start(bf16[2,256,512]{2,1,0:T(8,128)(2,1)} %collective-permute-done.5.n2x), channel_id=1, source_target_pairs={{4,7},{5,4},{6,5},{7,6},{12,15},{13,12},{14,13},{15,14},{20,23},{2... | collective-permute-start | bytes 1572872 | tf_op jit(solution)/shard_map/ppermute | solution.py:29
  53.4 1.0 %copy-start.1 = (bf16[2,256,512]{2,1,0:T(8,128)(2,1)S(1)}, bf16[2,256,512]{2,1,0:T(8,128)(2,1)}, u32[]{:S(2)}) copy-start(bf16[2,256,512]{2,1,0:T(8,128)(2,1)} %b0.1) | copy-start | bytes 1572868
  54.4 1.2 %copy-start = (bf16[8,128,512]{2,1,0:T(8,128)(2,1)S(1)}, bf16[8,128,512]{2,1,0:T(8,128)(2,1)}, u32[]{:S(2)}) copy-start(bf16[8,128,512]{2,1,0:T(8,128)(2,1)} %own.1) | copy-start | bytes 3145732
  54.4 1.4 %copy-start.3 = (bf16[2,256,512]{2,1,0:T(8,128)(2,1)S(1)}, bf16[2,256,512]{2,1,0:T(8,128)(2,1)}, u32[]{:S(2)}) copy-start(bf16[2,256,512]{2,1,0:T(8,128)(2,1)} %copy-done.2) | copy-start | bytes 1572868

commit v6 on v2

--- a/solution.py
+++ b/solution.py
@@ -6,6 +6,7 @@
 from jax.sharding import PartitionSpec as P
 
 damping = 0.7
+ROW = 16
 
 
 SMEM = pl.BlockSpec(memory_space=pltpu.SMEM)
@@ -25,7 +26,19 @@
 
 def along_rep_odd(x, distance):
     n, m = lax.axis_size("orb"), lax.axis_size("rep")
-    route = [(o * m + i, o * m + (i + distance * (o % 2)) % m) for o in range(n) for i in range(m)]
+    route = [(o * m + i, o * m + (i + distance) % m) for o in range(1, n, 2) for i in range(m)]
+    return lax.ppermute(x, ("orb", "rep"), route)
+
+
+def along_rows(x, distance):
+    n = lax.axis_size("orb")
+    route = [(i - distance, i) for i in range(n) if 0 <= i - distance < n]
+    return lax.ppermute(x, "orb", [(s, t) for s, t in route if s // ROW == t // ROW])
+
+
+def between_rows(x, distance):
+    n, m = lax.axis_size("orb"), lax.axis_size("rep")
+    route = [(o * m + i, (o - 1) * m + (i + distance) % m) for o in range(ROW, n, ROW) for i in range(m)]
     return lax.ppermute(x, ("orb", "rep"), route)
 
 
@@ -143,11 +156,13 @@
     return call(body, acc_shape(b0), [SMEM] + [VMEM] * 3)(ids, b0, b1, b2)
 
 
-def next_part(ids, b0, b1, b2, n0, n1, n2x, n2c):
-    def body(ids, b0, b1, b2, n0, n1, n2x, n2c, out):
-        products(ids, (b0, b1, b2), [whole(n0), whole(n1), either(ids, n2x, n2c)], out)
-
-    return call(body, acc_shape(b0), [SMEM] + [VMEM] * 7)(ids, b0, b1, b2, n0, n1, n2x, n2c)
+def next_part(ids, b0, b1, b2, n0, n1, n1e, n2x, n2c):
+    def body(ids, b0, b1, b2, n0, n1, n1e, n2x, n2c, out):
+        last = lax.rem(ids[0], ROW) == ROW - 1
+        lft = lambda j: jnp.where(last, n1e[j], n1[j])
+        products(ids, (b0, b1, b2), [whole(n0), lft, either(ids, n2x, n2c)], out)
+
+    return call(body, acc_shape(b0), [SMEM] + [VMEM] * 8)(ids, b0, b1, b2, n0, n1, n1e, n2x, n2c)
 
 
 def pair_slot(ids, orbs, p, orbitals):
@@ -238,7 +253,8 @@
     amps_prev = along_orb(amplitudes, 1)
     n2x = along_rep_odd(n0, -1)
     b3 = along_rep(b1, 1)
-    n1 = along_orb(b1, -1)
+    n1 = along_rows(b1, -1)
+    n1e = between_rows(b0, 1)
     n2c = odd_to_even(b2)
     n3x = along_rep_odd(n2x, -1)
     n3c = odd_to_even(b3)
@@ -250,7 +266,7 @@
         amps_prev, amplitudes, amps_next,
     )
     own_acc = own_part(ids, b0, b1, b2)
-    next_acc = next_part(ids, b0, b1, b2, n0, n1, n2x, n2c)
+    next_acc = next_part(ids, b0, b1, b2, n0, n1, n1e, n2x, n2c)
     part = partial_update(ids, orbs, own_acc, next_acc, pre, wgt, b3)
     return last_update(ids, orbs, part, wgt, b3, n3x, n3c)
 

time: 61.5 us -> 61.8 us (level)
  the two profiles are of different devices: /device:TPU:24 before, /device:TPU:251 now
where the time goes in v6:
time: 61.8 us; the launch traced here: 61.3 us
  starting transfers between devices  33.1 us (54%)
  waiting for transfers between devices  12.7 us (21%)
  Pallas kernels  10 us (16%)
  local copies, waits for them, and re-layouts  4.45 us (7%)
  other arithmetic  0.76 us (1%)
    ppermute x3, waiting for transfers between devices, along_rep(): return lax.ppermute(x, 'rep', [(i, (i + distance) % n) for i in range(n)])  12.7 us
    ppermute x1, starting transfers between devices, along_rows(): lax.ppermute(x, 'orb', [(s, t) for s, t in route if s // ROW == t // ROW])  9.07 us
    ppermute x3, starting transfers between devices, along_orb(): lax.ppermute(x, 'orb', [(i - distance, i) for i in range(n) if 0 <= i - d...  8.21 us
    ppermute x2, starting transfers between devices, along_rep_odd(): return lax.ppermute(x, ('orb', 'rep'), route)  6.74 us
    ppermute x2, starting transfers between devices, odd_to_even(): return lax.ppermute(x, 'orb', [(o, o - 1) for o in range(1, n, 2)])  5.67 us
    unnamed x24, local copies, waits for them, and re-layouts  3.57 us
    pallas_call x1, Pallas kernels, coupled_terms(): return call(couple_kernel, (shape, shape), specs, scratch)(*args)  3.12 us
    ppermute x3, starting transfers between devices, along_rep(): return lax.ppermute(x, 'rep', [(i, (i + distance) % n) for i in range(n)])  2.75 us
  transfers between devices with their start and end apart: 12, of which 2 were waited for; matrix products, arithmetic and copies ran while one was open for 3% of the time, Pallas kernels for 12%

profile of v6, /device:TPU:251, one launch (start us, length us, event | category | flops | bytes accessed | tf_op | source)
XLA Modules:
  0.0 61.3 jit_solution(18405638359870927073)
XLA Ops:
  0.0 1.2 %collective-permute-start = (bf16[2,256,512]{2,1,0:T(8,128)(2,1)}, bf16[2,256,512]{2,1,0:T(8,128)(2,1)S(1)}, u32[]{:S(2)}, u32[]{:S(2)}) collective-permute-start(bf16[2,256,512]{2,1,0:T(8,128)(2,1)} %b0.3), channel_id=1, source_target_pairs={{0,1},{1,2},{2,3},{3,0},{4,5},{5,6},{6,7},{7,4},{8,9},{9,10},{10,1... | collective-permute-start | bytes 1572872 | tf_op jit(solution)/shard_map/ppermute | solution.py:24
  1.2 2.9 %collective-permute-start.2 = (bf16[2,256,512]{2,1,0:T(8,128)(2,1)}, bf16[2,256,512]{2,1,0:T(8,128)(2,1)S(1)}, u32[]{:S(2)}, u32[]{:S(2)}) collective-permute-start(bf16[2,256,512]{2,1,0:T(8,128)(2,1)} %b0.3), channel_id=1, source_target_pairs={{4,0},{8,4},{12,8},{16,12},{20,16},{24,20},{28,24},{32,28},{36,32}... | collective-permute-start | bytes 1572872 | tf_op jit(solution)/shard_map/ppermute | solution.py:19
  4.1 0.3 collective-permute-start.1
  4.4 0.7 %collective-permute-start.4 = (bf16[2,256,512]{2,1,0:T(8,128)(2,1)}, bf16[2,256,512]{2,1,0:T(8,128)(2,1)S(1)}, u32[]{:S(2)}, u32[]{:S(2)}) collective-permute-start(bf16[2,256,512]{2,1,0:T(8,128)(2,1)} %b0.3), channel_id=1, source_target_pairs={{64,61},{65,62},{66,63},{67,60},{128,125},{129,126},{130,127},{131... | collective-permute-start | bytes 1572872 | tf_op jit(solution)/shard_map/ppermute | solution.py:42
  5.1 7.9 %collective-permute-done.b1 = bf16[2,256,512]{2,1,0:T(8,128)(2,1)S(1)} collective-permute-done((bf16[2,256,512]{2,1,0:T(8,128)(2,1)}, bf16[2,256,512]{2,1,0:T(8,128)(2,1)S(1)}, u32[]{:S(2)}, u32[]{:S(2)}) %collective-permute-start) | collective-permute-done | bytes 524320 | tf_op jit(solution)/shard_map/ppermute | solution.py:24
  13.0 9.1 %collective-permute-start.3 = (bf16[2,256,512]{2,1,0:T(8,128)(2,1)S(1)}, bf16[2,256,512]{2,1,0:T(8,128)(2,1)S(1)}, u32[]{:S(2)}, u32[]{:S(2)}) collective-permute-start(bf16[2,256,512]{2,1,0:T(8,128)(2,1)S(1)} %collective-permute-done.b1), channel_id=1, source_target_pairs={{4,0},{8,4},{12,8},{16,12},{20,16},{24,20},{28,24},{32,28},{36,32}... | collective-permute-start | bytes 1572872 | tf_op jit(solution)/shard_map/ppermute | solution.py:36
  22.1 1.3 %collective-permute-start.7 = (bf16[8,128,512]{2,1,0:T(8,128)(2,1)}, bf16[8,128,512]{2,1,0:T(8,128)(2,1)S(1)}, u32[]{:S(2)}, u32[]{:S(2)}) collective-permute-start(bf16[8,128,512]{2,1,0:T(8,128)(2,1)} %own.1), channel_id=1, source_target_pairs={{0,4},{4,8},{8,12},{12,16},{16,20},{20,24},{24,28},{28,32},{32,36}... | collective-permute-start | bytes 3145736 | tf_op jit(solution)/shard_map/ppermute | solution.py:19
  23.4 0.0 collective-permute-done.2.n0
  23.4 4.0 %collective-permute-start.8 = (bf16[8,128,512]{2,1,0:T(8,128)(2,1)}, bf16[8,128,512]{2,1,0:T(8,128)(2,1)}, u32[]{:S(2)}, u32[]{:S(2)}) collective-permute-start(bf16[8,128,512]{2,1,0:T(8,128)(2,1)} %own.1), channel_id=1, source_target_pairs={{4,0},{8,4},{12,8},{16,12},{20,16},{24,20},{28,24},{32,28},{36,32}... | collective-permute-start | bytes 3145736 | tf_op jit(solution)/shard_map/ppermute | solution.py:19
  27.4 0.0 collective-permute-done.1.b2
  27.4 1.2 %collective-permute-start.9 = (bf16[2,256,512]{2,1,0:T(8,128)(2,1)S(1)}, bf16[2,256,512]{2,1,0:T(8,128)(2,1)S(1)}, u32[]{:S(2)}, u32[]{:S(2)}) collective-permute-start(bf16[2,256,512]{2,1,0:T(8,128)(2,1)S(1)} %collective-permute-done.b1), channel_id=1, source_target_pairs={{0,1},{1,2},{2,3},{3,0},{4,5},{5,6},{6,7},{7,4},{8,9},{9,10},{10,1... | collective-permute-start | bytes 1572872 | tf_op jit(solution)/shard_map/ppermute | solution.py:24
  28.7 0.0 collective-permute-done.4.n1e
  28.7 0.8 %copy-done.4 = bf16[2,256,512]{2,1,0:T(8,128)(2,1)} copy-done((bf16[2,256,512]{2,1,0:T(8,128)(2,1)}, bf16[2,256,512]{2,1,0:T(8,128)(2,1)S(1)}, u32[]{:S(2)}) %copy-start.4) | copy-done | bytes 524312
  29.5 2.2 %collective-permute-start.5 = (bf16[2,256,512]{2,1,0:T(8,128)(2,1)S(1)}, bf16[2,256,512]{2,1,0:T(8,128)(2,1)}, u32[]{:S(2)}, u32[]{:S(2)}) collective-permute-start(bf16[2,256,512]{2,1,0:T(8,128)(2,1)S(1)} %collective-permute-done.2.n0), channel_id=1, source_target_pairs={{4,7},{5,4},{6,5},{7,6},{12,15},{13,12},{14,13},{15,14},{20,23},{2... | collective-permute-start | bytes 1572872 | tf_op jit(solution)/shard_map/ppermute | solution.py:30
  31.6 0.0 copy-start.2
  31.6 0.8 %copy-done.2 = bf16[2,256,512]{2,1,0:T(8,128)(2,1)} copy-done((bf16[2,256,512]{2,1,0:T(8,128)(2,1)}, bf16[2,256,512]{2,1,0:T(8,128)(2,1)S(1)}, u32[]{:S(2)}) %copy-start.2) | copy-done | bytes 524312
  32.4 0.0 collective-permute-done.3.n1
  32.4 0.8 %copy-done.6 = bf16[2,256,512]{2,1,0:T(8,128)(2,1)} copy-done((bf16[2,256,512]{2,1,0:T(8,128)(2,1)}, bf16[2,256,512]{2,1,0:T(8,128)(2,1)S(1)}, u32[]{:S(2)}) %copy-start.6) | copy-done | bytes 524312
  33.2 2.6 %collective-permute-start.6 = (bf16[2,256,512]{2,1,0:T(8,128)(2,1)S(1)}, bf16[2,256,512]{2,1,0:T(8,128)(2,1)}, u32[]{:S(2)}, u32[]{:S(2)}) collective-permute-start(bf16[2,256,512]{2,1,0:T(8,128)(2,1)S(1)} %collective-permute-done.1.b2), channel_id=1, source_target_pairs={{4,0},{12,8},{20,16},{28,24},{36,32},{44,40},{52,48},{60,56},{68,6... | collective-permute-start | bytes 1572872 | tf_op jit(solution)/shard_map/ppermute | solution.py:47
  35.8 4.8 %collective-permute-done.9.b3.left = bf16[2,256,512]{2,1,0:T(8,128)(2,1)S(1)} collective-permute-done((bf16[2,256,512]{2,1,0:T(8,128)(2,1)S(1)}, bf16[2,256,512]{2,1,0:T(8,128)(2,1)S(1)}, u32[]{:S(2)}, u32[]{:S(2)}) %collective-permute-start.9) | collective-permute-done | bytes 524320 | tf_op jit(solution)/shard_map/ppermute | solution.py:24
  40.6 3.1 %collective-permute-start.11 = (bf16[2,256,512]{2,1,0:T(8,128)(2,1)S(1)}, bf16[2,256,512]{2,1,0:T(8,128)(2,1)S(1)}, u32[]{:S(2)}, u32[]{:S(2)}) collective-permute-start(bf16[2,256,512]{2,1,0:T(8,128)(2,1)S(1)} %collective-permute-done.9.b3.left), channel_id=1, source_target_pairs={{4,0},{12,8},{20,16},{28,24},{36,32},{44,40},{52,48},{60,56},{68,6... | collective-permute-start | bytes 1572872 | tf_op jit(solution)/shard_map/ppermute | solution.py:47
  43.7 0.0 collective-permute-done.5.n2x
  43.7 4.6 %collective-permute-start.10 = (bf16[2,256,512]{2,1,0:T(8,128)(2,1)}, bf16[2,256,512]{2,1,0:T(8,128)(2,1)}, u32[]{:S(2)}, u32[]{:S(2)}) collective-permute-start(bf16[2,256,512]{2,1,0:T(8,128)(2,1)} %collective-permute-done.5.n2x), channel_id=1, source_target_pairs={{4,7},{5,4},{6,5},{7,6},{12,15},{13,12},{14,13},{15,14},{20,23},{2... | collective-permute-start | bytes 1572872 | tf_op jit(solution)/shard_map/ppermute | solution.py:30
  48.3 0.8 %dynamic-slice_bitcast_fusion = f32[128,1]{0,1:T(1,128)S(1)} fusion(f32[512]{0:T(512)} %param.12, s32[]{:T(128)S(6)} %select_n.3), kind=kLoop, calls=%fused_computation.2 | loop fusion | bytes 1028 | tf_op jit(solution)/shard_map/broadcast_in_dim | solution.py:262
  49.1 0.1 copy.8.mine
  49.2 0.1 pad_add_fusion.ids
  49.3 0.7 %convert_bitcast_fusion.fock = f32[4,8]{1,0:T(4,128)S(1)} fusion(bf16[8,4]{0,1:T(4,128)(2,1)} %param.11), kind=kLoop, calls=%fused_computation | loop fusion | flops 32 | bytes 192 | tf_op jit(solution)/shard_map/convert_element_type | solution.py:263
  50.0 1.0 %copy-done = bf16[2,256,512]{2,1,0:T(8,128)(2,1)S(1)} copy-done((bf16[2,256,512]{2,1,0:T(8,128)(2,1)S(1)}, bf16[2,256,512]{2,1,0:T(8,128)(2,1)}, u32[]{:S(2)}) %copy-start) | copy-done | bytes 524312
  51.0 1.1 %shard_map.73.own_acc = f32[2,2,128,512]{3,2,1,0:T(8,128)S(1)} custom-call(s32[2]{0:T(128)S(1)} %pad_add_fusion.ids, bf16[2,256,512]{2,1,0:T(8,128)(2,1)S(1)} %copy-done, bf16[2,256,512]{2,1,0:T(8,128)(2,1)S(1)} %collective-permute-done.b1, bf16[2,256,512]{2,1,0:T(8,128)(2,1)S(1)} %collective-permute-done.1.b2), custom_call_target="tpu_custom_call" | custom-call | flops 100000000 | bytes 4194304 | tf_op jit(solution)/shard_map/pallas_call | solution.py:156
  52.2 0.0 copy-start.1
  52.2 0.0 copy-start.8
  52.2 0.0 copy-start.9
  52.2 0.0 copy-start.10
  52.2 0.0 copy-start.11
  52.2 0.0 collective-permute-done.6.n2c
  52.2 0.0 copy-done.3
  52.2 0.0 copy-done.5
  52.3 0.1 copy-done.7
  52.4 1.9 %shard_map.74.next_acc = f32[2,2,128,512]{3,2,1,0:T(8,128)S(1)} custom-call(s32[2]{0:T(128)S(1)} %pad_add_fusion.ids, bf16[2,256,512]{2,1,0:T(8,128)(2,1)S(1)} %copy-done, bf16[2,256,512]{2,1,0:T(8,128)(2,1)S(1)} %collective-permute-done.b1, bf16[2,256,512]{2,1,0:T(8,128)(2,1)S(1)} %collective-permute-done.1.b2, bf16[2,256,512]{2,1,0:T(8,128)(2,1)S(1)} %copy-done.3, ...), custom_call_target="tpu_custom_call" | custom-call | flops 100000000 | bytes 4194304 | tf_op jit(solution)/shard_map/pallas_call | solution.py:165
  54.3 0.0 collective-permute-done.7.prev
  54.3 0.0 collective-permute-done.8.nxt
  54.3 0.0 copy-done.1
  54.3 0.0 copy-done.8
  54.3 3.1 %shard_map.75 = (f32[8,128,512]{2,1,0:T(8,128)S(1)}, f32[8,128,512]{2,1,0:T(8,128)S(1)}) custom-call(s32[2]{0:T(128)S(1)} %pad_add_fusion.ids, s32[2,8]{1,0:T(2,128)S(1)} %bitcast.9, s32[4,8]{1,0:T(4,128)S(1)} %bitcast.12, f32[4,8]{1,0:T(4,128)S(1)} %convert_bitcast_fusion.fock, f32[128]{0:T(128)S(1)} %copy-done.11, f32[128,1]{1,0:T(8,128)S(1)} %copy.8.mine, ...), custom_call_target="tpu_custom_call" | custom-call | flops 100000000 | bytes 4194304 | tf_op jit(solution)/shard_map/pallas_call | solution.py:109
  57.5 1.4 %shard_map.76.part = f32[8,128,512]{2,1,0:T(8,128)S(1)} custom-call(s32[2]{0:T(128)S(1)} %pad_add_fusion.ids, s32[2,8]{1,0:T(2,128)S(1)} %bitcast.10, f32[2,2,128,512]{3,2,1,0:T(8,128)S(1)} %shard_map.73.own_acc, f32[2,2,128,512]{3,2,1,0:T(8,128)S(1)} %shard_map.74.next_acc, f32[8,128,512]{2,1,0:T(8,128)S(1)} %get-tuple-element.7.pre, ...), custom_call_target="tpu_custom_call" | custom-call | flops 100000000 | bytes 4194304 | tf_op jit(solution)/shard_map/pallas_call | solution.py:197
  58.9 0.0 collective-permute-done.11.n3c
  58.9 0.0 collective-permute-done.10.n3x
  58.9 2.4 %shard_map.77 = bf16[8,128,512]{2,1,0:T(8,128)(2,1)} custom-call(s32[2]{0:T(128)S(1)} %pad_add_fusion.ids, s32[2,8]{1,0:T(2,128)S(1)} %bitcast.11, f32[8,128,512]{2,1,0:T(8,128)S(1)} %shard_map.76.part, f32[8,128,512]{2,1,0:T(8,128)S(1)} %get-tuple-element.8.wgt, bf16[2,256,512]{2,1,0:T(8,128)(2,1)S(1)} %collective-permute-done.9.b3.left, ...), custom_call_target="tpu_custom_call" | custom-call | flops 100000000 | bytes 4194304 | tf_op jit(solution)/shard_map/pallas_call | solution.py:235
  (9 shorter events, 0.0 us)
Async XLA Ops:
  0.0 13.0 %collective-permute-start = (bf16[2,256,512]{2,1,0:T(8,128)(2,1)}, bf16[2,256,512]{2,1,0:T(8,128)(2,1)S(1)}, u32[]{:S(2)}, u32[]{:S(2)}) collective-permute-start(bf16[2,256,512]{2,1,0:T(8,128)(2,1)} %b0.3), channel_id=1, source_target_pairs={{0,1},{1,2},{2,3},{3,0},{4,5},{5,6},{6,7},{7,4},{8,9},{9,10},{10,1... | collective-permute-start | bytes 1572872 | tf_op jit(solution)/shard_map/ppermute | solution.py:24
  1.2 22.2 %collective-permute-start.2 = (bf16[2,256,512]{2,1,0:T(8,128)(2,1)}, bf16[2,256,512]{2,1,0:T(8,128)(2,1)S(1)}, u32[]{:S(2)}, u32[]{:S(2)}) collective-permute-start(bf16[2,256,512]{2,1,0:T(8,128)(2,1)} %b0.3), channel_id=1, source_target_pairs={{4,0},{8,4},{12,8},{16,12},{20,16},{24,20},{28,24},{32,28},{36,32}... | collective-permute-start | bytes 1572872 | tf_op jit(solution)/shard_map/ppermute | solution.py:19
  4.1 23.3 %collective-permute-start.1 = (bf16[2,256,512]{2,1,0:T(8,128)(2,1)}, bf16[2,256,512]{2,1,0:T(8,128)(2,1)S(1)}, u32[]{:S(2)}, u32[]{:S(2)}) collective-permute-start(bf16[2,256,512]{2,1,0:T(8,128)(2,1)} %b0.3), channel_id=1, source_target_pairs={{0,3},{1,0},{2,1},{3,2},{4,7},{5,4},{6,5},{7,6},{8,11},{9,8},{10,9... | collective-permute-start | bytes 1572872 | tf_op jit(solution)/shard_map/ppermute | solution.py:24
  4.4 24.2 %collective-permute-start.4 = (bf16[2,256,512]{2,1,0:T(8,128)(2,1)}, bf16[2,256,512]{2,1,0:T(8,128)(2,1)S(1)}, u32[]{:S(2)}, u32[]{:S(2)}) collective-permute-start(bf16[2,256,512]{2,1,0:T(8,128)(2,1)} %b0.3), channel_id=1, source_target_pairs={{64,61},{65,62},{66,63},{67,60},{128,125},{129,126},{130,127},{131... | collective-permute-start | bytes 1572872 | tf_op jit(solution)/shard_map/ppermute | solution.py:42
  13.0 19.4 %collective-permute-start.3 = (bf16[2,256,512]{2,1,0:T(8,128)(2,1)S(1)}, bf16[2,256,512]{2,1,0:T(8,128)(2,1)S(1)}, u32[]{:S(2)}, u32[]{:S(2)}) collective-permute-start(bf16[2,256,512]{2,1,0:T(8,128)(2,1)S(1)} %collective-permute-done.b1), channel_id=1, source_target_pairs={{4,0},{8,4},{12,8},{16,12},{20,16},{24,20},{28,24},{32,28},{36,32}... | collective-permute-start | bytes 1572872 | tf_op jit(solution)/shard_map/ppermute | solution.py:36
  22.1 32.2 %collective-permute-start.7 = (bf16[8,128,512]{2,1,0:T(8,128)(2,1)}, bf16[8,128,512]{2,1,0:T(8,128)(2,1)S(1)}, u32[]{:S(2)}, u32[]{:S(2)}) collective-permute-start(bf16[8,128,512]{2,1,0:T(8,128)(2,1)} %own.1), channel_id=1, source_target_pairs={{0,4},{4,8},{8,12},{12,16},{16,20},{20,24},{24,28},{28,32},{32,36}... | collective-permute-start | bytes 3145736 | tf_op jit(solution)/shard_map/ppermute | solution.py:19
  23.4 30.9 %collective-permute-start.8 = (bf16[8,128,512]{2,1,0:T(8,128)(2,1)}, bf16[8,128,512]{2,1,0:T(8,128)(2,1)}, u32[]{:S(2)}, u32[]{:S(2)}) collective-permute-start(bf16[8,128,512]{2,1,0:T(8,128)(2,1)} %own.1), channel_id=1, source_target_pairs={{4,0},{8,4},{12,8},{16,12},{20,16},{24,20},{28,24},{32,28},{36,32}... | collective-permute-start | bytes 3145736 | tf_op jit(solution)/shard_map/ppermute | solution.py:19
  27.4 13.2 %collective-permute-start.9 = (bf16[2,256,512]{2,1,0:T(8,128)(2,1)S(1)}, bf16[2,256,512]{2,1,0:T(8,128)(2,1)S(1)}, u32[]{:S(2)}, u32[]{:S(2)}) collective-permute-start(bf16[2,256,512]{2,1,0:T(8,128)(2,1)S(1)} %collective-permute-done.b1), channel_id=1, source_target_pairs={{0,1},{1,2},{2,3},{3,0},{4,5},{5,6},{6,7},{7,4},{8,9},{9,10},{10,1... | collective-permute-start | bytes 1572872 | tf_op jit(solution)/shard_map/ppermute | solution.py:24
  28.7 0.8 %copy-start.4 = (bf16[2,256,512]{2,1,0:T(8,128)(2,1)}, bf16[2,256,512]{2,1,0:T(8,128)(2,1)S(1)}, u32[]{:S(2)}) copy-start(bf16[2,256,512]{2,1,0:T(8,128)(2,1)S(1)} %collective-permute-done.4.n1e) | copy-start | bytes 1572868
  29.5 14.3 %collective-permute-start.5 = (bf16[2,256,512]{2,1,0:T(8,128)(2,1)S(1)}, bf16[2,256,512]{2,1,0:T(8,128)(2,1)}, u32[]{:S(2)}, u32[]{:S(2)}) collective-permute-start(bf16[2,256,512]{2,1,0:T(8,128)(2,1)S(1)} %collective-permute-done.2.n0), channel_id=1, source_target_pairs={{4,7},{5,4},{6,5},{7,6},{12,15},{13,12},{14,13},{15,14},{20,23},{2... | collective-permute-start | bytes 1572872 | tf_op jit(solution)/shard_map/ppermute | solution.py:30
  31.6 0.8 %copy-start.2 = (bf16[2,256,512]{2,1,0:T(8,128)(2,1)}, bf16[2,256,512]{2,1,0:T(8,128)(2,1)S(1)}, u32[]{:S(2)}) copy-start(bf16[2,256,512]{2,1,0:T(8,128)(2,1)S(1)} %collective-permute-done.2.n0) | copy-start | bytes 1572868
  32.4 0.8 %copy-start.6 = (bf16[2,256,512]{2,1,0:T(8,128)(2,1)}, bf16[2,256,512]{2,1,0:T(8,128)(2,1)S(1)}, u32[]{:S(2)}) copy-start(bf16[2,256,512]{2,1,0:T(8,128)(2,1)S(1)} %collective-permute-done.3.n1) | copy-start | bytes 1572868
  33.2 19.0 %collective-permute-start.6 = (bf16[2,256,512]{2,1,0:T(8,128)(2,1)S(1)}, bf16[2,256,512]{2,1,0:T(8,128)(2,1)}, u32[]{:S(2)}, u32[]{:S(2)}) collective-permute-start(bf16[2,256,512]{2,1,0:T(8,128)(2,1)S(1)} %collective-permute-done.1.b2), channel_id=1, source_target_pairs={{4,0},{12,8},{20,16},{28,24},{36,32},{44,40},{52,48},{60,56},{68,6... | collective-permute-start | bytes 1572872 | tf_op jit(solution)/shard_map/ppermute | solution.py:47
  40.6 18.3 %collective-permute-start.11 = (bf16[2,256,512]{2,1,0:T(8,128)(2,1)S(1)}, bf16[2,256,512]{2,1,0:T(8,128)(2,1)S(1)}, u32[]{:S(2)}, u32[]{:S(2)}) collective-permute-start(bf16[2,256,512]{2,1,0:T(8,128)(2,1)S(1)} %collective-permute-done.9.b3.left), channel_id=1, source_target_pairs={{4,0},{12,8},{20,16},{28,24},{36,32},{44,40},{52,48},{60,56},{68,6... | collective-permute-start | bytes 1572872 | tf_op jit(solution)/shard_map/ppermute | solution.py:47
  43.7 15.2 %collective-permute-start.10 = (bf16[2,256,512]{2,1,0:T(8,128)(2,1)}, bf16[2,256,512]{2,1,0:T(8,128)(2,1)}, u32[]{:S(2)}, u32[]{:S(2)}) collective-permute-start(bf16[2,256,512]{2,1,0:T(8,128)(2,1)} %collective-permute-done.5.n2x), channel_id=1, source_target_pairs={{4,7},{5,4},{6,5},{7,6},{12,15},{13,12},{14,13},{15,14},{20,23},{2... | collective-permute-start | bytes 1572872 | tf_op jit(solution)/shard_map/ppermute | solution.py:30
  50.0 1.0 %copy-start = (bf16[2,256,512]{2,1,0:T(8,128)(2,1)S(1)}, bf16[2,256,512]{2,1,0:T(8,128)(2,1)}, u32[]{:S(2)}) copy-start(bf16[2,256,512]{2,1,0:T(8,128)(2,1)} %b0.3) | copy-start | bytes 1572868
  51.0 1.2 %copy-start.3 = (bf16[2,256,512]{2,1,0:T(8,128)(2,1)S(1)}, bf16[2,256,512]{2,1,0:T(8,128)(2,1)}, u32[]{:S(2)}) copy-start(bf16[2,256,512]{2,1,0:T(8,128)(2,1)} %copy-done.2) | copy-start | bytes 1572868
  51.0 1.2 %copy-start.5 = (bf16[2,256,512]{2,1,0:T(8,128)(2,1)S(1)}, bf16[2,256,512]{2,1,0:T(8,128)(2,1)}, u32[]{:S(2)}) copy-start(bf16[2,256,512]{2,1,0:T(8,128)(2,1)} %copy-done.4) | copy-start | bytes 1572868
  51.0 1.4 %copy-start.7 = (bf16[2,256,512]{2,1,0:T(8,128)(2,1)S(1)}, bf16[2,256,512]{2,1,0:T(8,128)(2,1)}, u32[]{:S(2)}) copy-start(bf16[2,256,512]{2,1,0:T(8,128)(2,1)} %copy-done.6) | copy-start | bytes 1572868
  52.2 2.1 %copy-start.1 = (bf16[8,128,512]{2,1,0:T(8,128)(2,1)S(1)}, bf16[8,128,512]{2,1,0:T(8,128)(2,1)}, u32[]{:S(2)}) copy-start(bf16[8,128,512]{2,1,0:T(8,128)(2,1)} %own.1) | copy-start | bytes 3145732
  52.2 2.1 %copy-start.8 = (s32[8,2]{0,1:T(2,128)S(1)}, s32[8,2]{0,1:T(2,128)}, u32[]{:S(2)}) copy-start(s32[8,2]{0,1:T(2,128)} %param.9) | copy-start | bytes 196
  52.2 2.1 %copy-start.9 = (s32[8,4]{0,1:T(4,128)S(1)}, s32[8,4]{0,1:T(4,128)}, u32[]{:S(2)}) copy-start(s32[8,4]{0,1:T(4,128)} %param.10) | copy-start | bytes 388
  52.2 2.1 %copy-start.10 = (f32[512]{0:T(512)S(1)}, f32[512]{0:T(512)}, u32[]{:S(2)}) copy-start(f32[512]{0:T(512)} %param.12) | copy-start | bytes 6148
  52.2 2.1 %copy-start.11 = (f32[128]{0:T(128)S(1)}, f32[128]{0:T(128)}, u32[]{:S(2)}) copy-start(f32[128]{0:T(128)} %occ.1) | copy-start | bytes 1540

commit v7 on v5

v7 whole, which is shorter than its diff:
```python
import jax
import jax.numpy as jnp
from jax import lax
from jax.experimental import pallas as pl
from jax.experimental.pallas import tpu as pltpu
from jax.sharding import PartitionSpec as P

damping = 0.7


SMEM = pl.BlockSpec(memory_space=pltpu.SMEM)
VMEM = pl.BlockSpec(memory_space=pltpu.VMEM)
ANY = pl.BlockSpec(memory_space=pl.ANY)


def along_orb(x, distance):
    n = lax.axis_size("orb")
    return lax.ppermute(x, "orb", [(i - distance, i) for i in range(n) if 0 <= i - distance < n])


def along_rep(x, distance):
    n = lax.axis_size("rep")
    return lax.ppermute(x, "rep", [(i, (i + distance) % n) for i in range(n)])


def along_rep_odd(x, distance):
    n, m = lax.axis_size("orb"), lax.axis_size("rep")
    route = [(o * m + i, o * m + (i + distance) % m) for o in range(1, n, 2) for i in range(m)]
    return lax.ppermute(x, ("orb", "rep"), route)


def odd_to_even(x):
    n = lax.axis_size("orb")
    return lax.ppermute(x, "orb", [(o, o - 1) for o in range(1, n, 2)])


def call(body, out_shape, in_specs, scratch):
    return pl.pallas_call(
        body,
        out_shape=out_shape,
        in_specs=in_specs,
        out_specs=jax.tree.map(lambda _: ANY, out_shape),
        scratch_shapes=scratch,
        compiler_params=pltpu.CompilerParams(vmem_limit_bytes=66 * 10**6),
        cost_estimate=pl.CostEstimate(flops=10**9, bytes_accessed=8 * 2**20, transcendentals=0),
    )


def dot_t(a, b):
    return lax.dot_general(a, b, (((0,), (0,)), ((), ())), preferred_element_type=jnp.float32)


def left_of(rep, blocks, rows):
    start = pl.multiple_of(rep[0] * rows, rows)
    return jnp.concatenate(
        [
            jnp.concatenate([b[i, :, pl.ds(start, rows)] for i in range(b.shape[0])], axis=1)
            for b in blocks
        ],
        axis=0,
    )


def products(lhs, right, out, offset=0):
    orbitals, _, rows, _ = out.shape
    for j in range(right[0].shape[0]):
        both = dot_t(lhs, jnp.concatenate([r[j] for r in right], axis=0))
        for i in range(orbitals):
            out[i, offset + j] = both[i * rows:(i + 1) * rows]


def pair_slot(orb, orbs, p, orbitals):
    base = orb[0] * orbitals
    return orbs[0, p] - base, orbs[1, p] - base


def on_odd(orb, odd_copy, even_copy):
    odd = lax.rem(orb[0], 2) == 1

    @pl.when(odd)
    def _():
        odd_copy.start()

    @pl.when(jnp.logical_not(odd))
    def _():
        even_copy.start()


def middle_kernel(
    orb, rep, fock, orbs_in, cpl_in, occ_in, energy_in, b0, b1, b2, b3, n0, n1, n2x, n2c,
    prev, own, nxt, part_out, wgt_out,
    orbs, cpl, occ, energy, mine, after, amps, acc, part, wgt, sems, part_sems, wgt_sem,
):
    pair_count, rows, width = part.shape
    orbitals, depth, _ = b0.shape
    copy = pltpu.make_async_copy
    tables = [
        copy(orbs_in, orbs, sems.at[0]), copy(cpl_in, cpl, sems.at[1]),
        copy(occ_in, occ, sems.at[2]), copy(energy_in, energy, sems.at[3]),
    ]
    first = [copy(b, mine.at[q], sems.at[4 + q]) for q, b in enumerate((b0, b1, b2, b3))]
    second = [copy(b, after.at[q], sems.at[8 + q]) for q, b in enumerate((n0, n1))]
    third = copy(n2x, after.at[2], sems.at[10])
    fourth = [
        copy(a, amps.at[pl.ds(k * pair_count, pair_count)], sems.at[11 + k])
        for k, a in enumerate((prev, own, nxt))
    ]
    for c in tables + first + second:
        c.start()
    on_odd(orb, third, copy(n2c, after.at[2], sems.at[10]))
    for c in fourth:
        c.start()
    for c in tables:
        c.wait()
    energies = energy[:, pl.ds(pl.multiple_of(rep[0] * rows, rows), rows)]
    tile = jnp.transpose(jnp.broadcast_to(energies, (rows, rows)))

    def denominators(p, carry):
        shift = occ[orbs[0, p]] + occ[orbs[1, p]]
        for c in range(0, width, rows):
            wgt[p, :, c:c + rows] = damping / (tile + (energy[:, c:c + rows] - shift))
        return carry

    lax.fori_loop(0, pair_count, denominators, 0)
    wgt_copy = copy(wgt, wgt_out, wgt_sem)
    wgt_copy.start()
    for c in first:
        c.wait()
    quarters = [mine.at[q] for q in range(4)]
    lhs = left_of(rep, quarters, rows)
    products(lhs, quarters, acc)
    for c in second + [third]:
        c.wait()
    products(lhs[:3 * depth], [after.at[q] for q in range(3)], acc, orbitals)
    for c in fourth:
        c.wait()
    before = (orb[0] - 1) * pair_count
    step = 32

    def pair(p, carry):
        i, j = pair_slot(orb, orbs, p, orbitals)
        slots = [cpl[c, p] - before for c in range(cpl.shape[0])]
        scales = [fock[c, p] for c in range(cpl.shape[0])]
        for r in range(0, rows, step):
            rs = pl.ds(r, step)
            total = -acc[i, j, rs, :]
            for s, f in zip(slots, scales):
                total = total + f * amps[s, rs, :].astype(jnp.float32)
            old = amps[p + pair_count, rs, :].astype(jnp.float32)
            part[p, rs, :] = (1.0 - damping) * old + wgt[p, rs, :] * total
        copy(part.at[p], part_out.at[p], part_sems.at[p]).start()
        return carry

    def wait(p, carry):
        copy(part.at[p], part_out.at[p], part_sems.at[p]).wait()
        return carry

    lax.fori_loop(0, pair_count, pair, 0)
    lax.fori_loop(0, pair_count, wait, 0)
    wgt_copy.wait()


def middle(*args):
    orbs, cpl, occ, energy, block = args[3:8]
    own = args[-2]
    orbitals, _, width = block.shape
    pairs, rows, _ = own.shape
    shape = jax.ShapeDtypeStruct(own.shape, jnp.float32)
    scratch = [
        pltpu.SMEM(orbs.shape, orbs.dtype),
        pltpu.SMEM(cpl.shape, cpl.dtype),
        pltpu.SMEM(occ.shape, occ.dtype),
        pltpu.VMEM(energy.shape, energy.dtype),
        pltpu.VMEM((4,) + block.shape, block.dtype),
        pltpu.VMEM((3,) + block.shape, block.dtype),
        pltpu.VMEM((3 * pairs, rows, width), own.dtype),
        pltpu.VMEM((orbitals, 2 * orbitals, rows, width), jnp.float32),
        pltpu.VMEM(own.shape, jnp.float32),
        pltpu.VMEM(own.shape, jnp.float32),
        pltpu.SemaphoreType.DMA((14,)),
        pltpu.SemaphoreType.DMA((pairs,)),
        pltpu.SemaphoreType.DMA,
    ]
    return call(middle_kernel, (shape, shape), [SMEM] * 3 + [ANY] * 15, scratch)(*args)


def last_kernel(
    orb, rep, orbs_in, part_in, wgt_in, b3, n3x, n3c, out,
    orbs, part, wgt, mine, after, acc, done, sems, in_sems, out_sems,
):
    orbitals, _, rows, _ = acc.shape
    copy = pltpu.make_async_copy
    first = [copy(orbs_in, orbs, sems.at[0]), copy(b3, mine, sems.at[1])]
    second = copy(n3x, after, sems.at[2])
    on_odd(orb, second, copy(n3c, after, sems.at[2]))
    for c in first:
        c.start()

    def load(p, carry):
        copy(part_in.at[p], part.at[p], in_sems.at[0, p]).start()
        copy(wgt_in.at[p], wgt.at[p], in_sems.at[1, p]).start()
        return carry

    lax.fori_loop(0, done.shape[0], load, 0)
    for c in first + [second]:
        c.wait()
    products(left_of(rep, [mine], rows), [after], acc)

    def pair(p, carry):
        i, j = pair_slot(orb, orbs, p, orbitals)
        copy(part_in.at[p], part.at[p], in_sems.at[0, p]).wait()
        copy(wgt_in.at[p], wgt.at[p], in_sems.at[1, p]).wait()

        @pl.when(j >= orbitals)
        def _():
            done[p] = (part[p] - wgt[p] * acc[i, j - orbitals]).astype(done.dtype)

        @pl.when(j < orbitals)
        def _():
            done[p] = part[p].astype(done.dtype)

        copy(done.at[p], out.at[p], out_sems.at[p]).start()
        return carry

    def wait(p, carry):
        copy(done.at[p], out.at[p], out_sems.at[p]).wait()
        return carry

    lax.fori_loop(0, done.shape[0], pair, 0)
    lax.fori_loop(0, done.shape[0], wait, 0)


def last_update(*args):
    orbs, part, _, block = args[2:6]
    orbitals, _, width = block.shape
    pairs, rows, _ = part.shape
    scratch = [
        pltpu.SMEM(orbs.shape, orbs.dtype),
        pltpu.VMEM(part.shape, part.dtype),
        pltpu.VMEM(part.shape, part.dtype),
        pltpu.VMEM(block.shape, block.dtype),
        pltpu.VMEM(block.shape, block.dtype),
        pltpu.VMEM((orbitals, orbitals, rows, width), jnp.float32),
        pltpu.VMEM(part.shape, jnp.bfloat16),
        pltpu.SemaphoreType.DMA((3,)),
        pltpu.SemaphoreType.DMA((2, pairs)),
        pltpu.SemaphoreType.DMA((pairs,)),
    ]
    shape = jax.ShapeDtypeStruct(part.shape, jnp.bfloat16)
    return call(last_kernel, shape, [SMEM] * 2 + [ANY] * 6, scratch)(*args)


def device_step(
    blocks, amplitudes, pair_orbitals, coupling, fock_coupling, virtual_energy, occupied_energy
):
    orb = lax.axis_index("orb").astype(jnp.int32).reshape(1)
    rep = lax.axis_index("rep").astype(jnp.int32).reshape(1)
    orbs = pair_orbitals.T
    b0 = blocks
    n0 = along_orb(b0, -1)
    b1 = along_rep(b0, 1)
    b2 = along_rep(b0, -1)
    amps_next = along_orb(amplitudes, -1)
    amps_prev = along_orb(amplitudes, 1)
    n2x = along_rep_odd(n0, -1)
    b3 = along_rep(b1, 1)
    n1 = along_orb(b1, -1)
    n2c = odd_to_even(b2)
    n3x = along_rep_odd(n2x, -1)
    n3c = odd_to_even(b3)
    fock = fock_coupling.T.astype(jnp.float32)
    part, wgt = middle(
        orb, rep, fock, orbs, coupling.T, occupied_energy, virtual_energy[None, :],
        b0, b1, b2, b3, n0, n1, n2x, n2c, amps_prev, amplitudes, amps_next,
    )
    return last_update(orb, rep, orbs, part, wgt, b3, n3x, n3c)


def solution(mesh):
    placed = (
        P("orb", "rep", None),
        P("orb", "rep", None),
        P("orb", None),
        P("orb", None),
        P("orb", None),
        P(),
        P(),
    )
    return jax.shard_map(
        device_step, mesh=mesh, in_specs=placed, out_specs=P("orb", "rep", None), check_vma=False
    )
```

time: 62.9 us -> 63 us (level)
  the two profiles are of different devices: /device:TPU:97 before, /device:TPU:121 now
where the time goes in v7:
time: 63 us; the launch traced here: 62.7 us
  starting transfers between devices  29.7 us (47%)
  waiting for transfers between devices  20.8 us (33%)
  Pallas kernels  10 us (16%)
  other arithmetic  1.22 us (2%)
  local copies, waits for them, and re-layouts  0.83 us (1%)
    ppermute x4, starting transfers between devices, along_orb(): lax.ppermute(x, 'orb', [(i - distance, i) for i in range(n) if 0 <= i - d...  13.1 us
    ppermute x4, waiting for transfers between devices, along_orb(): lax.ppermute(x, 'orb', [(i - distance, i) for i in range(n) if 0 <= i - d...  12.1 us
    ppermute x2, starting transfers between devices, along_rep_odd(): return lax.ppermute(x, ('orb', 'rep'), route)  9.16 us
    ppermute x3, waiting for transfers between devices, along_rep(): return lax.ppermute(x, 'rep', [(i, (i + distance) % n) for i in range(n)])  8.62 us
    pallas_call x1, Pallas kernels, middle(): call(middle_kernel, (shape, shape), [SMEM] * 3 + [ANY] * 15, scratch)(*args)  6.62 us
    ppermute x2, starting transfers between devices, odd_to_even(): return lax.ppermute(x, 'orb', [(o, o - 1) for o in range(1, n, 2)])  4.65 us
    pallas_call x1, Pallas kernels, last_update(): return call(last_kernel, shape, [SMEM] * 2 + [ANY] * 6, scratch)(*args)  3.4 us
    ppermute x3, starting transfers between devices, along_rep(): return lax.ppermute(x, 'rep', [(i, (i + distance) % n) for i in range(n)])  2.76 us
  transfers between devices with their start and end apart: 11, of which 2 were waited for; matrix products, arithmetic and copies ran while one was open for 2% of the time, Pallas kernels for 11%

profile of v7, /device:TPU:121, one launch (start us, length us, event | category | flops | bytes accessed | tf_op | source)
XLA Modules:
  0.0 62.7 jit_solution(17539911920788535033)
XLA Ops:
  0.0 1.2 %collective-permute-start = (bf16[2,256,512]{2,1,0:T(8,128)(2,1)}, bf16[2,256,512]{2,1,0:T(8,128)(2,1)S(1)}, u32[]{:S(2)}, u32[]{:S(2)}) collective-permute-start(bf16[2,256,512]{2,1,0:T(8,128)(2,1)} %b0.1), channel_id=1, source_target_pairs={{0,1},{1,2},{2,3},{3,0},{4,5},{5,6},{6,7},{7,4},{8,9},{9,10},{10,1... | collective-permute-start | bytes 1572872 | tf_op jit(solution)/shard_map/ppermute | solution.py:23
  1.2 2.9 %collective-permute-start.3 = (bf16[2,256,512]{2,1,0:T(8,128)(2,1)}, bf16[2,256,512]{2,1,0:T(8,128)(2,1)S(1)}, u32[]{:S(2)}, u32[]{:S(2)}) collective-permute-start(bf16[2,256,512]{2,1,0:T(8,128)(2,1)} %b0.1), channel_id=1, source_target_pairs={{4,0},{8,4},{12,8},{16,12},{20,16},{24,20},{28,24},{32,28},{36,32}... | collective-permute-start | bytes 1572872 | tf_op jit(solution)/shard_map/ppermute | solution.py:18
  4.1 1.5 %collective-permute-start.1 = (bf16[2,256,512]{2,1,0:T(8,128)(2,1)}, bf16[2,256,512]{2,1,0:T(8,128)(2,1)S(1)}, u32[]{:S(2)}, u32[]{:S(2)}) collective-permute-start(bf16[2,256,512]{2,1,0:T(8,128)(2,1)} %b0.1), channel_id=1, source_target_pairs={{0,3},{1,0},{2,1},{3,2},{4,7},{5,4},{6,5},{7,6},{8,11},{9,8},{10,9... | collective-permute-start | bytes 1572872 | tf_op jit(solution)/shard_map/ppermute | solution.py:23
  5.6 8.6 %collective-permute-done.b1 = bf16[2,256,512]{2,1,0:T(8,128)(2,1)S(1)} collective-permute-done((bf16[2,256,512]{2,1,0:T(8,128)(2,1)}, bf16[2,256,512]{2,1,0:T(8,128)(2,1)S(1)}, u32[]{:S(2)}, u32[]{:S(2)}) %collective-permute-start) | collective-permute-done | bytes 524320 | tf_op jit(solution)/shard_map/ppermute | solution.py:23
  14.2 0.0 copy-start.1
  14.2 0.0 collective-permute-start.2
  14.2 6.4 %collective-permute-start.7 = (bf16[8,128,512]{2,1,0:T(8,128)(2,1)}, bf16[8,128,512]{2,1,0:T(8,128)(2,1)}, u32[]{:S(2)}, u32[]{:S(2)}) collective-permute-start(bf16[8,128,512]{2,1,0:T(8,128)(2,1)} %own.1), channel_id=1, source_target_pairs={{0,4},{4,8},{8,12},{12,16},{16,20},{20,24},{24,28},{28,32},{32,36}... | collective-permute-start | bytes 3145736 | tf_op jit(solution)/shard_map/ppermute | solution.py:18
  20.7 1.9 %collective-permute-start.8 = (bf16[8,128,512]{2,1,0:T(8,128)(2,1)}, bf16[8,128,512]{2,1,0:T(8,128)(2,1)}, u32[]{:S(2)}, u32[]{:S(2)}) collective-permute-start(bf16[8,128,512]{2,1,0:T(8,128)(2,1)} %own.1), channel_id=1, source_target_pairs={{4,0},{8,4},{12,8},{16,12},{20,16},{24,20},{28,24},{32,28},{36,32}... | collective-permute-start | bytes 3145736 | tf_op jit(solution)/shard_map/ppermute | solution.py:18
  22.6 0.0 collective-permute-done.3.n0
  22.6 0.0 copy-start.2
  22.6 1.9 %collective-permute-start.4 = (bf16[2,256,512]{2,1,0:T(8,128)(2,1)S(1)}, bf16[2,256,512]{2,1,0:T(8,128)(2,1)S(1)}, u32[]{:S(2)}, u32[]{:S(2)}) collective-permute-start(bf16[2,256,512]{2,1,0:T(8,128)(2,1)S(1)} %collective-permute-done.b1), channel_id=1, source_target_pairs={{4,0},{8,4},{12,8},{16,12},{20,16},{24,20},{28,24},{32,28},{36,32}... | collective-permute-start | bytes 1572872 | tf_op jit(solution)/shard_map/ppermute | solution.py:18
  24.6 0.0 collective-permute-done.1.b2
  24.6 0.0 copy-start.3
  24.6 4.6 %collective-permute-start.5 = (bf16[2,256,512]{2,1,0:T(8,128)(2,1)S(1)}, bf16[2,256,512]{2,1,0:T(8,128)(2,1)}, u32[]{:S(2)}, u32[]{:S(2)}) collective-permute-start(bf16[2,256,512]{2,1,0:T(8,128)(2,1)S(1)} %collective-permute-done.3.n0), channel_id=1, source_target_pairs={{4,7},{5,4},{6,5},{7,6},{12,15},{13,12},{14,13},{15,14},{20,23},{2... | collective-permute-start | bytes 1572872 | tf_op jit(solution)/shard_map/ppermute | solution.py:29
  29.2 0.0 collective-permute-done.2.b3
  29.2 0.0 copy-start
  29.2 2.5 %collective-permute-start.6 = (bf16[2,256,512]{2,1,0:T(8,128)(2,1)S(1)}, bf16[2,256,512]{2,1,0:T(8,128)(2,1)S(1)}, u32[]{:S(2)}, u32[]{:S(2)}) collective-permute-start(bf16[2,256,512]{2,1,0:T(8,128)(2,1)S(1)} %collective-permute-done.1.b2), channel_id=1, source_target_pairs={{4,0},{12,8},{20,16},{28,24},{36,32},{44,40},{52,48},{60,56},{68,6... | collective-permute-start | bytes 1572872 | tf_op jit(solution)/shard_map/ppermute | solution.py:34
  31.7 0.0 copy-done.1
  31.7 12.1 %collective-permute-done.4.n1 = bf16[2,256,512]{2,1,0:T(8,128)(2,1)S(1)} collective-permute-done((bf16[2,256,512]{2,1,0:T(8,128)(2,1)S(1)}, bf16[2,256,512]{2,1,0:T(8,128)(2,1)S(1)}, u32[]{:S(2)}, u32[]{:S(2)}) %collective-permute-start.4) | collective-permute-done | bytes 524320 | tf_op jit(solution)/shard_map/ppermute | solution.py:18
  43.8 0.0 copy-done.2
  43.8 0.0 copy-start.4
  43.8 2.1 %collective-permute-start.10 = (bf16[2,256,512]{2,1,0:T(8,128)(2,1)S(1)}, bf16[2,256,512]{2,1,0:T(8,128)(2,1)}, u32[]{:S(2)}, u32[]{:S(2)}) collective-permute-start(bf16[2,256,512]{2,1,0:T(8,128)(2,1)S(1)} %collective-permute-done.2.b3), channel_id=1, source_target_pairs={{4,0},{12,8},{20,16},{28,24},{36,32},{44,40},{52,48},{60,56},{68,6... | collective-permute-start | bytes 1572872 | tf_op jit(solution)/shard_map/ppermute | solution.py:34
  46.0 0.0 collective-permute-done.5.n2x
  46.0 0.0 copy-done.3
  46.0 4.6 %collective-permute-start.9 = (bf16[2,256,512]{2,1,0:T(8,128)(2,1)}, bf16[2,256,512]{2,1,0:T(8,128)(2,1)}, u32[]{:S(2)}, u32[]{:S(2)}) collective-permute-start(bf16[2,256,512]{2,1,0:T(8,128)(2,1)} %collective-permute-done.5.n2x), channel_id=1, source_target_pairs={{4,7},{5,4},{6,5},{7,6},{12,15},{13,12},{14,13},{15,14},{20,23},{2... | collective-permute-start | bytes 1572872 | tf_op jit(solution)/shard_map/ppermute | solution.py:29
  50.6 1.2 %convert_bitcast_fusion.fock = f32[4,8]{1,0:T(4,128)} fusion(bf16[8,4]{0,1:T(4,128)(2,1)} %param.11), kind=kLoop, calls=%fused_computation | loop fusion | flops 32 | bytes 192 | tf_op jit(solution)/shard_map/convert_element_type | solution.py:271
  51.8 0.0 collective-permute-done.6.n2c
  51.8 0.0 copy-done.4
  51.8 0.0 copy-start.5
  51.8 0.0 collective-permute-done.7.prev
  51.8 0.8 %copy-done.5 = bf16[2,256,512]{2,1,0:T(8,128)(2,1)} copy-done((bf16[2,256,512]{2,1,0:T(8,128)(2,1)}, bf16[2,256,512]{2,1,0:T(8,128)(2,1)S(1)}, u32[]{:S(2)}) %copy-start.5) | copy-done | bytes 524312
  52.6 0.0 collective-permute-done.8.nxt
  52.6 0.0 copy-done
  52.6 6.6 %shard_map.73 = (f32[8,128,512]{2,1,0:T(8,128)}, f32[8,128,512]{2,1,0:T(8,128)}) custom-call(s32[1]{0:T(128)} %bitcast.orb, s32[1]{0:T(128)} %bitcast.1.rep, f32[4,8]{1,0:T(4,128)} %convert_bitcast_fusion.fock, s32[2,8]{1,0:T(2,128)} %bitcast.7, s32[4,8]{1,0:T(4,128)} %bitcast.9, f32[128]{0:T(128)} %occ_in.1, f32[1,512]{1,0:T(1,128)} %bitcast.10, ...), custom_call_target="tpu_custom_call" | custom-call | flops 1000000000 | bytes 8388608 | tf_op jit(solution)/shard_map/pallas_call | solution.py:184
  59.3 0.0 collective-permute-done.10.n3c
  59.3 0.0 collective-permute-done.9.n3x
  59.3 3.4 %shard_map.74 = bf16[8,128,512]{2,1,0:T(8,128)(2,1)} custom-call(s32[1]{0:T(128)} %bitcast.orb, s32[1]{0:T(128)} %bitcast.1.rep, s32[2,8]{1,0:T(2,128)} %bitcast.8, f32[8,128,512]{2,1,0:T(8,128)} %get-tuple-element.7.part_in, f32[8,128,512]{2,1,0:T(8,128)} %get-tuple-element.8.wgt_in, bf16[2,256,512]{2,1,0:T(8,128)(2,1)} %copy-done, ...), custom_call_target="tpu_custom_call" | custom-call | flops 1000000000 | bytes 8388608 | tf_op jit(solution)/shard_map/pallas_call | solution.py:250
Async XLA Ops:
  0.0 14.2 %collective-permute-start = (bf16[2,256,512]{2,1,0:T(8,128)(2,1)}, bf16[2,256,512]{2,1,0:T(8,128)(2,1)S(1)}, u32[]{:S(2)}, u32[]{:S(2)}) collective-permute-start(bf16[2,256,512]{2,1,0:T(8,128)(2,1)} %b0.1), channel_id=1, source_target_pairs={{0,1},{1,2},{2,3},{3,0},{4,5},{5,6},{6,7},{7,4},{8,9},{9,10},{10,1... | collective-permute-start | bytes 1572872 | tf_op jit(solution)/shard_map/ppermute | solution.py:23
  1.2 21.4 %collective-permute-start.3 = (bf16[2,256,512]{2,1,0:T(8,128)(2,1)}, bf16[2,256,512]{2,1,0:T(8,128)(2,1)S(1)}, u32[]{:S(2)}, u32[]{:S(2)}) collective-permute-start(bf16[2,256,512]{2,1,0:T(8,128)(2,1)} %b0.1), channel_id=1, source_target_pairs={{4,0},{8,4},{12,8},{16,12},{20,16},{24,20},{28,24},{32,28},{36,32}... | collective-permute-start | bytes 1572872 | tf_op jit(solution)/shard_map/ppermute | solution.py:18
  4.1 20.5 %collective-permute-start.1 = (bf16[2,256,512]{2,1,0:T(8,128)(2,1)}, bf16[2,256,512]{2,1,0:T(8,128)(2,1)S(1)}, u32[]{:S(2)}, u32[]{:S(2)}) collective-permute-start(bf16[2,256,512]{2,1,0:T(8,128)(2,1)} %b0.1), channel_id=1, source_target_pairs={{0,3},{1,0},{2,1},{3,2},{4,7},{5,4},{6,5},{7,6},{8,11},{9,8},{10,9... | collective-permute-start | bytes 1572872 | tf_op jit(solution)/shard_map/ppermute | solution.py:23
  14.2 17.5 %copy-start.1 = (bf16[2,256,512]{2,1,0:T(8,128)(2,1)}, bf16[2,256,512]{2,1,0:T(8,128)(2,1)S(1)}, u32[]{:S(2)}) copy-start(bf16[2,256,512]{2,1,0:T(8,128)(2,1)S(1)} %collective-permute-done.b1) | copy-start | bytes 1572868
  14.2 14.9 %collective-permute-start.2 = (bf16[2,256,512]{2,1,0:T(8,128)(2,1)S(1)}, bf16[2,256,512]{2,1,0:T(8,128)(2,1)S(1)}, u32[]{:S(2)}, u32[]{:S(2)}) collective-permute-start(bf16[2,256,512]{2,1,0:T(8,128)(2,1)S(1)} %collective-permute-done.b1), channel_id=1, source_target_pairs={{0,1},{1,2},{2,3},{3,0},{4,5},{5,6},{6,7},{7,4},{8,9},{9,10},{10,1... | collective-permute-start | bytes 1572872 | tf_op jit(solution)/shard_map/ppermute | solution.py:23
  14.2 37.6 %collective-permute-start.7 = (bf16[8,128,512]{2,1,0:T(8,128)(2,1)}, bf16[8,128,512]{2,1,0:T(8,128)(2,1)}, u32[]{:S(2)}, u32[]{:S(2)}) collective-permute-start(bf16[8,128,512]{2,1,0:T(8,128)(2,1)} %own.1), channel_id=1, source_target_pairs={{0,4},{4,8},{8,12},{12,16},{16,20},{20,24},{24,28},{28,32},{32,36}... | collective-permute-start | bytes 3145736 | tf_op jit(solution)/shard_map/ppermute | solution.py:18
  20.7 31.9 %collective-permute-start.8 = (bf16[8,128,512]{2,1,0:T(8,128)(2,1)}, bf16[8,128,512]{2,1,0:T(8,128)(2,1)}, u32[]{:S(2)}, u32[]{:S(2)}) collective-permute-start(bf16[8,128,512]{2,1,0:T(8,128)(2,1)} %own.1), channel_id=1, source_target_pairs={{4,0},{8,4},{12,8},{16,12},{20,16},{24,20},{28,24},{32,28},{36,32}... | collective-permute-start | bytes 3145736 | tf_op jit(solution)/shard_map/ppermute | solution.py:18
  22.6 21.2 %copy-start.2 = (bf16[2,256,512]{2,1,0:T(8,128)(2,1)}, bf16[2,256,512]{2,1,0:T(8,128)(2,1)S(1)}, u32[]{:S(2)}) copy-start(bf16[2,256,512]{2,1,0:T(8,128)(2,1)S(1)} %collective-permute-done.3.n0) | copy-start | bytes 1572868
  22.6 21.2 %collective-permute-start.4 = (bf16[2,256,512]{2,1,0:T(8,128)(2,1)S(1)}, bf16[2,256,512]{2,1,0:T(8,128)(2,1)S(1)}, u32[]{:S(2)}, u32[]{:S(2)}) collective-permute-start(bf16[2,256,512]{2,1,0:T(8,128)(2,1)S(1)} %collective-permute-done.b1), channel_id=1, source_target_pairs={{4,0},{8,4},{12,8},{16,12},{20,16},{24,20},{28,24},{32,28},{36,32}... | collective-permute-start | bytes 1572872 | tf_op jit(solution)/shard_map/ppermute | solution.py:18
  24.6 21.4 %copy-start.3 = (bf16[2,256,512]{2,1,0:T(8,128)(2,1)}, bf16[2,256,512]{2,1,0:T(8,128)(2,1)S(1)}, u32[]{:S(2)}) copy-start(bf16[2,256,512]{2,1,0:T(8,128)(2,1)S(1)} %collective-permute-done.1.b2) | copy-start | bytes 1572868
  24.6 21.4 %collective-permute-start.5 = (bf16[2,256,512]{2,1,0:T(8,128)(2,1)S(1)}, bf16[2,256,512]{2,1,0:T(8,128)(2,1)}, u32[]{:S(2)}, u32[]{:S(2)}) collective-permute-start(bf16[2,256,512]{2,1,0:T(8,128)(2,1)S(1)} %collective-permute-done.3.n0), channel_id=1, source_target_pairs={{4,7},{5,4},{6,5},{7,6},{12,15},{13,12},{14,13},{15,14},{20,23},{2... | collective-permute-start | bytes 1572872 | tf_op jit(solution)/shard_map/ppermute | solution.py:29
  29.2 23.4 %copy-start = (bf16[2,256,512]{2,1,0:T(8,128)(2,1)}, bf16[2,256,512]{2,1,0:T(8,128)(2,1)S(1)}, u32[]{:S(2)}) copy-start(bf16[2,256,512]{2,1,0:T(8,128)(2,1)S(1)} %collective-permute-done.2.b3) | copy-start | bytes 1572868
  29.2 22.6 %collective-permute-start.6 = (bf16[2,256,512]{2,1,0:T(8,128)(2,1)S(1)}, bf16[2,256,512]{2,1,0:T(8,128)(2,1)S(1)}, u32[]{:S(2)}, u32[]{:S(2)}) collective-permute-start(bf16[2,256,512]{2,1,0:T(8,128)(2,1)S(1)} %collective-permute-done.1.b2), channel_id=1, source_target_pairs={{4,0},{12,8},{20,16},{28,24},{36,32},{44,40},{52,48},{60,56},{68,6... | collective-permute-start | bytes 1572872 | tf_op jit(solution)/shard_map/ppermute | solution.py:34
  43.8 8.0 %copy-start.4 = (bf16[2,256,512]{2,1,0:T(8,128)(2,1)}, bf16[2,256,512]{2,1,0:T(8,128)(2,1)S(1)}, u32[]{:S(2)}) copy-start(bf16[2,256,512]{2,1,0:T(8,128)(2,1)S(1)} %collective-permute-done.4.n1) | copy-start | bytes 1572868
  43.8 15.4 %collective-permute-start.10 = (bf16[2,256,512]{2,1,0:T(8,128)(2,1)S(1)}, bf16[2,256,512]{2,1,0:T(8,128)(2,1)}, u32[]{:S(2)}, u32[]{:S(2)}) collective-permute-start(bf16[2,256,512]{2,1,0:T(8,128)(2,1)S(1)} %collective-permute-done.2.b3), channel_id=1, source_target_pairs={{4,0},{12,8},{20,16},{28,24},{36,32},{44,40},{52,48},{60,56},{68,6... | collective-permute-start | bytes 1572872 | tf_op jit(solution)/shard_map/ppermute | solution.py:34
  46.0 13.3 %collective-permute-start.9 = (bf16[2,256,512]{2,1,0:T(8,128)(2,1)}, bf16[2,256,512]{2,1,0:T(8,128)(2,1)}, u32[]{:S(2)}, u32[]{:S(2)}) collective-permute-start(bf16[2,256,512]{2,1,0:T(8,128)(2,1)} %collective-permute-done.5.n2x), channel_id=1, source_target_pairs={{4,7},{5,4},{6,5},{7,6},{12,15},{13,12},{14,13},{15,14},{20,23},{2... | collective-permute-start | bytes 1572872 | tf_op jit(solution)/shard_map/ppermute | solution.py:29
  51.8 0.8 %copy-start.5 = (bf16[2,256,512]{2,1,0:T(8,128)(2,1)}, bf16[2,256,512]{2,1,0:T(8,128)(2,1)S(1)}, u32[]{:S(2)}) copy-start(bf16[2,256,512]{2,1,0:T(8,128)(2,1)S(1)} %collective-permute-done.6.n2c) | copy-start | bytes 1572868

commit v8 on v5

--- a/solution.py
+++ b/solution.py
@@ -50,8 +50,8 @@
     return lax.dot_general(a, b, (((0,), (0,)), ((), ())), preferred_element_type=jnp.float32)
 
 
-def left_of(rep, blocks, rows):
-    start = pl.multiple_of(rep[0] * rows, rows)
+def left_of(blocks, rows):
+    start = pl.multiple_of(lax.axis_index("rep") * rows, rows)
     return jnp.concatenate(
         [
             jnp.concatenate([b[i, :, pl.ds(start, rows)] for i in range(b.shape[0])], axis=1)
@@ -61,9 +61,9 @@
     )
 
 
-def products(rep, left, right, out, offset=0, base=None):
+def products(left, right, out, offset=0, base=None):
     orbitals, _, rows, _ = out.shape
-    lhs = left_of(rep, left, rows)
+    lhs = left_of(left, rows)
     for j in range(left[0].shape[0]):
         both = dot_t(lhs, jnp.concatenate([r(j) for r in right], axis=0))
         for i in range(orbitals):
@@ -81,26 +81,26 @@
     return lambda j: ref[j]
 
 
-def either(orb, odd_ref, even_ref):
-    odd = lax.rem(orb[0], 2) == 1
+def either(odd_ref, even_ref):
+    odd = lax.rem(lax.axis_index("orb"), 2) == 1
     return lambda j: jnp.where(odd, odd_ref[j], even_ref[j])
 
 
-def own_part(rep, b0, b1, b2, n0):
-    def body(rep, b0, b1, b2, n0, out):
-        products(rep, (b0, b1, b2), [whole(b) for b in (b0, b1, b2)], out)
-        products(rep, (b0,), [whole(n0)], out, b0.shape[0])
-
-    return call(body, acc_shape(b0, 2), [SMEM] + [VMEM] * 4)(rep, b0, b1, b2, n0)
-
-
-def pair_slot(orb, ints, p, orbitals):
-    base = orb[0] * orbitals
+def own_part(b0, b1, b2, n0):
+    def body(b0, b1, b2, n0, out):
+        products((b0, b1, b2), [whole(b) for b in (b0, b1, b2)], out)
+        products((b0,), [whole(n0)], out, b0.shape[0])
+
+    return call(body, acc_shape(b0, 2), [VMEM] * 4)(b0, b1, b2, n0)
+
+
+def pair_slot(ints, p, orbitals):
+    base = lax.axis_index("orb") * orbitals
     return ints[0, p] - base, ints[1, p] - base
 
 
 def middle_kernel(
-    orb, rep, ints, fock, occ, energies, base, b1, b2, b3, n1, n2x, n2c, prev, own, nxt,
+    ints, fock, occ, energies, base, b1, b2, b3, n1, n2x, n2c, prev, own, nxt,
     part, wgt, acc, amps, sems,
 ):
     pair_count, rows, width = part.shape
@@ -112,7 +112,7 @@
     for c in copies:
         c.start()
     first = energies.shape[1] - width
-    mine = energies[:, pl.ds(pl.multiple_of(first + rep[0] * rows, rows), rows)]
+    mine = energies[:, pl.ds(pl.multiple_of(first + lax.axis_index("rep") * rows, rows), rows)]
     tile = jnp.transpose(jnp.broadcast_to(mine, (rows, rows)))
 
     def denominators(p, carry):
@@ -123,15 +123,15 @@
         return carry
 
     lax.fori_loop(0, pair_count, denominators, 0)
-    products(rep, (b3,), [whole(b3)], acc, 0, base)
-    products(rep, (b1, b2), [whole(n1), either(orb, n2x, n2c)], acc, orbitals, base)
+    products((b3,), [whole(b3)], acc, 0, base)
+    products((b1, b2), [whole(n1), either(n2x, n2c)], acc, orbitals, base)
     for c in copies:
         c.wait()
-    before = (orb[0] - 1) * pair_count
+    before = (lax.axis_index("orb") - 1) * pair_count
     step = 32
 
     def pair(p, carry):
-        i, j = pair_slot(orb, ints, p, orbitals)
+        i, j = pair_slot(ints, p, orbitals)
         slots = [ints[2 + c, p] - before for c in range(fock.shape[0])]
         scales = [fock[c, p] for c in range(fock.shape[0])]
         for r in range(0, rows, step):
@@ -147,24 +147,24 @@
 
 
 def middle(*args):
-    base, own = args[6], args[-2]
+    base, own = args[4], args[-2]
     shape = jax.ShapeDtypeStruct(own.shape, jnp.float32)
     scratch = (
         pltpu.VMEM(base.shape, jnp.float32),
         pltpu.VMEM((3 * own.shape[0],) + own.shape[1:], own.dtype),
         pltpu.SemaphoreType.DMA((3,)),
     )
-    specs = [SMEM] * 5 + [VMEM] * 8 + [ANY] * 3
+    specs = [SMEM] * 3 + [VMEM] * 8 + [ANY] * 3
     return call(middle_kernel, (shape, shape), specs, scratch)(*args)
 
 
-def last_update(orb, rep, ints, part, wgt, b3, n3x, n3c):
-    def body(orb, rep, ints, part, wgt, b3, n3x, n3c, out, acc, done, sem):
+def last_update(ints, part, wgt, b3, n3x, n3c):
+    def body(ints, part, wgt, b3, n3x, n3c, out, acc, done, sem):
         orbitals = acc.shape[0]
-        products(rep, (b3,), [either(orb, n3x, n3c)], acc)
+        products((b3,), [either(n3x, n3c)], acc)
 
         def pair(p, carry):
-            i, j = pair_slot(orb, ints, p, orbitals)
+            i, j = pair_slot(ints, p, orbitals)
 
             @pl.when(j >= orbitals)
             def _():
@@ -192,15 +192,13 @@
     ]
     return call(
         body, jax.ShapeDtypeStruct(part.shape, jnp.bfloat16),
-        [SMEM] * 3 + [VMEM] * 5, scratch, out_specs=ANY,
-    )(orb, rep, ints, part, wgt, b3, n3x, n3c)
+        [SMEM] + [VMEM] * 5, scratch, out_specs=ANY,
+    )(ints, part, wgt, b3, n3x, n3c)
 
 
 def device_step(
     blocks, amplitudes, pair_orbitals, coupling, fock_coupling, virtual_energy, occupied_energy
 ):
-    orb = lax.axis_index("orb").astype(jnp.int32).reshape(1)
-    rep = lax.axis_index("rep").astype(jnp.int32).reshape(1)
     b0 = blocks
     n0 = along_orb(b0, -1)
     b1 = along_rep(b0, 1)
@@ -216,12 +214,12 @@
     fock = fock_coupling.T.astype(jnp.float32)
     ints = jnp.concatenate([pair_orbitals.T, coupling.T], axis=0)
     energies = jnp.concatenate([occupied_energy[None, :], virtual_energy[None, :]], axis=1)
-    base = own_part(rep, b0, b1, b2, n0)
+    base = own_part(b0, b1, b2, n0)
     part, wgt = middle(
-        orb, rep, ints, fock, energies, energies, base, b1, b2, b3, n1, n2x, n2c,
+        ints, fock, energies, energies, base, b1, b2, b3, n1, n2x, n2c,
         amps_prev, amplitudes, amps_next,
     )
-    return last_update(orb, rep, ints, part, wgt, b3, n3x, n3c)
+    return last_update(ints, part, wgt, b3, n3x, n3c)
 
 
 def solution(mesh):

time: 62.9 us -> 59.9 us (0.952)
  starting transfers between devices: 30.7 us -> 29.1 us
  Pallas kernels: 7.27 us -> 6.1 us
  local copies, waits for them, and re-layouts: 2.42 us -> 1.48 us
  waiting for transfers between devices: 19.8 us -> 20.6 us
    ppermute x2, starting transfers between devices: 5.42 us -> 3.85 us  [odd_to_even(): return lax.ppermute(x, 'orb', [(o, o - 1) for o in range(1, n, 2)])]
    unnamed x8 -> x4, local copies, waits for them, and re-layouts: 2.42 us -> 1.48 us
    ppermute x4, waiting for transfers between devices: 11.4 us -> 12.1 us  [along_orb(): lax.ppermute(x, 'orb', [(i - distance, i) for i in range(n) if 0 <= i - d...]
where the time goes in v8:
time: 59.9 us; the launch traced here: 59.5 us
  starting transfers between devices  29.1 us (49%)
  waiting for transfers between devices  20.6 us (34%)
  Pallas kernels  6.1 us (10%)
  other arithmetic  2.07 us (3%)
  local copies, waits for them, and re-layouts  1.48 us (2%)
    ppermute x4, starting transfers between devices, along_orb(): lax.ppermute(x, 'orb', [(i - distance, i) for i in range(n) if 0 <= i - d...  13.4 us
    ppermute x4, waiting for transfers between devices, along_orb(): lax.ppermute(x, 'orb', [(i - distance, i) for i in range(n) if 0 <= i - d...  12.1 us
    ppermute x2, starting transfers between devices, along_rep_odd(): return lax.ppermute(x, ('orb', 'rep'), route)  9.17 us
    ppermute x3, waiting for transfers between devices, along_rep(): return lax.ppermute(x, 'rep', [(i, (i + distance) % n) for i in range(n)])  8.42 us
    ppermute x2, starting transfers between devices, odd_to_even(): return lax.ppermute(x, 'orb', [(o, o - 1) for o in range(1, n, 2)])  3.85 us
    pallas_call x1, Pallas kernels, middle(): return call(middle_kernel, (shape, shape), specs, scratch)(*args)  3.29 us
    ppermute x3, starting transfers between devices, along_rep(): return lax.ppermute(x, 'rep', [(i, (i + distance) % n) for i in range(n)])  2.68 us
    pallas_call x1, Pallas kernels, last_update(): call(body, jax.ShapeDtypeStruct(part.shape, jnp.bfloat16), [SMEM] + [VMEM...  2.07 us
  transfers between devices with their start and end apart: 11, of which 2 were waited for; matrix products, arithmetic and copies ran while one was open for 3% of the time, Pallas kernels for 7%

profile of v8, /device:TPU:97, one launch (start us, length us, event | category | flops | bytes accessed | tf_op | source)
XLA Modules:
  0.0 59.5 jit_solution(18210512999348739476)
XLA Ops:
  0.0 1.2 %collective-permute-start = (bf16[2,256,512]{2,1,0:T(8,128)(2,1)}, bf16[2,256,512]{2,1,0:T(8,128)(2,1)S(1)}, u32[]{:S(2)}, u32[]{:S(2)}) collective-permute-start(bf16[2,256,512]{2,1,0:T(8,128)(2,1)} %b0.1), channel_id=1, source_target_pairs={{0,1},{1,2},{2,3},{3,0},{4,5},{5,6},{6,7},{7,4},{8,9},{9,10},{10,1... | collective-permute-start | bytes 1572872 | tf_op jit(solution)/shard_map/ppermute | solution.py:23
  1.2 1.5 %collective-permute-start.1 = (bf16[2,256,512]{2,1,0:T(8,128)(2,1)}, bf16[2,256,512]{2,1,0:T(8,128)(2,1)S(1)}, u32[]{:S(2)}, u32[]{:S(2)}) collective-permute-start(bf16[2,256,512]{2,1,0:T(8,128)(2,1)} %b0.1), channel_id=1, source_target_pairs={{0,3},{1,0},{2,1},{3,2},{4,7},{5,4},{6,5},{7,6},{8,11},{9,8},{10,9... | collective-permute-start | bytes 1572872 | tf_op jit(solution)/shard_map/ppermute | solution.py:23
  2.7 3.1 %collective-permute-start.2 = (bf16[2,256,512]{2,1,0:T(8,128)(2,1)}, bf16[2,256,512]{2,1,0:T(8,128)(2,1)S(1)}, u32[]{:S(2)}, u32[]{:S(2)}) collective-permute-start(bf16[2,256,512]{2,1,0:T(8,128)(2,1)} %b0.1), channel_id=1, source_target_pairs={{4,0},{8,4},{12,8},{16,12},{20,16},{24,20},{28,24},{32,28},{36,32}... | collective-permute-start | bytes 1572872 | tf_op jit(solution)/shard_map/ppermute | solution.py:18
  5.8 8.4 %collective-permute-done.b1 = bf16[2,256,512]{2,1,0:T(8,128)(2,1)S(1)} collective-permute-done((bf16[2,256,512]{2,1,0:T(8,128)(2,1)}, bf16[2,256,512]{2,1,0:T(8,128)(2,1)S(1)}, u32[]{:S(2)}, u32[]{:S(2)}) %collective-permute-start) | collective-permute-done | bytes 524320 | tf_op jit(solution)/shard_map/ppermute | solution.py:23
  14.2 0.0 collective-permute-start.3
  14.2 6.4 %collective-permute-start.7 = (bf16[8,128,512]{2,1,0:T(8,128)(2,1)}, bf16[8,128,512]{2,1,0:T(8,128)(2,1)S(1)}, u32[]{:S(2)}, u32[]{:S(2)}) collective-permute-start(bf16[8,128,512]{2,1,0:T(8,128)(2,1)} %own.1), channel_id=1, source_target_pairs={{0,4},{4,8},{8,12},{12,16},{16,20},{20,24},{24,28},{28,32},{32,36}... | collective-permute-start | bytes 3145736 | tf_op jit(solution)/shard_map/ppermute | solution.py:18
  20.7 1.9 %collective-permute-start.8 = (bf16[8,128,512]{2,1,0:T(8,128)(2,1)}, bf16[8,128,512]{2,1,0:T(8,128)(2,1)S(1)}, u32[]{:S(2)}, u32[]{:S(2)}) collective-permute-start(bf16[8,128,512]{2,1,0:T(8,128)(2,1)} %own.1), channel_id=1, source_target_pairs={{4,0},{8,4},{12,8},{16,12},{20,16},{24,20},{28,24},{32,28},{36,32}... | collective-permute-start | bytes 3145736 | tf_op jit(solution)/shard_map/ppermute | solution.py:18
  22.6 0.0 collective-permute-done.1.b2
  22.6 1.9 %collective-permute-start.4 = (bf16[2,256,512]{2,1,0:T(8,128)(2,1)S(1)}, bf16[2,256,512]{2,1,0:T(8,128)(2,1)S(1)}, u32[]{:S(2)}, u32[]{:S(2)}) collective-permute-start(bf16[2,256,512]{2,1,0:T(8,128)(2,1)S(1)} %collective-permute-done.b1), channel_id=1, source_target_pairs={{4,0},{8,4},{12,8},{16,12},{20,16},{24,20},{28,24},{32,28},{36,32}... | collective-permute-start | bytes 1572872 | tf_op jit(solution)/shard_map/ppermute | solution.py:18
  24.6 0.0 collective-permute-done.2.n0
  24.6 4.6 %collective-permute-start.5 = (bf16[2,256,512]{2,1,0:T(8,128)(2,1)S(1)}, bf16[2,256,512]{2,1,0:T(8,128)(2,1)S(1)}, u32[]{:S(2)}, u32[]{:S(2)}) collective-permute-start(bf16[2,256,512]{2,1,0:T(8,128)(2,1)S(1)} %collective-permute-done.2.n0), channel_id=1, source_target_pairs={{4,7},{5,4},{6,5},{7,6},{12,15},{13,12},{14,13},{15,14},{20,23},{2... | collective-permute-start | bytes 1572872 | tf_op jit(solution)/shard_map/ppermute | solution.py:29
  29.2 0.0 collective-permute-done.3.b3
  29.2 2.5 %collective-permute-start.6 = (bf16[2,256,512]{2,1,0:T(8,128)(2,1)S(1)}, bf16[2,256,512]{2,1,0:T(8,128)(2,1)S(1)}, u32[]{:S(2)}, u32[]{:S(2)}) collective-permute-start(bf16[2,256,512]{2,1,0:T(8,128)(2,1)S(1)} %collective-permute-done.1.b2), channel_id=1, source_target_pairs={{4,0},{12,8},{20,16},{28,24},{36,32},{44,40},{52,48},{60,56},{68,6... | collective-permute-start | bytes 1572872 | tf_op jit(solution)/shard_map/ppermute | solution.py:34
  31.7 12.1 %collective-permute-done.4.n1 = bf16[2,256,512]{2,1,0:T(8,128)(2,1)S(1)} collective-permute-done((bf16[2,256,512]{2,1,0:T(8,128)(2,1)S(1)}, bf16[2,256,512]{2,1,0:T(8,128)(2,1)S(1)}, u32[]{:S(2)}, u32[]{:S(2)}) %collective-permute-start.4) | collective-permute-done | bytes 524320 | tf_op jit(solution)/shard_map/ppermute | solution.py:18
  43.8 1.3 %collective-permute-start.10 = (bf16[2,256,512]{2,1,0:T(8,128)(2,1)S(1)}, bf16[2,256,512]{2,1,0:T(8,128)(2,1)S(1)}, u32[]{:S(2)}, u32[]{:S(2)}) collective-permute-start(bf16[2,256,512]{2,1,0:T(8,128)(2,1)S(1)} %collective-permute-done.3.b3), channel_id=1, source_target_pairs={{4,0},{12,8},{20,16},{28,24},{36,32},{44,40},{52,48},{60,56},{68,6... | collective-permute-start | bytes 1572872 | tf_op jit(solution)/shard_map/ppermute | solution.py:34
  45.2 0.0 collective-permute-done.5.n2x
  45.2 4.6 %collective-permute-start.9 = (bf16[2,256,512]{2,1,0:T(8,128)(2,1)S(1)}, bf16[2,256,512]{2,1,0:T(8,128)(2,1)S(1)}, u32[]{:S(2)}, u32[]{:S(2)}) collective-permute-start(bf16[2,256,512]{2,1,0:T(8,128)(2,1)S(1)} %collective-permute-done.5.n2x), channel_id=1, source_target_pairs={{4,7},{5,4},{6,5},{7,6},{12,15},{13,12},{14,13},{15,14},{20,23},{2... | collective-permute-start | bytes 1572872 | tf_op jit(solution)/shard_map/ppermute | solution.py:29
  49.8 0.7 %pad_maximum_fusion.occ.energies = f32[1,640]{1,0:T(1,128)S(1)} fusion(f32[1,512]{1,0:T(1,128)} %bitcast.7, f32[1,128]{1,0:T(1,128)} %bitcast.9), kind=kLoop, calls=%fused_computation.1 | loop fusion | flops 640 | bytes 5120 | tf_op jit(solution)/shard_map/concatenate | solution.py:216
  50.5 0.7 %pad_add_fusion.ints = s32[6,8]{1,0:T(8,128)S(1)} fusion(s32[4,8]{1,0:T(4,128)} %bitcast.6, s32[2,8]{1,0:T(2,128)} %bitcast.8), kind=kLoop, calls=%fused_computation | loop fusion | flops 48 | bytes 384 | tf_op jit(solution)/shard_map/concatenate | solution.py:215
  51.2 0.7 %convert_bitcast_fusion.fock = f32[4,8]{1,0:T(4,128)S(1)} fusion(bf16[8,4]{0,1:T(4,128)(2,1)} %param.11), kind=kLoop, calls=%fused_computation.2 | loop fusion | flops 32 | bytes 192 | tf_op jit(solution)/shard_map/convert_element_type | solution.py:214
  51.8 0.0 copy-start.1
  51.8 1.0 %copy-done.1 = bf16[2,256,512]{2,1,0:T(8,128)(2,1)S(1)} copy-done((bf16[2,256,512]{2,1,0:T(8,128)(2,1)S(1)}, bf16[2,256,512]{2,1,0:T(8,128)(2,1)}, u32[]{:S(2)}) %copy-start.1) | copy-done | bytes 524312
  52.9 0.0 copy-start
  52.9 0.7 %shard_map.73.base = f32[2,4,128,512]{3,2,1,0:T(8,128)S(1)} custom-call(bf16[2,256,512]{2,1,0:T(8,128)(2,1)S(1)} %copy-done.1, bf16[2,256,512]{2,1,0:T(8,128)(2,1)S(1)} %collective-permute-done.b1, bf16[2,256,512]{2,1,0:T(8,128)(2,1)S(1)} %collective-permute-done.1.b2, bf16[2,256,512]{2,1,0:T(8,128)(2,1)S(1)} %collective-permute-done.2.n0), custom_call_target="tpu_custom_call" | custom-call | flops 100000000 | bytes 4194304 | tf_op jit(solution)/shard_map/pallas_call | solution.py:94
  53.6 0.0 collective-permute-done.6.n2c
  53.6 0.0 collective-permute-done.7.prev
  53.7 0.0 collective-permute-done.8.nxt
  53.7 0.4 copy-done
  54.1 3.3 %shard_map.74 = (f32[8,128,512]{2,1,0:T(8,128)S(1)}, f32[8,128,512]{2,1,0:T(8,128)S(1)}) custom-call(s32[6,8]{1,0:T(8,128)S(1)} %pad_add_fusion.ints, f32[4,8]{1,0:T(4,128)S(1)} %convert_bitcast_fusion.fock, f32[1,640]{1,0:T(1,128)S(1)} %pad_maximum_fusion.occ.energies, f32[1,640]{1,0:T(1,128)S(1)} %pad_maximum_fusion.occ.energies, ...), custom_call_target="tpu_custom_call" | custom-call | flops 100000000 | bytes 4194304 | tf_op jit(solution)/shard_map/pallas_call | solution.py:158
  57.4 0.0 collective-permute-done.10.n3c
  57.4 0.0 collective-permute-done.9.n3x
  57.4 2.1 %shard_map.75 = bf16[8,128,512]{2,1,0:T(8,128)(2,1)} custom-call(s32[6,8]{1,0:T(8,128)S(1)} %pad_add_fusion.ints, f32[8,128,512]{2,1,0:T(8,128)S(1)} %get-tuple-element.7.part, f32[8,128,512]{2,1,0:T(8,128)S(1)} %get-tuple-element.8.wgt, bf16[2,256,512]{2,1,0:T(8,128)(2,1)S(1)} %collective-permute-done.3.b3, ...), custom_call_target="tpu_custom_call" | custom-call | flops 100000000 | bytes 4194304 | tf_op jit(solution)/shard_map/pallas_call | solution.py:193
Async XLA Ops:
  0.0 14.2 %collective-permute-start = (bf16[2,256,512]{2,1,0:T(8,128)(2,1)}, bf16[2,256,512]{2,1,0:T(8,128)(2,1)S(1)}, u32[]{:S(2)}, u32[]{:S(2)}) collective-permute-start(bf16[2,256,512]{2,1,0:T(8,128)(2,1)} %b0.1), channel_id=1, source_target_pairs={{0,1},{1,2},{2,3},{3,0},{4,5},{5,6},{6,7},{7,4},{8,9},{9,10},{10,1... | collective-permute-start | bytes 1572872 | tf_op jit(solution)/shard_map/ppermute | solution.py:23
  1.2 21.4 %collective-permute-start.1 = (bf16[2,256,512]{2,1,0:T(8,128)(2,1)}, bf16[2,256,512]{2,1,0:T(8,128)(2,1)S(1)}, u32[]{:S(2)}, u32[]{:S(2)}) collective-permute-start(bf16[2,256,512]{2,1,0:T(8,128)(2,1)} %b0.1), channel_id=1, source_target_pairs={{0,3},{1,0},{2,1},{3,2},{4,7},{5,4},{6,5},{7,6},{8,11},{9,8},{10,9... | collective-permute-start | bytes 1572872 | tf_op jit(solution)/shard_map/ppermute | solution.py:23
  2.7 21.9 %collective-permute-start.2 = (bf16[2,256,512]{2,1,0:T(8,128)(2,1)}, bf16[2,256,512]{2,1,0:T(8,128)(2,1)S(1)}, u32[]{:S(2)}, u32[]{:S(2)}) collective-permute-start(bf16[2,256,512]{2,1,0:T(8,128)(2,1)} %b0.1), channel_id=1, source_target_pairs={{4,0},{8,4},{12,8},{16,12},{20,16},{24,20},{28,24},{32,28},{36,32}... | collective-permute-start | bytes 1572872 | tf_op jit(solution)/shard_map/ppermute | solution.py:18
  14.2 14.9 %collective-permute-start.3 = (bf16[2,256,512]{2,1,0:T(8,128)(2,1)S(1)}, bf16[2,256,512]{2,1,0:T(8,128)(2,1)S(1)}, u32[]{:S(2)}, u32[]{:S(2)}) collective-permute-start(bf16[2,256,512]{2,1,0:T(8,128)(2,1)S(1)} %collective-permute-done.b1), channel_id=1, source_target_pairs={{0,1},{1,2},{2,3},{3,0},{4,5},{5,6},{6,7},{7,4},{8,9},{9,10},{10,1... | collective-permute-start | bytes 1572872 | tf_op jit(solution)/shard_map/ppermute | solution.py:23
  14.2 39.4 %collective-permute-start.7 = (bf16[8,128,512]{2,1,0:T(8,128)(2,1)}, bf16[8,128,512]{2,1,0:T(8,128)(2,1)S(1)}, u32[]{:S(2)}, u32[]{:S(2)}) collective-permute-start(bf16[8,128,512]{2,1,0:T(8,128)(2,1)} %own.1), channel_id=1, source_target_pairs={{0,4},{4,8},{8,12},{12,16},{16,20},{20,24},{24,28},{28,32},{32,36}... | collective-permute-start | bytes 3145736 | tf_op jit(solution)/shard_map/ppermute | solution.py:18
  20.7 33.0 %collective-permute-start.8 = (bf16[8,128,512]{2,1,0:T(8,128)(2,1)}, bf16[8,128,512]{2,1,0:T(8,128)(2,1)S(1)}, u32[]{:S(2)}, u32[]{:S(2)}) collective-permute-start(bf16[8,128,512]{2,1,0:T(8,128)(2,1)} %own.1), channel_id=1, source_target_pairs={{4,0},{8,4},{12,8},{16,12},{20,16},{24,20},{28,24},{32,28},{36,32}... | collective-permute-start | bytes 3145736 | tf_op jit(solution)/shard_map/ppermute | solution.py:18
  22.6 21.2 %collective-permute-start.4 = (bf16[2,256,512]{2,1,0:T(8,128)(2,1)S(1)}, bf16[2,256,512]{2,1,0:T(8,128)(2,1)S(1)}, u32[]{:S(2)}, u32[]{:S(2)}) collective-permute-start(bf16[2,256,512]{2,1,0:T(8,128)(2,1)S(1)} %collective-permute-done.b1), channel_id=1, source_target_pairs={{4,0},{8,4},{12,8},{16,12},{20,16},{24,20},{28,24},{32,28},{36,32}... | collective-permute-start | bytes 1572872 | tf_op jit(solution)/shard_map/ppermute | solution.py:18
  24.6 20.6 %collective-permute-start.5 = (bf16[2,256,512]{2,1,0:T(8,128)(2,1)S(1)}, bf16[2,256,512]{2,1,0:T(8,128)(2,1)S(1)}, u32[]{:S(2)}, u32[]{:S(2)}) collective-permute-start(bf16[2,256,512]{2,1,0:T(8,128)(2,1)S(1)} %collective-permute-done.2.n0), channel_id=1, source_target_pairs={{4,7},{5,4},{6,5},{7,6},{12,15},{13,12},{14,13},{15,14},{20,23},{2... | collective-permute-start | bytes 1572872 | tf_op jit(solution)/shard_map/ppermute | solution.py:29
  29.2 24.5 %collective-permute-start.6 = (bf16[2,256,512]{2,1,0:T(8,128)(2,1)S(1)}, bf16[2,256,512]{2,1,0:T(8,128)(2,1)S(1)}, u32[]{:S(2)}, u32[]{:S(2)}) collective-permute-start(bf16[2,256,512]{2,1,0:T(8,128)(2,1)S(1)} %collective-permute-done.1.b2), channel_id=1, source_target_pairs={{4,0},{12,8},{20,16},{28,24},{36,32},{44,40},{52,48},{60,56},{68,6... | collective-permute-start | bytes 1572872 | tf_op jit(solution)/shard_map/ppermute | solution.py:34
  43.8 13.6 %collective-permute-start.10 = (bf16[2,256,512]{2,1,0:T(8,128)(2,1)S(1)}, bf16[2,256,512]{2,1,0:T(8,128)(2,1)S(1)}, u32[]{:S(2)}, u32[]{:S(2)}) collective-permute-start(bf16[2,256,512]{2,1,0:T(8,128)(2,1)S(1)} %collective-permute-done.3.b3), channel_id=1, source_target_pairs={{4,0},{12,8},{20,16},{28,24},{36,32},{44,40},{52,48},{60,56},{68,6... | collective-permute-start | bytes 1572872 | tf_op jit(solution)/shard_map/ppermute | solution.py:34
  45.2 12.2 %collective-permute-start.9 = (bf16[2,256,512]{2,1,0:T(8,128)(2,1)S(1)}, bf16[2,256,512]{2,1,0:T(8,128)(2,1)S(1)}, u32[]{:S(2)}, u32[]{:S(2)}) collective-permute-start(bf16[2,256,512]{2,1,0:T(8,128)(2,1)S(1)} %collective-permute-done.5.n2x), channel_id=1, source_target_pairs={{4,7},{5,4},{6,5},{7,6},{12,15},{13,12},{14,13},{15,14},{20,23},{2... | collective-permute-start | bytes 1572872 | tf_op jit(solution)/shard_map/ppermute | solution.py:29
  51.8 1.0 %copy-start.1 = (bf16[2,256,512]{2,1,0:T(8,128)(2,1)S(1)}, bf16[2,256,512]{2,1,0:T(8,128)(2,1)}, u32[]{:S(2)}) copy-start(bf16[2,256,512]{2,1,0:T(8,128)(2,1)} %b0.1) | copy-start | bytes 1572868
  52.9 1.2 %copy-start = (bf16[8,128,512]{2,1,0:T(8,128)(2,1)S(1)}, bf16[8,128,512]{2,1,0:T(8,128)(2,1)}, u32[]{:S(2)}) copy-start(bf16[8,128,512]{2,1,0:T(8,128)(2,1)} %own.1) | copy-start | bytes 3145732

commit v9 on v8

--- a/solution.py
+++ b/solution.py
@@ -100,8 +100,8 @@
 
 
 def middle_kernel(
-    ints, fock, occ, energies, base, b1, b2, b3, n1, n2x, n2c, prev, own, nxt,
-    part, wgt, acc, amps, sems,
+    orbs, cpl, fock_in, occ, energies, base, b1, b2, b3, n1, n2x, n2c, prev, own, nxt,
+    part, wgt, acc, amps, wide, fock, sems,
 ):
     pair_count, rows, width = part.shape
     orbitals = b1.shape[0]
@@ -109,14 +109,17 @@
         pltpu.make_async_copy(src, amps.at[pl.ds(k * pair_count, pair_count)], sems.at[k])
         for k, src in enumerate((prev, own, nxt))
     ]
+    wide[...] = fock_in[...].astype(jnp.float32)
+    table = pltpu.make_async_copy(wide, fock, sems.at[3])
+    table.start()
     for c in copies:
         c.start()
-    first = energies.shape[1] - width
+    first = 0
     mine = energies[:, pl.ds(pl.multiple_of(first + lax.axis_index("rep") * rows, rows), rows)]
     tile = jnp.transpose(jnp.broadcast_to(mine, (rows, rows)))
 
     def denominators(p, carry):
-        shift = occ[0, ints[0, p]] + occ[0, ints[1, p]]
+        shift = occ[orbs[0, p]] + occ[orbs[1, p]]
         for c in range(0, width, rows):
             row = energies[:, first + c:first + c + rows]
             wgt[p, :, c:c + rows] = damping / (tile + (row - shift))
@@ -125,14 +128,15 @@
     lax.fori_loop(0, pair_count, denominators, 0)
     products((b3,), [whole(b3)], acc, 0, base)
     products((b1, b2), [whole(n1), either(n2x, n2c)], acc, orbitals, base)
+    table.wait()
     for c in copies:
         c.wait()
     before = (lax.axis_index("orb") - 1) * pair_count
     step = 32
 
     def pair(p, carry):
-        i, j = pair_slot(ints, p, orbitals)
-        slots = [ints[2 + c, p] - before for c in range(fock.shape[0])]
+        i, j = pair_slot(orbs, p, orbitals)
+        slots = [cpl[c, p] - before for c in range(fock.shape[0])]
         scales = [fock[c, p] for c in range(fock.shape[0])]
         for r in range(0, rows, step):
             rs = pl.ds(r, step)
@@ -147,14 +151,16 @@
 
 
 def middle(*args):
-    base, own = args[4], args[-2]
+    base, own = args[5], args[-2]
     shape = jax.ShapeDtypeStruct(own.shape, jnp.float32)
     scratch = (
         pltpu.VMEM(base.shape, jnp.float32),
         pltpu.VMEM((3 * own.shape[0],) + own.shape[1:], own.dtype),
-        pltpu.SemaphoreType.DMA((3,)),
-    )
-    specs = [SMEM] * 3 + [VMEM] * 8 + [ANY] * 3
+        pltpu.VMEM(args[2].shape, jnp.float32),
+        pltpu.SMEM(args[2].shape, jnp.float32),
+        pltpu.SemaphoreType.DMA((4,)),
+    )
+    specs = [SMEM] * 2 + [VMEM, SMEM] + [VMEM] * 8 + [ANY] * 3
     return call(middle_kernel, (shape, shape), specs, scratch)(*args)
 
 
@@ -211,15 +217,13 @@
     n2c = odd_to_even(b2)
     n3x = along_rep_odd(n2x, -1)
     n3c = odd_to_even(b3)
-    fock = fock_coupling.T.astype(jnp.float32)
-    ints = jnp.concatenate([pair_orbitals.T, coupling.T], axis=0)
-    energies = jnp.concatenate([occupied_energy[None, :], virtual_energy[None, :]], axis=1)
+    orbs = pair_orbitals.T
     base = own_part(b0, b1, b2, n0)
     part, wgt = middle(
-        ints, fock, energies, energies, base, b1, b2, b3, n1, n2x, n2c,
-        amps_prev, amplitudes, amps_next,
-    )
-    return last_update(ints, part, wgt, b3, n3x, n3c)
+        orbs, coupling.T, fock_coupling.T, occupied_energy, virtual_energy[None, :], base,
+        b1, b2, b3, n1, n2x, n2c, amps_prev, amplitudes, amps_next,
+    )
+    return last_update(orbs, part, wgt, b3, n3x, n3c)
 
 
 def solution(mesh):

time: 59.9 us -> 58.8 us (0.982)
  the two profiles are of different devices: /device:TPU:97 before, /device:TPU:103 now
where the time goes in v9:
time: 58.8 us; the launch traced here: 58.5 us
  waiting for transfers between devices  27.2 us (46%)
  starting transfers between devices  24.1 us (41%)
  Pallas kernels  5.98 us (10%)
  local copies, waits for them, and re-layouts  1.06 us (2%)
    ppermute x4, waiting for transfers between devices, along_orb(): lax.ppermute(x, 'orb', [(i - distance, i) for i in range(n) if 0 <= i - d...  14.7 us
    ppermute x4, starting transfers between devices, along_orb(): lax.ppermute(x, 'orb', [(i - distance, i) for i in range(n) if 0 <= i - d...  13.4 us
    ppermute x3, waiting for transfers between devices, along_rep(): return lax.ppermute(x, 'rep', [(i, (i + distance) % n) for i in range(n)])  8.42 us
    ppermute x2, waiting for transfers between devices, along_rep_odd(): return lax.ppermute(x, ('orb', 'rep'), route)  4.01 us
    ppermute x2, starting transfers between devices, along_rep_odd(): return lax.ppermute(x, ('orb', 'rep'), route)  3.93 us
    ppermute x2, starting transfers between devices, odd_to_even(): return lax.ppermute(x, 'orb', [(o, o - 1) for o in range(1, n, 2)])  3.86 us
    pallas_call x1, Pallas kernels, middle(): return call(middle_kernel, (shape, shape), specs, scratch)(*args)  3.22 us
    ppermute x3, starting transfers between devices, along_rep(): return lax.ppermute(x, 'rep', [(i, (i + distance) % n) for i in range(n)])  2.87 us
  transfers between devices with their start and end apart: 11, of which 3 were waited for; matrix products, arithmetic and copies ran while one was open for 0% of the time, Pallas kernels for 7%

profile of v9, /device:TPU:103, one launch (start us, length us, event | category | flops | bytes accessed | tf_op | source)
XLA Modules:
  0.0 58.5 jit_solution(7592564319938080315)
XLA Ops:
  0.0 0.0 copy-start
  0.0 0.2 collective-permute-start
  0.2 1.3 %collective-permute-start.1 = (bf16[2,256,512]{2,1,0:T(8,128)(2,1)}, bf16[2,256,512]{2,1,0:T(8,128)(2,1)S(1)}, u32[]{:S(2)}, u32[]{:S(2)}) collective-permute-start(bf16[2,256,512]{2,1,0:T(8,128)(2,1)} %b0.1), channel_id=1, source_target_pairs={{0,3},{1,0},{2,1},{3,2},{4,7},{5,4},{6,5},{7,6},{8,11},{9,8},{10,9... | collective-permute-start | bytes 1572872 | tf_op jit(solution)/shard_map/ppermute | solution.py:23
  1.5 3.1 %collective-permute-start.2 = (bf16[2,256,512]{2,1,0:T(8,128)(2,1)}, bf16[2,256,512]{2,1,0:T(8,128)(2,1)S(1)}, u32[]{:S(2)}, u32[]{:S(2)}) collective-permute-start(bf16[2,256,512]{2,1,0:T(8,128)(2,1)} %b0.1), channel_id=1, source_target_pairs={{4,0},{8,4},{12,8},{16,12},{20,16},{24,20},{28,24},{32,28},{36,32}... | collective-permute-start | bytes 1572872 | tf_op jit(solution)/shard_map/ppermute | solution.py:18
  4.6 8.4 %collective-permute-done.b1 = bf16[2,256,512]{2,1,0:T(8,128)(2,1)S(1)} collective-permute-done((bf16[2,256,512]{2,1,0:T(8,128)(2,1)}, bf16[2,256,512]{2,1,0:T(8,128)(2,1)S(1)}, u32[]{:S(2)}, u32[]{:S(2)}) %collective-permute-start) | collective-permute-done | bytes 524320 | tf_op jit(solution)/shard_map/ppermute | solution.py:23
  13.0 1.4 %collective-permute-start.3 = (bf16[2,256,512]{2,1,0:T(8,128)(2,1)S(1)}, bf16[2,256,512]{2,1,0:T(8,128)(2,1)S(1)}, u32[]{:S(2)}, u32[]{:S(2)}) collective-permute-start(bf16[2,256,512]{2,1,0:T(8,128)(2,1)S(1)} %collective-permute-done.b1), channel_id=1, source_target_pairs={{0,1},{1,2},{2,3},{3,0},{4,5},{5,6},{6,7},{7,4},{8,9},{9,10},{10,1... | collective-permute-start | bytes 1572872 | tf_op jit(solution)/shard_map/ppermute | solution.py:23
  14.4 6.4 %collective-permute-start.7 = (bf16[8,128,512]{2,1,0:T(8,128)(2,1)}, bf16[8,128,512]{2,1,0:T(8,128)(2,1)S(1)}, u32[]{:S(2)}, u32[]{:S(2)}) collective-permute-start(bf16[8,128,512]{2,1,0:T(8,128)(2,1)} %own.1), channel_id=1, source_target_pairs={{0,4},{4,8},{8,12},{12,16},{16,20},{20,24},{24,28},{28,32},{32,36}... | collective-permute-start | bytes 3145736 | tf_op jit(solution)/shard_map/ppermute | solution.py:18
  20.9 1.9 %collective-permute-start.8 = (bf16[8,128,512]{2,1,0:T(8,128)(2,1)}, bf16[8,128,512]{2,1,0:T(8,128)(2,1)S(1)}, u32[]{:S(2)}, u32[]{:S(2)}) collective-permute-start(bf16[8,128,512]{2,1,0:T(8,128)(2,1)} %own.1), channel_id=1, source_target_pairs={{4,0},{8,4},{12,8},{16,12},{20,16},{24,20},{28,24},{32,28},{36,32}... | collective-permute-start | bytes 3145736 | tf_op jit(solution)/shard_map/ppermute | solution.py:18
  22.8 0.0 collective-permute-done.1.b2
  22.8 1.9 %collective-permute-start.4 = (bf16[2,256,512]{2,1,0:T(8,128)(2,1)S(1)}, bf16[2,256,512]{2,1,0:T(8,128)(2,1)S(1)}, u32[]{:S(2)}, u32[]{:S(2)}) collective-permute-start(bf16[2,256,512]{2,1,0:T(8,128)(2,1)S(1)} %collective-permute-done.b1), channel_id=1, source_target_pairs={{4,0},{8,4},{12,8},{16,12},{20,16},{24,20},{28,24},{32,28},{36,32}... | collective-permute-start | bytes 1572872 | tf_op jit(solution)/shard_map/ppermute | solution.py:18
  24.7 0.0 collective-permute-done.2.n0
  24.8 2.0 %collective-permute-start.5 = (bf16[2,256,512]{2,1,0:T(8,128)(2,1)S(1)}, bf16[2,256,512]{2,1,0:T(8,128)(2,1)S(1)}, u32[]{:S(2)}, u32[]{:S(2)}) collective-permute-start(bf16[2,256,512]{2,1,0:T(8,128)(2,1)S(1)} %collective-permute-done.2.n0), channel_id=1, source_target_pairs={{4,7},{5,4},{6,5},{7,6},{12,15},{13,12},{14,13},{15,14},{20,23},{2... | collective-permute-start | bytes 1572872 | tf_op jit(solution)/shard_map/ppermute | solution.py:29
  26.7 0.0 collective-permute-done.3.b3
  26.7 2.5 %collective-permute-start.6 = (bf16[2,256,512]{2,1,0:T(8,128)(2,1)S(1)}, bf16[2,256,512]{2,1,0:T(8,128)(2,1)S(1)}, u32[]{:S(2)}, u32[]{:S(2)}) collective-permute-start(bf16[2,256,512]{2,1,0:T(8,128)(2,1)S(1)} %collective-permute-done.1.b2), channel_id=1, source_target_pairs={{4,0},{12,8},{20,16},{28,24},{36,32},{44,40},{52,48},{60,56},{68,6... | collective-permute-start | bytes 1572872 | tf_op jit(solution)/shard_map/ppermute | solution.py:34
  29.3 14.7 %collective-permute-done.4.n1 = bf16[2,256,512]{2,1,0:T(8,128)(2,1)S(1)} collective-permute-done((bf16[2,256,512]{2,1,0:T(8,128)(2,1)S(1)}, bf16[2,256,512]{2,1,0:T(8,128)(2,1)S(1)}, u32[]{:S(2)}, u32[]{:S(2)}) %collective-permute-start.4) | collective-permute-done | bytes 524320 | tf_op jit(solution)/shard_map/ppermute | solution.py:18
  44.0 1.3 %collective-permute-start.10 = (bf16[2,256,512]{2,1,0:T(8,128)(2,1)S(1)}, bf16[2,256,512]{2,1,0:T(8,128)(2,1)S(1)}, u32[]{:S(2)}, u32[]{:S(2)}) collective-permute-start(bf16[2,256,512]{2,1,0:T(8,128)(2,1)S(1)} %collective-permute-done.3.b3), channel_id=1, source_target_pairs={{4,0},{12,8},{20,16},{28,24},{36,32},{44,40},{52,48},{60,56},{68,6... | collective-permute-start | bytes 1572872 | tf_op jit(solution)/shard_map/ppermute | solution.py:34
  45.4 0.0 collective-permute-done.5.n2x
  45.4 2.0 %collective-permute-start.9 = (bf16[2,256,512]{2,1,0:T(8,128)(2,1)S(1)}, bf16[2,256,512]{2,1,0:T(8,128)(2,1)S(1)}, u32[]{:S(2)}, u32[]{:S(2)}) collective-permute-start(bf16[2,256,512]{2,1,0:T(8,128)(2,1)S(1)} %collective-permute-done.5.n2x), channel_id=1, source_target_pairs={{4,7},{5,4},{6,5},{7,6},{12,15},{13,12},{14,13},{15,14},{20,23},{2... | collective-permute-start | bytes 1572872 | tf_op jit(solution)/shard_map/ppermute | solution.py:29
  47.3 0.0 copy-start.1
  47.3 1.0 %copy-done.1 = bf16[2,256,512]{2,1,0:T(8,128)(2,1)S(1)} copy-done((bf16[2,256,512]{2,1,0:T(8,128)(2,1)S(1)}, bf16[2,256,512]{2,1,0:T(8,128)(2,1)}, u32[]{:S(2)}) %copy-start.1) | copy-done | bytes 524312
  48.4 0.0 copy-start.2
  48.4 0.0 copy-start.3
  48.4 0.0 copy-start.4
  48.4 0.0 copy-start.5
  48.4 0.0 copy-start.6
  48.4 0.8 %shard_map.73.base = f32[2,4,128,512]{3,2,1,0:T(8,128)S(1)} custom-call(bf16[2,256,512]{2,1,0:T(8,128)(2,1)S(1)} %copy-done.1, bf16[2,256,512]{2,1,0:T(8,128)(2,1)S(1)} %collective-permute-done.b1, bf16[2,256,512]{2,1,0:T(8,128)(2,1)S(1)} %collective-permute-done.1.b2, bf16[2,256,512]{2,1,0:T(8,128)(2,1)S(1)} %collective-permute-done.2.n0), custom_call_target="tpu_custom_call" | custom-call | flops 100000000 | bytes 4194304 | tf_op jit(solution)/shard_map/pallas_call | solution.py:94
  49.2 0.0 collective-permute-done.6.n2c
  49.2 0.0 collective-permute-done.7.prev
  49.2 0.0 collective-permute-done.8.nxt
  49.2 0.0 copy-done
  49.2 0.0 copy-done.2
  49.2 0.0 copy-done.3
  49.2 0.0 copy-done.4
  49.2 0.0 copy-done.5
  49.2 0.0 copy-done.6
  49.3 3.2 %shard_map.74 = (f32[8,128,512]{2,1,0:T(8,128)S(1)}, f32[8,128,512]{2,1,0:T(8,128)S(1)}) custom-call(s32[2,8]{1,0:T(2,128)S(1)} %bitcast.4, s32[4,8]{1,0:T(4,128)S(1)} %bitcast.6, bf16[4,8]{1,0:T(4,128)(2,1)S(1)} %bitcast.8, f32[128]{0:T(128)S(1)} %copy-done.6, f32[1,512]{1,0:T(1,128)S(1)} %bitcast.7, f32[2,4,128,512]{3,2,1,0:T(8,128)S(1)} %shard_map.73.base, ...), custom_call_target="tpu_custom_call" | custom-call | flops 100000000 | bytes 4194304 | tf_op jit(solution)/shard_map/pallas_call | solution.py:164
  52.5 0.0 collective-permute-done.10.n3c
  52.5 4.0 %collective-permute-done.9.n3x = bf16[2,256,512]{2,1,0:T(8,128)(2,1)S(1)} collective-permute-done((bf16[2,256,512]{2,1,0:T(8,128)(2,1)S(1)}, bf16[2,256,512]{2,1,0:T(8,128)(2,1)S(1)}, u32[]{:S(2)}, u32[]{:S(2)}) %collective-permute-start.9) | collective-permute-done | bytes 524320 | tf_op jit(solution)/shard_map/ppermute | solution.py:29
  56.5 2.0 %shard_map.75 = bf16[8,128,512]{2,1,0:T(8,128)(2,1)} custom-call(s32[2,8]{1,0:T(2,128)S(1)} %bitcast.5, f32[8,128,512]{2,1,0:T(8,128)S(1)} %get-tuple-element.7.part, f32[8,128,512]{2,1,0:T(8,128)S(1)} %get-tuple-element.8.wgt, bf16[2,256,512]{2,1,0:T(8,128)(2,1)S(1)} %collective-permute-done.3.b3, bf16[2,256,512]{2,1,0:T(8,128)(2,1)S(1)} %collective-permute-done.9.n3x, ...), custom_call_target="tpu_custom_call" | custom-call | flops 100000000 | bytes 4194304 | tf_op jit(solution)/shard_map/pallas_call | solution.py:199
Async XLA Ops:
  0.0 49.2 %copy-start = (bf16[8,128,512]{2,1,0:T(8,128)(2,1)S(1)}, bf16[8,128,512]{2,1,0:T(8,128)(2,1)}, u32[]{:S(2)}) copy-start(bf16[8,128,512]{2,1,0:T(8,128)(2,1)} %own.1) | copy-start | bytes 3145732
  0.0 13.0 %collective-permute-start = (bf16[2,256,512]{2,1,0:T(8,128)(2,1)}, bf16[2,256,512]{2,1,0:T(8,128)(2,1)S(1)}, u32[]{:S(2)}, u32[]{:S(2)}) collective-permute-start(bf16[2,256,512]{2,1,0:T(8,128)(2,1)} %b0.1), channel_id=1, source_target_pairs={{0,1},{1,2},{2,3},{3,0},{4,5},{5,6},{6,7},{7,4},{8,9},{9,10},{10,1... | collective-permute-start | bytes 1572872 | tf_op jit(solution)/shard_map/ppermute | solution.py:23
  0.2 22.6 %collective-permute-start.1 = (bf16[2,256,512]{2,1,0:T(8,128)(2,1)}, bf16[2,256,512]{2,1,0:T(8,128)(2,1)S(1)}, u32[]{:S(2)}, u32[]{:S(2)}) collective-permute-start(bf16[2,256,512]{2,1,0:T(8,128)(2,1)} %b0.1), channel_id=1, source_target_pairs={{0,3},{1,0},{2,1},{3,2},{4,7},{5,4},{6,5},{7,6},{8,11},{9,8},{10,9... | collective-permute-start | bytes 1572872 | tf_op jit(solution)/shard_map/ppermute | solution.py:23
  1.5 23.3 %collective-permute-start.2 = (bf16[2,256,512]{2,1,0:T(8,128)(2,1)}, bf16[2,256,512]{2,1,0:T(8,128)(2,1)S(1)}, u32[]{:S(2)}, u32[]{:S(2)}) collective-permute-start(bf16[2,256,512]{2,1,0:T(8,128)(2,1)} %b0.1), channel_id=1, source_target_pairs={{4,0},{8,4},{12,8},{16,12},{20,16},{24,20},{28,24},{32,28},{36,32}... | collective-permute-start | bytes 1572872 | tf_op jit(solution)/shard_map/ppermute | solution.py:18
  13.0 13.7 %collective-permute-start.3 = (bf16[2,256,512]{2,1,0:T(8,128)(2,1)S(1)}, bf16[2,256,512]{2,1,0:T(8,128)(2,1)S(1)}, u32[]{:S(2)}, u32[]{:S(2)}) collective-permute-start(bf16[2,256,512]{2,1,0:T(8,128)(2,1)S(1)} %collective-permute-done.b1), channel_id=1, source_target_pairs={{0,1},{1,2},{2,3},{3,0},{4,5},{5,6},{6,7},{7,4},{8,9},{9,10},{10,1... | collective-permute-start | bytes 1572872 | tf_op jit(solution)/shard_map/ppermute | solution.py:23
  14.4 34.7 %collective-permute-start.7 = (bf16[8,128,512]{2,1,0:T(8,128)(2,1)}, bf16[8,128,512]{2,1,0:T(8,128)(2,1)S(1)}, u32[]{:S(2)}, u32[]{:S(2)}) collective-permute-start(bf16[8,128,512]{2,1,0:T(8,128)(2,1)} %own.1), channel_id=1, source_target_pairs={{0,4},{4,8},{8,12},{12,16},{16,20},{20,24},{24,28},{28,32},{32,36}... | collective-permute-start | bytes 3145736 | tf_op jit(solution)/shard_map/ppermute | solution.py:18
  20.9 28.3 %collective-permute-start.8 = (bf16[8,128,512]{2,1,0:T(8,128)(2,1)}, bf16[8,128,512]{2,1,0:T(8,128)(2,1)S(1)}, u32[]{:S(2)}, u32[]{:S(2)}) collective-permute-start(bf16[8,128,512]{2,1,0:T(8,128)(2,1)} %own.1), channel_id=1, source_target_pairs={{4,0},{8,4},{12,8},{16,12},{20,16},{24,20},{28,24},{32,28},{36,32}... | collective-permute-start | bytes 3145736 | tf_op jit(solution)/shard_map/ppermute | solution.py:18
  22.8 21.2 %collective-permute-start.4 = (bf16[2,256,512]{2,1,0:T(8,128)(2,1)S(1)}, bf16[2,256,512]{2,1,0:T(8,128)(2,1)S(1)}, u32[]{:S(2)}, u32[]{:S(2)}) collective-permute-start(bf16[2,256,512]{2,1,0:T(8,128)(2,1)S(1)} %collective-permute-done.b1), channel_id=1, source_target_pairs={{4,0},{8,4},{12,8},{16,12},{20,16},{24,20},{28,24},{32,28},{36,32}... | collective-permute-start | bytes 1572872 | tf_op jit(solution)/shard_map/ppermute | solution.py:18
  24.8 20.6 %collective-permute-start.5 = (bf16[2,256,512]{2,1,0:T(8,128)(2,1)S(1)}, bf16[2,256,512]{2,1,0:T(8,128)(2,1)S(1)}, u32[]{:S(2)}, u32[]{:S(2)}) collective-permute-start(bf16[2,256,512]{2,1,0:T(8,128)(2,1)S(1)} %collective-permute-done.2.n0), channel_id=1, source_target_pairs={{4,7},{5,4},{6,5},{7,6},{12,15},{13,12},{14,13},{15,14},{20,23},{2... | collective-permute-start | bytes 1572872 | tf_op jit(solution)/shard_map/ppermute | solution.py:29
  26.7 22.4 %collective-permute-start.6 = (bf16[2,256,512]{2,1,0:T(8,128)(2,1)S(1)}, bf16[2,256,512]{2,1,0:T(8,128)(2,1)S(1)}, u32[]{:S(2)}, u32[]{:S(2)}) collective-permute-start(bf16[2,256,512]{2,1,0:T(8,128)(2,1)S(1)} %collective-permute-done.1.b2), channel_id=1, source_target_pairs={{4,0},{12,8},{20,16},{28,24},{36,32},{44,40},{52,48},{60,56},{68,6... | collective-permute-start | bytes 1572872 | tf_op jit(solution)/shard_map/ppermute | solution.py:34
  44.0 8.4 %collective-permute-start.10 = (bf16[2,256,512]{2,1,0:T(8,128)(2,1)S(1)}, bf16[2,256,512]{2,1,0:T(8,128)(2,1)S(1)}, u32[]{:S(2)}, u32[]{:S(2)}) collective-permute-start(bf16[2,256,512]{2,1,0:T(8,128)(2,1)S(1)} %collective-permute-done.3.b3), channel_id=1, source_target_pairs={{4,0},{12,8},{20,16},{28,24},{36,32},{44,40},{52,48},{60,56},{68,6... | collective-permute-start | bytes 1572872 | tf_op jit(solution)/shard_map/ppermute | solution.py:34
  45.4 11.1 %collective-permute-start.9 = (bf16[2,256,512]{2,1,0:T(8,128)(2,1)S(1)}, bf16[2,256,512]{2,1,0:T(8,128)(2,1)S(1)}, u32[]{:S(2)}, u32[]{:S(2)}) collective-permute-start(bf16[2,256,512]{2,1,0:T(8,128)(2,1)S(1)} %collective-permute-done.5.n2x), channel_id=1, source_target_pairs={{4,7},{5,4},{6,5},{7,6},{12,15},{13,12},{14,13},{15,14},{20,23},{2... | collective-permute-start | bytes 1572872 | tf_op jit(solution)/shard_map/ppermute | solution.py:29
  47.3 1.0 %copy-start.1 = (bf16[2,256,512]{2,1,0:T(8,128)(2,1)S(1)}, bf16[2,256,512]{2,1,0:T(8,128)(2,1)}, u32[]{:S(2)}) copy-start(bf16[2,256,512]{2,1,0:T(8,128)(2,1)} %b0.1) | copy-start | bytes 1572868
  48.4 0.8 %copy-start.2 = (s32[8,2]{0,1:T(2,128)S(1)}, s32[8,2]{0,1:T(2,128)}, u32[]{:S(2)}) copy-start(s32[8,2]{0,1:T(2,128)} %param.9) | copy-start | bytes 196
  48.4 0.8 %copy-start.3 = (s32[8,4]{0,1:T(4,128)S(1)}, s32[8,4]{0,1:T(4,128)}, u32[]{:S(2)}) copy-start(s32[8,4]{0,1:T(4,128)} %param.10) | copy-start | bytes 388
  48.4 0.8 %copy-start.4 = (f32[512]{0:T(512)S(1)}, f32[512]{0:T(512)}, u32[]{:S(2)}) copy-start(f32[512]{0:T(512)} %param.12) | copy-start | bytes 6148
  48.4 0.8 %copy-start.5 = (bf16[8,4]{0,1:T(4,128)(2,1)S(1)}, bf16[8,4]{0,1:T(4,128)(2,1)}, u32[]{:S(2)}) copy-start(bf16[8,4]{0,1:T(4,128)(2,1)} %param.11) | copy-start | bytes 196
  48.4 0.9 %copy-start.6 = (f32[128]{0:T(128)S(1)}, f32[128]{0:T(128)}, u32[]{:S(2)}) copy-start(f32[128]{0:T(128)} %occ.1) | copy-start | bytes 1540

commit v10 on v9

--- a/solution.py
+++ b/solution.py
@@ -23,9 +23,11 @@
     return lax.ppermute(x, "rep", [(i, (i + distance) % n) for i in range(n)])
 
 
-def along_rep_odd(x, distance):
+def along_rep_some(x, distance, parity):
     n, m = lax.axis_size("orb"), lax.axis_size("rep")
-    route = [(o * m + i, o * m + (i + distance) % m) for o in range(1, n, 2) for i in range(m)]
+    route = [
+        (o * m + i, o * m + (i + distance) % m) for o in range(parity, n, 2) for i in range(m)
+    ]
     return lax.ppermute(x, ("orb", "rep"), route)
 
 
@@ -50,21 +52,17 @@
     return lax.dot_general(a, b, (((0,), (0,)), ((), ())), preferred_element_type=jnp.float32)
 
 
-def left_of(blocks, rows):
-    start = pl.multiple_of(lax.axis_index("rep") * rows, rows)
+def left_of(blocks, rows, orbitals):
+    part = pl.ds(pl.multiple_of(lax.axis_index("rep") * rows, rows), rows)
     return jnp.concatenate(
-        [
-            jnp.concatenate([b[i, :, pl.ds(start, rows)] for i in range(b.shape[0])], axis=1)
-            for b in blocks
-        ],
-        axis=0,
+        [jnp.concatenate([b(i, part) for i in range(orbitals)], axis=1) for b in blocks], axis=0
     )
 
 
 def products(left, right, out, offset=0, base=None):
     orbitals, _, rows, _ = out.shape
-    lhs = left_of(left, rows)
-    for j in range(left[0].shape[0]):
+    lhs = left_of(left, rows, orbitals)
+    for j in range(orbitals):
         both = dot_t(lhs, jnp.concatenate([r(j) for r in right], axis=0))
         for i in range(orbitals):
             part = both[i * rows:(i + 1) * rows]
@@ -78,18 +76,19 @@
 
 
 def whole(ref):
-    return lambda j: ref[j]
+    return lambda j, part=slice(None): ref[j, :, part]
 
 
 def either(odd_ref, even_ref):
     odd = lax.rem(lax.axis_index("orb"), 2) == 1
-    return lambda j: jnp.where(odd, odd_ref[j], even_ref[j])
+    return lambda j, part=slice(None): jnp.where(odd, odd_ref[j, :, part], even_ref[j, :, part])
 
 
 def own_part(b0, b1, b2, n0):
     def body(b0, b1, b2, n0, out):
-        products((b0, b1, b2), [whole(b) for b in (b0, b1, b2)], out)
-        products((b0,), [whole(n0)], out, b0.shape[0])
+        mine = [whole(b) for b in (b0, b1, b2)]
+        products(mine, mine, out)
+        products(mine[:1], [whole(n0)], out, b0.shape[0])
 
     return call(body, acc_shape(b0, 2), [VMEM] * 4)(b0, b1, b2, n0)
 
@@ -100,11 +99,11 @@
 
 
 def middle_kernel(
-    orbs, cpl, fock_in, occ, energies, base, b1, b2, b3, n1, n2x, n2c, prev, own, nxt,
+    orbs, cpl, fock_in, occ, energies, base, b2, b3e, b3o, n2x, n2c, prev, own, nxt,
     part, wgt, acc, amps, wide, fock, sems,
 ):
     pair_count, rows, width = part.shape
-    orbitals = b1.shape[0]
+    orbitals = b2.shape[0]
     copies = [
         pltpu.make_async_copy(src, amps.at[pl.ds(k * pair_count, pair_count)], sems.at[k])
         for k, src in enumerate((prev, own, nxt))
@@ -126,8 +125,9 @@
         return carry
 
     lax.fori_loop(0, pair_count, denominators, 0)
-    products((b3,), [whole(b3)], acc, 0, base)
-    products((b1, b2), [whole(n1), either(n2x, n2c)], acc, orbitals, base)
+    opposite = [either(b3o, b3e)]
+    products(opposite, opposite, acc, 0, base)
+    products([whole(b2)], [either(n2x, n2c)], acc, orbitals, base)
     table.wait()
     for c in copies:
         c.wait()
@@ -160,14 +160,14 @@
         pltpu.SMEM(args[2].shape, jnp.float32),
         pltpu.SemaphoreType.DMA((4,)),
     )
-    specs = [SMEM] * 2 + [VMEM, SMEM] + [VMEM] * 8 + [ANY] * 3
+    specs = [SMEM] * 2 + [VMEM, SMEM] + [VMEM] * 7 + [ANY] * 3
     return call(middle_kernel, (shape, shape), specs, scratch)(*args)
 
 
-def last_update(ints, part, wgt, b3, n3x, n3c):
-    def body(ints, part, wgt, b3, n3x, n3c, out, acc, done, sem):
+def last_update(ints, part, wgt, b1, b3e, b3o, n1, n3x, n3c):
+    def body(ints, part, wgt, b1, b3e, b3o, n1, n3x, n3c, out, acc, done, sem):
         orbitals = acc.shape[0]
-        products((b3,), [either(n3x, n3c)], acc)
+        products([whole(b1), either(b3o, b3e)], [whole(n1), either(n3x, n3c)], acc)
 
         def pair(p, carry):
             i, j = pair_slot(ints, p, orbitals)
@@ -190,7 +190,7 @@
         lax.fori_loop(0, done.shape[0], pair, 0)
         lax.fori_loop(0, done.shape[0], wait, 0)
 
-    acc = acc_shape(b3)
+    acc = acc_shape(b1)
     scratch = [
         pltpu.VMEM(acc.shape, acc.dtype),
         pltpu.VMEM(part.shape, jnp.bfloat16),
@@ -198,8 +198,8 @@
     ]
     return call(
         body, jax.ShapeDtypeStruct(part.shape, jnp.bfloat16),
-        [SMEM] + [VMEM] * 5, scratch, out_specs=ANY,
-    )(ints, part, wgt, b3, n3x, n3c)
+        [SMEM] + [VMEM] * 8, scratch, out_specs=ANY,
+    )(ints, part, wgt, b1, b3e, b3o, n1, n3x, n3c)
 
 
 def device_step(
@@ -211,19 +211,20 @@
     b2 = along_rep(b0, -1)
     amps_next = along_orb(amplitudes, -1)
     amps_prev = along_orb(amplitudes, 1)
-    n2x = along_rep_odd(n0, -1)
-    b3 = along_rep(b1, 1)
+    n2x = along_rep_some(n0, -1, 1)
+    b3e = along_rep_some(b1, 1, 0)
+    b3o = along_rep_some(b2, -1, 1)
     n1 = along_orb(b1, -1)
     n2c = odd_to_even(b2)
-    n3x = along_rep_odd(n2x, -1)
-    n3c = odd_to_even(b3)
+    n3x = along_rep_some(n2x, -1, 1)
+    n3c = odd_to_even(b3o)
     orbs = pair_orbitals.T
     base = own_part(b0, b1, b2, n0)
     part, wgt = middle(
         orbs, coupling.T, fock_coupling.T, occupied_energy, virtual_energy[None, :], base,
-        b1, b2, b3, n1, n2x, n2c, amps_prev, amplitudes, amps_next,
-    )
-    return last_update(orbs, part, wgt, b3, n3x, n3c)
+        b2, b3e, b3o, n2x, n2c, amps_prev, amplitudes, amps_next,
+    )
+    return last_update(orbs, part, wgt, b1, b3e, b3o, n1, n3x, n3c)
 
 
 def solution(mesh):

time: 58.8 us -> 57.7 us (0.981)
  the two profiles are of different devices: /device:TPU:103 before, /device:TPU:31 now
where the time goes in v10:
time: 57.7 us; the launch traced here: 57.4 us
  starting transfers between devices  34.9 us (60%)
  waiting for transfers between devices  15.1 us (26%)
  Pallas kernels  6.01 us (10%)
  local copies, waits for them, and re-layouts  1.06 us (2%)
    ppermute x4, starting transfers between devices, along_orb(): lax.ppermute(x, 'orb', [(i - distance, i) for i in range(n) if 0 <= i - d...  13.5 us
    ppermute x2, starting transfers between devices, odd_to_even(): return lax.ppermute(x, 'orb', [(o, o - 1) for o in range(1, n, 2)])  12.4 us
    ppermute x2, waiting for transfers between devices, along_rep(): return lax.ppermute(x, 'rep', [(i, (i + distance) % n) for i in range(n)])  8.42 us
    ppermute x4, waiting for transfers between devices, along_rep_some(): return lax.ppermute(x, ('orb', 'rep'), route)  6.7 us
    ppermute x4, starting transfers between devices, along_rep_some(): return lax.ppermute(x, ('orb', 'rep'), route)  6.43 us
    pallas_call x1, Pallas kernels, middle(): return call(middle_kernel, (shape, shape), specs, scratch)(*args)  3.13 us
    ppermute x2, starting transfers between devices, along_rep(): return lax.ppermute(x, 'rep', [(i, (i + distance) % n) for i in range(n)])  2.68 us
    pallas_call x1, Pallas kernels, last_update(): call(body, jax.ShapeDtypeStruct(part.shape, jnp.bfloat16), [SMEM] + [VMEM...  2.13 us
  transfers between devices with their start and end apart: 12, of which 3 were waited for; matrix products, arithmetic and copies ran while one was open for 0% of the time, Pallas kernels for 7%

profile of v10, /device:TPU:31, one launch (start us, length us, event | category | flops | bytes accessed | tf_op | source)
XLA Modules:
  0.0 57.4 jit_solution(5687347096957689579)
XLA Ops:
  0.0 0.0 copy-start
  0.0 0.5 collective-permute-start.1
  0.6 2.1 %collective-permute-start = (bf16[2,256,512]{2,1,0:T(8,128)(2,1)}, bf16[2,256,512]{2,1,0:T(8,128)(2,1)S(1)}, u32[]{:S(2)}, u32[]{:S(2)}) collective-permute-start(bf16[2,256,512]{2,1,0:T(8,128)(2,1)} %b0.1), channel_id=1, source_target_pairs={{0,1},{1,2},{2,3},{3,0},{4,5},{5,6},{6,7},{7,4},{8,9},{9,10},{10,1... | collective-permute-start | bytes 1572872 | tf_op jit(solution)/shard_map/ppermute | solution.py:23
  2.7 3.1 %collective-permute-start.2 = (bf16[2,256,512]{2,1,0:T(8,128)(2,1)}, bf16[2,256,512]{2,1,0:T(8,128)(2,1)S(1)}, u32[]{:S(2)}, u32[]{:S(2)}) collective-permute-start(bf16[2,256,512]{2,1,0:T(8,128)(2,1)} %b0.1), channel_id=1, source_target_pairs={{4,0},{8,4},{12,8},{16,12},{20,16},{24,20},{28,24},{32,28},{36,32}... | collective-permute-start | bytes 1572872 | tf_op jit(solution)/shard_map/ppermute | solution.py:18
  5.8 8.4 %collective-permute-done.1.b2 = bf16[2,256,512]{2,1,0:T(8,128)(2,1)S(1)} collective-permute-done((bf16[2,256,512]{2,1,0:T(8,128)(2,1)}, bf16[2,256,512]{2,1,0:T(8,128)(2,1)S(1)}, u32[]{:S(2)}, u32[]{:S(2)}) %collective-permute-start.1) | collective-permute-done | bytes 524320 | tf_op jit(solution)/shard_map/ppermute | solution.py:23
  14.2 1.9 %collective-permute-start.4 = (bf16[2,256,512]{2,1,0:T(8,128)(2,1)S(1)}, bf16[2,256,512]{2,1,0:T(8,128)(2,1)S(1)}, u32[]{:S(2)}, u32[]{:S(2)}) collective-permute-start(bf16[2,256,512]{2,1,0:T(8,128)(2,1)S(1)} %collective-permute-done.1.b2), channel_id=1, source_target_pairs={{4,7},{5,4},{6,5},{7,6},{12,15},{13,12},{14,13},{15,14},{20,23},{2... | collective-permute-start | bytes 1572872 | tf_op jit(solution)/shard_map/ppermute | solution.py:31
  16.1 3.7 %collective-permute-start.7 = (bf16[8,128,512]{2,1,0:T(8,128)(2,1)}, bf16[8,128,512]{2,1,0:T(8,128)(2,1)S(1)}, u32[]{:S(2)}, u32[]{:S(2)}) collective-permute-start(bf16[8,128,512]{2,1,0:T(8,128)(2,1)} %own.1), channel_id=1, source_target_pairs={{0,4},{4,8},{8,12},{12,16},{16,20},{20,24},{24,28},{28,32},{32,36}... | collective-permute-start | bytes 3145736 | tf_op jit(solution)/shard_map/ppermute | solution.py:18
  19.9 1.9 %collective-permute-start.8 = (bf16[8,128,512]{2,1,0:T(8,128)(2,1)}, bf16[8,128,512]{2,1,0:T(8,128)(2,1)S(1)}, u32[]{:S(2)}, u32[]{:S(2)}) collective-permute-start(bf16[8,128,512]{2,1,0:T(8,128)(2,1)} %own.1), channel_id=1, source_target_pairs={{4,0},{8,4},{12,8},{16,12},{20,16},{24,20},{28,24},{32,28},{36,32}... | collective-permute-start | bytes 3145736 | tf_op jit(solution)/shard_map/ppermute | solution.py:18
  21.8 0.0 collective-permute-done.b1
  21.8 0.7 %collective-permute-start.3 = (bf16[2,256,512]{2,1,0:T(8,128)(2,1)S(1)}, bf16[2,256,512]{2,1,0:T(8,128)(2,1)S(1)}, u32[]{:S(2)}, u32[]{:S(2)}) collective-permute-start(bf16[2,256,512]{2,1,0:T(8,128)(2,1)S(1)} %collective-permute-done.b1), channel_id=1, source_target_pairs={{0,1},{1,2},{2,3},{3,0},{8,9},{9,10},{10,11},{11,8},{16,17},{17,18... | collective-permute-start | bytes 1572872 | tf_op jit(solution)/shard_map/ppermute | solution.py:31
  22.5 0.0 collective-permute-done.2.n0
  22.5 10.4 %collective-permute-start.6 = (bf16[2,256,512]{2,1,0:T(8,128)(2,1)S(1)}, bf16[2,256,512]{2,1,0:T(8,128)(2,1)S(1)}, u32[]{:S(2)}, u32[]{:S(2)}) collective-permute-start(bf16[2,256,512]{2,1,0:T(8,128)(2,1)S(1)} %collective-permute-done.1.b2), channel_id=1, source_target_pairs={{4,0},{12,8},{20,16},{28,24},{36,32},{44,40},{52,48},{60,56},{68,6... | collective-permute-start | bytes 1572872 | tf_op jit(solution)/shard_map/ppermute | solution.py:36
  33.0 0.0 collective-permute-done.4.b3o
  33.0 1.9 %collective-permute-start.5 = (bf16[2,256,512]{2,1,0:T(8,128)(2,1)S(1)}, bf16[2,256,512]{2,1,0:T(8,128)(2,1)S(1)}, u32[]{:S(2)}, u32[]{:S(2)}) collective-permute-start(bf16[2,256,512]{2,1,0:T(8,128)(2,1)S(1)} %collective-permute-done.2.n0), channel_id=1, source_target_pairs={{4,7},{5,4},{6,5},{7,6},{12,15},{13,12},{14,13},{15,14},{20,23},{2... | collective-permute-start | bytes 1572872 | tf_op jit(solution)/shard_map/ppermute | solution.py:31
  34.9 0.0 collective-permute-done.3.b3e
  34.9 4.7 %collective-permute-start.9 = (bf16[2,256,512]{2,1,0:T(8,128)(2,1)S(1)}, bf16[2,256,512]{2,1,0:T(8,128)(2,1)S(1)}, u32[]{:S(2)}, u32[]{:S(2)}) collective-permute-start(bf16[2,256,512]{2,1,0:T(8,128)(2,1)S(1)} %collective-permute-done.b1), channel_id=1, source_target_pairs={{4,0},{8,4},{12,8},{16,12},{20,16},{24,20},{28,24},{32,28},{36,32}... | collective-permute-start | bytes 1572872 | tf_op jit(solution)/shard_map/ppermute | solution.py:18
  39.6 0.0 collective-permute-done.6.n2c
  39.6 1.9 %collective-permute-start.11 = (bf16[2,256,512]{2,1,0:T(8,128)(2,1)S(1)}, bf16[2,256,512]{2,1,0:T(8,128)(2,1)S(1)}, u32[]{:S(2)}, u32[]{:S(2)}) collective-permute-start(bf16[2,256,512]{2,1,0:T(8,128)(2,1)S(1)} %collective-permute-done.4.b3o), channel_id=1, source_target_pairs={{4,0},{12,8},{20,16},{28,24},{36,32},{44,40},{52,48},{60,56},{68,6... | collective-permute-start | bytes 1572872 | tf_op jit(solution)/shard_map/ppermute | solution.py:36
  41.6 2.6 %collective-permute-done.5.n2x = bf16[2,256,512]{2,1,0:T(8,128)(2,1)S(1)} collective-permute-done((bf16[2,256,512]{2,1,0:T(8,128)(2,1)S(1)}, bf16[2,256,512]{2,1,0:T(8,128)(2,1)S(1)}, u32[]{:S(2)}, u32[]{:S(2)}) %collective-permute-start.5) | collective-permute-done | bytes 524320 | tf_op jit(solution)/shard_map/ppermute | solution.py:31
  44.1 1.9 %collective-permute-start.10 = (bf16[2,256,512]{2,1,0:T(8,128)(2,1)S(1)}, bf16[2,256,512]{2,1,0:T(8,128)(2,1)S(1)}, u32[]{:S(2)}, u32[]{:S(2)}) collective-permute-start(bf16[2,256,512]{2,1,0:T(8,128)(2,1)S(1)} %collective-permute-done.5.n2x), channel_id=1, source_target_pairs={{4,7},{5,4},{6,5},{7,6},{12,15},{13,12},{14,13},{15,14},{20,23},{2... | collective-permute-start | bytes 1572872 | tf_op jit(solution)/shard_map/ppermute | solution.py:31
  46.0 0.0 copy-start.1
  46.0 1.0 %copy-done.1 = bf16[2,256,512]{2,1,0:T(8,128)(2,1)S(1)} copy-done((bf16[2,256,512]{2,1,0:T(8,128)(2,1)S(1)}, bf16[2,256,512]{2,1,0:T(8,128)(2,1)}, u32[]{:S(2)}) %copy-start.1) | copy-done | bytes 524312
  47.1 0.0 copy-start.2
  47.1 0.0 copy-start.3
  47.1 0.0 copy-start.4
  47.1 0.0 copy-start.5
  47.1 0.0 copy-start.6
  47.1 0.8 %shard_map.73.base = f32[2,4,128,512]{3,2,1,0:T(8,128)S(1)} custom-call(bf16[2,256,512]{2,1,0:T(8,128)(2,1)S(1)} %copy-done.1, bf16[2,256,512]{2,1,0:T(8,128)(2,1)S(1)} %collective-permute-done.b1, bf16[2,256,512]{2,1,0:T(8,128)(2,1)S(1)} %collective-permute-done.1.b2, bf16[2,256,512]{2,1,0:T(8,128)(2,1)S(1)} %collective-permute-done.2.n0), custom_call_target="tpu_custom_call" | custom-call | flops 100000000 | bytes 4194304 | tf_op jit(solution)/shard_map/pallas_call | solution.py:93
  47.9 0.0 collective-permute-done.7.prev
  47.9 0.0 collective-permute-done.8.nxt
  47.9 0.0 copy-done
  47.9 0.0 copy-done.2
  47.9 0.0 copy-done.3
  47.9 0.0 copy-done.4
  47.9 0.0 copy-done.5
  47.9 0.0 copy-done.6
  47.9 3.1 %shard_map.74 = (f32[8,128,512]{2,1,0:T(8,128)S(1)}, f32[8,128,512]{2,1,0:T(8,128)S(1)}) custom-call(s32[2,8]{1,0:T(2,128)S(1)} %bitcast.4, s32[4,8]{1,0:T(4,128)S(1)} %bitcast.6, bf16[4,8]{1,0:T(4,128)(2,1)S(1)} %bitcast.8, f32[128]{0:T(128)S(1)} %copy-done.6, f32[1,512]{1,0:T(1,128)S(1)} %bitcast.7, f32[2,4,128,512]{3,2,1,0:T(8,128)S(1)} %shard_map.73.base, ...), custom_call_target="tpu_custom_call" | custom-call | flops 100000000 | bytes 4194304 | tf_op jit(solution)/shard_map/pallas_call | solution.py:164
  51.1 0.0 collective-permute-done.9.n1
  51.1 0.0 collective-permute-done.11.n3c
  51.1 4.1 %collective-permute-done.10.n3x = bf16[2,256,512]{2,1,0:T(8,128)(2,1)S(1)} collective-permute-done((bf16[2,256,512]{2,1,0:T(8,128)(2,1)S(1)}, bf16[2,256,512]{2,1,0:T(8,128)(2,1)S(1)}, u32[]{:S(2)}, u32[]{:S(2)}) %collective-permute-start.10) | collective-permute-done | bytes 524320 | tf_op jit(solution)/shard_map/ppermute | solution.py:31
  55.2 2.1 %shard_map.75 = bf16[8,128,512]{2,1,0:T(8,128)(2,1)} custom-call(s32[2,8]{1,0:T(2,128)S(1)} %bitcast.5, f32[8,128,512]{2,1,0:T(8,128)S(1)} %get-tuple-element.7.part, f32[8,128,512]{2,1,0:T(8,128)S(1)} %get-tuple-element.8.wgt, bf16[2,256,512]{2,1,0:T(8,128)(2,1)S(1)} %collective-permute-done.b1, bf16[2,256,512]{2,1,0:T(8,128)(2,1)S(1)} %collective-permute-done.3.b3e, ...), custom_call_target="tpu_custom_call" | custom-call | flops 100000000 | bytes 4194304 | tf_op jit(solution)/shard_map/pallas_call | solution.py:199
Async XLA Ops:
  0.0 47.9 %copy-start = (bf16[8,128,512]{2,1,0:T(8,128)(2,1)S(1)}, bf16[8,128,512]{2,1,0:T(8,128)(2,1)}, u32[]{:S(2)}) copy-start(bf16[8,128,512]{2,1,0:T(8,128)(2,1)} %own.1) | copy-start | bytes 3145732
  0.0 14.2 %collective-permute-start.1 = (bf16[2,256,512]{2,1,0:T(8,128)(2,1)}, bf16[2,256,512]{2,1,0:T(8,128)(2,1)S(1)}, u32[]{:S(2)}, u32[]{:S(2)}) collective-permute-start(bf16[2,256,512]{2,1,0:T(8,128)(2,1)} %b0.1), channel_id=1, source_target_pairs={{0,3},{1,0},{2,1},{3,2},{4,7},{5,4},{6,5},{7,6},{8,11},{9,8},{10,9... | collective-permute-start | bytes 1572872 | tf_op jit(solution)/shard_map/ppermute | solution.py:23
  0.6 21.3 %collective-permute-start = (bf16[2,256,512]{2,1,0:T(8,128)(2,1)}, bf16[2,256,512]{2,1,0:T(8,128)(2,1)S(1)}, u32[]{:S(2)}, u32[]{:S(2)}) collective-permute-start(bf16[2,256,512]{2,1,0:T(8,128)(2,1)} %b0.1), channel_id=1, source_target_pairs={{0,1},{1,2},{2,3},{3,0},{4,5},{5,6},{6,7},{7,4},{8,9},{9,10},{10,1... | collective-permute-start | bytes 1572872 | tf_op jit(solution)/shard_map/ppermute | solution.py:23
  2.7 19.9 %collective-permute-start.2 = (bf16[2,256,512]{2,1,0:T(8,128)(2,1)}, bf16[2,256,512]{2,1,0:T(8,128)(2,1)S(1)}, u32[]{:S(2)}, u32[]{:S(2)}) collective-permute-start(bf16[2,256,512]{2,1,0:T(8,128)(2,1)} %b0.1), channel_id=1, source_target_pairs={{4,0},{8,4},{12,8},{16,12},{20,16},{24,20},{28,24},{32,28},{36,32}... | collective-permute-start | bytes 1572872 | tf_op jit(solution)/shard_map/ppermute | solution.py:18
  14.2 18.7 %collective-permute-start.4 = (bf16[2,256,512]{2,1,0:T(8,128)(2,1)S(1)}, bf16[2,256,512]{2,1,0:T(8,128)(2,1)S(1)}, u32[]{:S(2)}, u32[]{:S(2)}) collective-permute-start(bf16[2,256,512]{2,1,0:T(8,128)(2,1)S(1)} %collective-permute-done.1.b2), channel_id=1, source_target_pairs={{4,7},{5,4},{6,5},{7,6},{12,15},{13,12},{14,13},{15,14},{20,23},{2... | collective-permute-start | bytes 1572872 | tf_op jit(solution)/shard_map/ppermute | solution.py:31
  16.1 31.7 %collective-permute-start.7 = (bf16[8,128,512]{2,1,0:T(8,128)(2,1)}, bf16[8,128,512]{2,1,0:T(8,128)(2,1)S(1)}, u32[]{:S(2)}, u32[]{:S(2)}) collective-permute-start(bf16[8,128,512]{2,1,0:T(8,128)(2,1)} %own.1), channel_id=1, source_target_pairs={{0,4},{4,8},{8,12},{12,16},{16,20},{20,24},{24,28},{28,32},{32,36}... | collective-permute-start | bytes 3145736 | tf_op jit(solution)/shard_map/ppermute | solution.py:18
  19.9 28.0 %collective-permute-start.8 = (bf16[8,128,512]{2,1,0:T(8,128)(2,1)}, bf16[8,128,512]{2,1,0:T(8,128)(2,1)S(1)}, u32[]{:S(2)}, u32[]{:S(2)}) collective-permute-start(bf16[8,128,512]{2,1,0:T(8,128)(2,1)} %own.1), channel_id=1, source_target_pairs={{4,0},{8,4},{12,8},{16,12},{20,16},{24,20},{28,24},{32,28},{36,32}... | collective-permute-start | bytes 3145736 | tf_op jit(solution)/shard_map/ppermute | solution.py:18
  21.8 13.1 %collective-permute-start.3 = (bf16[2,256,512]{2,1,0:T(8,128)(2,1)S(1)}, bf16[2,256,512]{2,1,0:T(8,128)(2,1)S(1)}, u32[]{:S(2)}, u32[]{:S(2)}) collective-permute-start(bf16[2,256,512]{2,1,0:T(8,128)(2,1)S(1)} %collective-permute-done.b1), channel_id=1, source_target_pairs={{0,1},{1,2},{2,3},{3,0},{8,9},{9,10},{10,11},{11,8},{16,17},{17,18... | collective-permute-start | bytes 1572872 | tf_op jit(solution)/shard_map/ppermute | solution.py:31
  22.5 17.1 %collective-permute-start.6 = (bf16[2,256,512]{2,1,0:T(8,128)(2,1)S(1)}, bf16[2,256,512]{2,1,0:T(8,128)(2,1)S(1)}, u32[]{:S(2)}, u32[]{:S(2)}) collective-permute-start(bf16[2,256,512]{2,1,0:T(8,128)(2,1)S(1)} %collective-permute-done.1.b2), channel_id=1, source_target_pairs={{4,0},{12,8},{20,16},{28,24},{36,32},{44,40},{52,48},{60,56},{68,6... | collective-permute-start | bytes 1572872 | tf_op jit(solution)/shard_map/ppermute | solution.py:36
  33.0 11.1 %collective-permute-start.5 = (bf16[2,256,512]{2,1,0:T(8,128)(2,1)S(1)}, bf16[2,256,512]{2,1,0:T(8,128)(2,1)S(1)}, u32[]{:S(2)}, u32[]{:S(2)}) collective-permute-start(bf16[2,256,512]{2,1,0:T(8,128)(2,1)S(1)} %collective-permute-done.2.n0), channel_id=1, source_target_pairs={{4,7},{5,4},{6,5},{7,6},{12,15},{13,12},{14,13},{15,14},{20,23},{2... | collective-permute-start | bytes 1572872 | tf_op jit(solution)/shard_map/ppermute | solution.py:31
  34.9 16.2 %collective-permute-start.9 = (bf16[2,256,512]{2,1,0:T(8,128)(2,1)S(1)}, bf16[2,256,512]{2,1,0:T(8,128)(2,1)S(1)}, u32[]{:S(2)}, u32[]{:S(2)}) collective-permute-start(bf16[2,256,512]{2,1,0:T(8,128)(2,1)S(1)} %collective-permute-done.b1), channel_id=1, source_target_pairs={{4,0},{8,4},{12,8},{16,12},{20,16},{24,20},{28,24},{32,28},{36,32}... | collective-permute-start | bytes 1572872 | tf_op jit(solution)/shard_map/ppermute | solution.py:18
  39.6 11.5 %collective-permute-start.11 = (bf16[2,256,512]{2,1,0:T(8,128)(2,1)S(1)}, bf16[2,256,512]{2,1,0:T(8,128)(2,1)S(1)}, u32[]{:S(2)}, u32[]{:S(2)}) collective-permute-start(bf16[2,256,512]{2,1,0:T(8,128)(2,1)S(1)} %collective-permute-done.4.b3o), channel_id=1, source_target_pairs={{4,0},{12,8},{20,16},{28,24},{36,32},{44,40},{52,48},{60,56},{68,6... | collective-permute-start | bytes 1572872 | tf_op jit(solution)/shard_map/ppermute | solution.py:36
  44.1 11.1 %collective-permute-start.10 = (bf16[2,256,512]{2,1,0:T(8,128)(2,1)S(1)}, bf16[2,256,512]{2,1,0:T(8,128)(2,1)S(1)}, u32[]{:S(2)}, u32[]{:S(2)}) collective-permute-start(bf16[2,256,512]{2,1,0:T(8,128)(2,1)S(1)} %collective-permute-done.5.n2x), channel_id=1, source_target_pairs={{4,7},{5,4},{6,5},{7,6},{12,15},{13,12},{14,13},{15,14},{20,23},{2... | collective-permute-start | bytes 1572872 | tf_op jit(solution)/shard_map/ppermute | solution.py:31
  46.0 1.0 %copy-start.1 = (bf16[2,256,512]{2,1,0:T(8,128)(2,1)S(1)}, bf16[2,256,512]{2,1,0:T(8,128)(2,1)}, u32[]{:S(2)}) copy-start(bf16[2,256,512]{2,1,0:T(8,128)(2,1)} %b0.1) | copy-start | bytes 1572868
  47.1 0.8 %copy-start.2 = (s32[8,2]{0,1:T(2,128)S(1)}, s32[8,2]{0,1:T(2,128)}, u32[]{:S(2)}) copy-start(s32[8,2]{0,1:T(2,128)} %param.9) | copy-start | bytes 196
  47.1 0.8 %copy-start.3 = (s32[8,4]{0,1:T(4,128)S(1)}, s32[8,4]{0,1:T(4,128)}, u32[]{:S(2)}) copy-start(s32[8,4]{0,1:T(4,128)} %param.10) | copy-start | bytes 388
  47.1 0.8 %copy-start.4 = (f32[512]{0:T(512)S(1)}, f32[512]{0:T(512)}, u32[]{:S(2)}) copy-start(f32[512]{0:T(512)} %param.12) | copy-start | bytes 6148
  47.1 0.8 %copy-start.5 = (bf16[8,4]{0,1:T(4,128)(2,1)S(1)}, bf16[8,4]{0,1:T(4,128)(2,1)}, u32[]{:S(2)}) copy-start(bf16[8,4]{0,1:T(4,128)(2,1)} %param.11) | copy-start | bytes 196
  47.1 0.8 %copy-start.6 = (f32[128]{0:T(128)S(1)}, f32[128]{0:T(128)}, u32[]{:S(2)}) copy-start(f32[128]{0:T(128)} %occ.1) | copy-start | bytes 1540

commit v11 on v9

--- a/solution.py
+++ b/solution.py
@@ -100,11 +100,11 @@
 
 
 def middle_kernel(
-    orbs, cpl, fock_in, occ, energies, base, b1, b2, b3, n1, n2x, n2c, prev, own, nxt,
+    orbs, cpl, fock_in, occ, energies, base, b2, b3, n2x, n2c, prev, own, nxt,
     part, wgt, acc, amps, wide, fock, sems,
 ):
     pair_count, rows, width = part.shape
-    orbitals = b1.shape[0]
+    orbitals = b2.shape[0]
     copies = [
         pltpu.make_async_copy(src, amps.at[pl.ds(k * pair_count, pair_count)], sems.at[k])
         for k, src in enumerate((prev, own, nxt))
@@ -127,7 +127,7 @@
 
     lax.fori_loop(0, pair_count, denominators, 0)
     products((b3,), [whole(b3)], acc, 0, base)
-    products((b1, b2), [whole(n1), either(n2x, n2c)], acc, orbitals, base)
+    products((b2,), [either(n2x, n2c)], acc, orbitals, base)
     table.wait()
     for c in copies:
         c.wait()
@@ -160,14 +160,27 @@
         pltpu.SMEM(args[2].shape, jnp.float32),
         pltpu.SemaphoreType.DMA((4,)),
     )
-    specs = [SMEM] * 2 + [VMEM, SMEM] + [VMEM] * 8 + [ANY] * 3
+    specs = [SMEM] * 2 + [VMEM, SMEM] + [VMEM] * 6 + [ANY] * 3
     return call(middle_kernel, (shape, shape), specs, scratch)(*args)
 
 
-def last_update(ints, part, wgt, b3, n3x, n3c):
-    def body(ints, part, wgt, b3, n3x, n3c, out, acc, done, sem):
+def last_update(ints, part, wgt, b1, b3, n1, n3x, n3c):
+    def body(ints, part, wgt, b1, b3, n1, n3x, n3c, out, acc, done, sem):
         orbitals = acc.shape[0]
-        products((b3,), [either(n3x, n3c)], acc)
+        write = lambda p: pltpu.make_async_copy(done.at[p], out.at[p], sem.at[p])
+
+        def settled(p, carry):
+            _, j = pair_slot(ints, p, orbitals)
+
+            @pl.when(j < orbitals)
+            def _():
+                done[p] = part[p].astype(done.dtype)
+                write(p).start()
+
+            return carry
+
+        lax.fori_loop(0, done.shape[0], settled, 0)
+        products((b1, b3), [whole(n1), either(n3x, n3c)], acc)
 
         def pair(p, carry):
             i, j = pair_slot(ints, p, orbitals)
@@ -175,12 +188,8 @@
             @pl.when(j >= orbitals)
             def _():
                 done[p] = (part[p] - wgt[p] * acc[i, j - orbitals]).astype(done.dtype)
-
-            @pl.when(j < orbitals)
-            def _():
-                done[p] = part[p].astype(done.dtype)
-
-            pltpu.make_async_copy(done.at[p], out.at[p], sem.at[p]).start()
+                write(p).start()
+
             return carry
 
         def wait(p, carry):
@@ -198,8 +207,8 @@
     ]
     return call(
         body, jax.ShapeDtypeStruct(part.shape, jnp.bfloat16),
-        [SMEM] + [VMEM] * 5, scratch, out_specs=ANY,
-    )(ints, part, wgt, b3, n3x, n3c)
+        [SMEM] + [VMEM] * 7, scratch, out_specs=ANY,
+    )(ints, part, wgt, b1, b3, n1, n3x, n3c)
 
 
 def device_step(
@@ -221,9 +230,9 @@
     base = own_part(b0, b1, b2, n0)
     part, wgt = middle(
         orbs, coupling.T, fock_coupling.T, occupied_energy, virtual_energy[None, :], base,
-        b1, b2, b3, n1, n2x, n2c, amps_prev, amplitudes, amps_next,
-    )
-    return last_update(orbs, part, wgt, b3, n3x, n3c)
+        b2, b3, n2x, n2c, amps_prev, amplitudes, amps_next,
+    )
+    return last_update(orbs, part, wgt, b1, b3, n1, n3x, n3c)
 
 
 def solution(mesh):

time: 58.8 us -> 49.9 us (0.85)
  the two profiles are of different devices: /device:TPU:103 before, /device:TPU:25 now
where the time goes in v11:
time: 49.9 us; the launch traced here: 49.5 us
  starting transfers between devices  35.1 us (70%)
  waiting for transfers between devices  7.15 us (14%)
  Pallas kernels  6.04 us (12%)
  local copies, waits for them, and re-layouts  1.06 us (2%)
    ppermute x4, starting transfers between devices, along_orb(): lax.ppermute(x, 'orb', [(i - distance, i) for i in range(n) if 0 <= i - d...  18.9 us
    ppermute x2, starting transfers between devices, odd_to_even(): return lax.ppermute(x, 'orb', [(o, o - 1) for o in range(1, n, 2)])  6.83 us
    ppermute x2, starting transfers between devices, along_rep_odd(): return lax.ppermute(x, ('orb', 'rep'), route)  6.52 us
    ppermute x3, waiting for transfers between devices, along_rep(): return lax.ppermute(x, 'rep', [(i, (i + distance) % n) for i in range(n)])  4.21 us
    pallas_call x1, Pallas kernels, middle(): return call(middle_kernel, (shape, shape), specs, scratch)(*args)  3.1 us
    ppermute x2, waiting for transfers between devices, along_rep_odd(): return lax.ppermute(x, ('orb', 'rep'), route)  2.93 us
    ppermute x3, starting transfers between devices, along_rep(): return lax.ppermute(x, 'rep', [(i, (i + distance) % n) for i in range(n)])  2.84 us
    pallas_call x1, Pallas kernels, last_update(): call(body, jax.ShapeDtypeStruct(part.shape, jnp.bfloat16), [SMEM] + [VMEM...  2.19 us
  transfers between devices with their start and end apart: 11, of which 2 were waited for; matrix products, arithmetic and copies ran while one was open for 0% of the time, Pallas kernels for 8%

profile of v11, /device:TPU:25, one launch (start us, length us, event | category | flops | bytes accessed | tf_op | source)
XLA Modules:
  0.0 49.5 jit_solution(5426646549632932537)
XLA Ops:
  0.0 0.0 copy-start
  0.0 1.2 %collective-permute-start = (bf16[2,256,512]{2,1,0:T(8,128)(2,1)}, bf16[2,256,512]{2,1,0:T(8,128)(2,1)S(1)}, u32[]{:S(2)}, u32[]{:S(2)}) collective-permute-start(bf16[2,256,512]{2,1,0:T(8,128)(2,1)} %b0.1), channel_id=1, source_target_pairs={{0,1},{1,2},{2,3},{3,0},{4,5},{5,6},{6,7},{7,4},{8,9},{9,10},{10,1... | collective-permute-start | bytes 1572872 | tf_op jit(solution)/shard_map/ppermute | solution.py:23
  1.2 2.9 %collective-permute-start.2 = (bf16[2,256,512]{2,1,0:T(8,128)(2,1)}, bf16[2,256,512]{2,1,0:T(8,128)(2,1)S(1)}, u32[]{:S(2)}, u32[]{:S(2)}) collective-permute-start(bf16[2,256,512]{2,1,0:T(8,128)(2,1)} %b0.1), channel_id=1, source_target_pairs={{4,0},{8,4},{12,8},{16,12},{20,16},{24,20},{28,24},{32,28},{36,32}... | collective-permute-start | bytes 1572872 | tf_op jit(solution)/shard_map/ppermute | solution.py:18
  4.1 1.5 %collective-permute-start.1 = (bf16[2,256,512]{2,1,0:T(8,128)(2,1)}, bf16[2,256,512]{2,1,0:T(8,128)(2,1)S(1)}, u32[]{:S(2)}, u32[]{:S(2)}) collective-permute-start(bf16[2,256,512]{2,1,0:T(8,128)(2,1)} %b0.1), channel_id=1, source_target_pairs={{0,3},{1,0},{2,1},{3,2},{4,7},{5,4},{6,5},{7,6},{8,11},{9,8},{10,9... | collective-permute-start | bytes 1572872 | tf_op jit(solution)/shard_map/ppermute | solution.py:23
  5.6 3.7 %collective-permute-start.6 = (bf16[8,128,512]{2,1,0:T(8,128)(2,1)}, bf16[8,128,512]{2,1,0:T(8,128)(2,1)S(1)}, u32[]{:S(2)}, u32[]{:S(2)}) collective-permute-start(bf16[8,128,512]{2,1,0:T(8,128)(2,1)} %own.1), channel_id=1, source_target_pairs={{0,4},{4,8},{8,12},{12,16},{16,20},{20,24},{24,28},{28,32},{32,36}... | collective-permute-start | bytes 3145736 | tf_op jit(solution)/shard_map/ppermute | solution.py:18
  9.3 5.7 %collective-permute-start.7 = (bf16[8,128,512]{2,1,0:T(8,128)(2,1)}, bf16[8,128,512]{2,1,0:T(8,128)(2,1)S(1)}, u32[]{:S(2)}, u32[]{:S(2)}) collective-permute-start(bf16[8,128,512]{2,1,0:T(8,128)(2,1)} %own.1), channel_id=1, source_target_pairs={{4,0},{8,4},{12,8},{16,12},{20,16},{24,20},{28,24},{32,28},{36,32}... | collective-permute-start | bytes 3145736 | tf_op jit(solution)/shard_map/ppermute | solution.py:18
  15.1 0.0 collective-permute-done.b1
  15.1 0.1 collective-permute-start.3
  15.2 0.0 collective-permute-done.2.n0
  15.2 4.6 %collective-permute-start.4 = (bf16[2,256,512]{2,1,0:T(8,128)(2,1)S(1)}, bf16[2,256,512]{2,1,0:T(8,128)(2,1)S(1)}, u32[]{:S(2)}, u32[]{:S(2)}) collective-permute-start(bf16[2,256,512]{2,1,0:T(8,128)(2,1)S(1)} %collective-permute-done.2.n0), channel_id=1, source_target_pairs={{4,7},{5,4},{6,5},{7,6},{12,15},{13,12},{14,13},{15,14},{20,23},{2... | collective-permute-start | bytes 1572872 | tf_op jit(solution)/shard_map/ppermute | solution.py:29
  19.7 0.0 collective-permute-done.1.b2
  19.7 2.0 %collective-permute-start.5 = (bf16[2,256,512]{2,1,0:T(8,128)(2,1)S(1)}, bf16[2,256,512]{2,1,0:T(8,128)(2,1)S(1)}, u32[]{:S(2)}, u32[]{:S(2)}) collective-permute-start(bf16[2,256,512]{2,1,0:T(8,128)(2,1)S(1)} %collective-permute-done.1.b2), channel_id=1, source_target_pairs={{4,0},{12,8},{20,16},{28,24},{36,32},{44,40},{52,48},{60,56},{68,6... | collective-permute-start | bytes 1572872 | tf_op jit(solution)/shard_map/ppermute | solution.py:34
  21.8 4.2 %collective-permute-done.3.b3 = bf16[2,256,512]{2,1,0:T(8,128)(2,1)S(1)} collective-permute-done((bf16[2,256,512]{2,1,0:T(8,128)(2,1)S(1)}, bf16[2,256,512]{2,1,0:T(8,128)(2,1)S(1)}, u32[]{:S(2)}, u32[]{:S(2)}) %collective-permute-start.3) | collective-permute-done | bytes 524320 | tf_op jit(solution)/shard_map/ppermute | solution.py:23
  26.0 6.6 %collective-permute-start.8 = (bf16[2,256,512]{2,1,0:T(8,128)(2,1)S(1)}, bf16[2,256,512]{2,1,0:T(8,128)(2,1)S(1)}, u32[]{:S(2)}, u32[]{:S(2)}) collective-permute-start(bf16[2,256,512]{2,1,0:T(8,128)(2,1)S(1)} %collective-permute-done.b1), channel_id=1, source_target_pairs={{4,0},{8,4},{12,8},{16,12},{20,16},{24,20},{28,24},{32,28},{36,32}... | collective-permute-start | bytes 1572872 | tf_op jit(solution)/shard_map/ppermute | solution.py:18
  32.6 0.0 collective-permute-done.4.n2x
  32.6 4.8 %collective-permute-start.10 = (bf16[2,256,512]{2,1,0:T(8,128)(2,1)S(1)}, bf16[2,256,512]{2,1,0:T(8,128)(2,1)S(1)}, u32[]{:S(2)}, u32[]{:S(2)}) collective-permute-start(bf16[2,256,512]{2,1,0:T(8,128)(2,1)S(1)} %collective-permute-done.3.b3), channel_id=1, source_target_pairs={{4,0},{12,8},{20,16},{28,24},{36,32},{44,40},{52,48},{60,56},{68,6... | collective-permute-start | bytes 1572872 | tf_op jit(solution)/shard_map/ppermute | solution.py:34
  37.4 0.0 collective-permute-done.5.n2c
  37.4 2.0 %collective-permute-start.9 = (bf16[2,256,512]{2,1,0:T(8,128)(2,1)S(1)}, bf16[2,256,512]{2,1,0:T(8,128)(2,1)S(1)}, u32[]{:S(2)}, u32[]{:S(2)}) collective-permute-start(bf16[2,256,512]{2,1,0:T(8,128)(2,1)S(1)} %collective-permute-done.4.n2x), channel_id=1, source_target_pairs={{4,7},{5,4},{6,5},{7,6},{12,15},{13,12},{14,13},{15,14},{20,23},{2... | collective-permute-start | bytes 1572872 | tf_op jit(solution)/shard_map/ppermute | solution.py:29
  39.4 0.0 copy-start.1
  39.4 1.0 %copy-done.1 = bf16[2,256,512]{2,1,0:T(8,128)(2,1)S(1)} copy-done((bf16[2,256,512]{2,1,0:T(8,128)(2,1)S(1)}, bf16[2,256,512]{2,1,0:T(8,128)(2,1)}, u32[]{:S(2)}) %copy-start.1) | copy-done | bytes 524312
  40.4 0.0 copy-start.2
  40.4 0.0 copy-start.3
  40.4 0.0 copy-start.4
  40.4 0.0 copy-start.5
  40.4 0.0 copy-start.6
  40.5 0.8 %shard_map.73.base = f32[2,4,128,512]{3,2,1,0:T(8,128)S(1)} custom-call(bf16[2,256,512]{2,1,0:T(8,128)(2,1)S(1)} %copy-done.1, bf16[2,256,512]{2,1,0:T(8,128)(2,1)S(1)} %collective-permute-done.b1, bf16[2,256,512]{2,1,0:T(8,128)(2,1)S(1)} %collective-permute-done.1.b2, bf16[2,256,512]{2,1,0:T(8,128)(2,1)S(1)} %collective-permute-done.2.n0), custom_call_target="tpu_custom_call" | custom-call | flops 100000000 | bytes 4194304 | tf_op jit(solution)/shard_map/pallas_call | solution.py:94
  41.2 0.0 collective-permute-done.6.prev
  41.2 0.0 collective-permute-done.7.nxt
  41.2 0.0 copy-done
  41.2 0.0 copy-done.2
  41.3 0.0 copy-done.3
  41.3 0.0 copy-done.4
  41.3 0.0 copy-done.5
  41.3 0.0 copy-done.6
  41.3 3.1 %shard_map.74 = (f32[8,128,512]{2,1,0:T(8,128)S(1)}, f32[8,128,512]{2,1,0:T(8,128)S(1)}) custom-call(s32[2,8]{1,0:T(2,128)S(1)} %bitcast.4, s32[4,8]{1,0:T(4,128)S(1)} %bitcast.6, bf16[4,8]{1,0:T(4,128)(2,1)S(1)} %bitcast.8, f32[128]{0:T(128)S(1)} %copy-done.6, f32[1,512]{1,0:T(1,128)S(1)} %bitcast.7, f32[2,4,128,512]{3,2,1,0:T(8,128)S(1)} %shard_map.73.base, ...), custom_call_target="tpu_custom_call" | custom-call | flops 100000000 | bytes 4194304 | tf_op jit(solution)/shard_map/pallas_call | solution.py:164
  44.4 0.0 collective-permute-done.8.n1
  44.4 0.0 collective-permute-done.10.n3c
  44.4 2.9 %collective-permute-done.9.n3x = bf16[2,256,512]{2,1,0:T(8,128)(2,1)S(1)} collective-permute-done((bf16[2,256,512]{2,1,0:T(8,128)(2,1)S(1)}, bf16[2,256,512]{2,1,0:T(8,128)(2,1)S(1)}, u32[]{:S(2)}, u32[]{:S(2)}) %collective-permute-start.9) | collective-permute-done | bytes 524320 | tf_op jit(solution)/shard_map/ppermute | solution.py:29
  47.3 2.2 %shard_map.75 = bf16[8,128,512]{2,1,0:T(8,128)(2,1)} custom-call(s32[2,8]{1,0:T(2,128)S(1)} %bitcast.5, f32[8,128,512]{2,1,0:T(8,128)S(1)} %get-tuple-element.7.part, f32[8,128,512]{2,1,0:T(8,128)S(1)} %get-tuple-element.8.wgt, bf16[2,256,512]{2,1,0:T(8,128)(2,1)S(1)} %collective-permute-done.b1, bf16[2,256,512]{2,1,0:T(8,128)(2,1)S(1)} %collective-permute-done.3.b3, ...), custom_call_target="tpu_custom_call" | custom-call | flops 100000000 | bytes 4194304 | tf_op jit(solution)/shard_map/pallas_call | solution.py:208
Async XLA Ops:
  0.0 41.2 %copy-start = (bf16[8,128,512]{2,1,0:T(8,128)(2,1)S(1)}, bf16[8,128,512]{2,1,0:T(8,128)(2,1)}, u32[]{:S(2)}) copy-start(bf16[8,128,512]{2,1,0:T(8,128)(2,1)} %own.1) | copy-start | bytes 3145732
  0.0 15.1 %collective-permute-start = (bf16[2,256,512]{2,1,0:T(8,128)(2,1)}, bf16[2,256,512]{2,1,0:T(8,128)(2,1)S(1)}, u32[]{:S(2)}, u32[]{:S(2)}) collective-permute-start(bf16[2,256,512]{2,1,0:T(8,128)(2,1)} %b0.1), channel_id=1, source_target_pairs={{0,1},{1,2},{2,3},{3,0},{4,5},{5,6},{6,7},{7,4},{8,9},{9,10},{10,1... | collective-permute-start | bytes 1572872 | tf_op jit(solution)/shard_map/ppermute | solution.py:23
  1.2 13.9 %collective-permute-start.2 = (bf16[2,256,512]{2,1,0:T(8,128)(2,1)}, bf16[2,256,512]{2,1,0:T(8,128)(2,1)S(1)}, u32[]{:S(2)}, u32[]{:S(2)}) collective-permute-start(bf16[2,256,512]{2,1,0:T(8,128)(2,1)} %b0.1), channel_id=1, source_target_pairs={{4,0},{8,4},{12,8},{16,12},{20,16},{24,20},{28,24},{32,28},{36,32}... | collective-permute-start | bytes 1572872 | tf_op jit(solution)/shard_map/ppermute | solution.py:18
  4.1 15.7 %collective-permute-start.1 = (bf16[2,256,512]{2,1,0:T(8,128)(2,1)}, bf16[2,256,512]{2,1,0:T(8,128)(2,1)S(1)}, u32[]{:S(2)}, u32[]{:S(2)}) collective-permute-start(bf16[2,256,512]{2,1,0:T(8,128)(2,1)} %b0.1), channel_id=1, source_target_pairs={{0,3},{1,0},{2,1},{3,2},{4,7},{5,4},{6,5},{7,6},{8,11},{9,8},{10,9... | collective-permute-start | bytes 1572872 | tf_op jit(solution)/shard_map/ppermute | solution.py:23
  5.6 35.6 %collective-permute-start.6 = (bf16[8,128,512]{2,1,0:T(8,128)(2,1)}, bf16[8,128,512]{2,1,0:T(8,128)(2,1)S(1)}, u32[]{:S(2)}, u32[]{:S(2)}) collective-permute-start(bf16[8,128,512]{2,1,0:T(8,128)(2,1)} %own.1), channel_id=1, source_target_pairs={{0,4},{4,8},{8,12},{12,16},{16,20},{20,24},{24,28},{28,32},{32,36}... | collective-permute-start | bytes 3145736 | tf_op jit(solution)/shard_map/ppermute | solution.py:18
  9.3 31.9 %collective-permute-start.7 = (bf16[8,128,512]{2,1,0:T(8,128)(2,1)}, bf16[8,128,512]{2,1,0:T(8,128)(2,1)S(1)}, u32[]{:S(2)}, u32[]{:S(2)}) collective-permute-start(bf16[8,128,512]{2,1,0:T(8,128)(2,1)} %own.1), channel_id=1, source_target_pairs={{4,0},{8,4},{12,8},{16,12},{20,16},{24,20},{28,24},{32,28},{36,32}... | collective-permute-start | bytes 3145736 | tf_op jit(solution)/shard_map/ppermute | solution.py:18
  15.1 10.9 %collective-permute-start.3 = (bf16[2,256,512]{2,1,0:T(8,128)(2,1)S(1)}, bf16[2,256,512]{2,1,0:T(8,128)(2,1)S(1)}, u32[]{:S(2)}, u32[]{:S(2)}) collective-permute-start(bf16[2,256,512]{2,1,0:T(8,128)(2,1)S(1)} %collective-permute-done.b1), channel_id=1, source_target_pairs={{0,1},{1,2},{2,3},{3,0},{4,5},{5,6},{6,7},{7,4},{8,9},{9,10},{10,1... | collective-permute-start | bytes 1572872 | tf_op jit(solution)/shard_map/ppermute | solution.py:23
  15.2 17.4 %collective-permute-start.4 = (bf16[2,256,512]{2,1,0:T(8,128)(2,1)S(1)}, bf16[2,256,512]{2,1,0:T(8,128)(2,1)S(1)}, u32[]{:S(2)}, u32[]{:S(2)}) collective-permute-start(bf16[2,256,512]{2,1,0:T(8,128)(2,1)S(1)} %collective-permute-done.2.n0), channel_id=1, source_target_pairs={{4,7},{5,4},{6,5},{7,6},{12,15},{13,12},{14,13},{15,14},{20,23},{2... | collective-permute-start | bytes 1572872 | tf_op jit(solution)/shard_map/ppermute | solution.py:29
  19.7 17.7 %collective-permute-start.5 = (bf16[2,256,512]{2,1,0:T(8,128)(2,1)S(1)}, bf16[2,256,512]{2,1,0:T(8,128)(2,1)S(1)}, u32[]{:S(2)}, u32[]{:S(2)}) collective-permute-start(bf16[2,256,512]{2,1,0:T(8,128)(2,1)S(1)} %collective-permute-done.1.b2), channel_id=1, source_target_pairs={{4,0},{12,8},{20,16},{28,24},{36,32},{44,40},{52,48},{60,56},{68,6... | collective-permute-start | bytes 1572872 | tf_op jit(solution)/shard_map/ppermute | solution.py:34
  26.0 18.4 %collective-permute-start.8 = (bf16[2,256,512]{2,1,0:T(8,128)(2,1)S(1)}, bf16[2,256,512]{2,1,0:T(8,128)(2,1)S(1)}, u32[]{:S(2)}, u32[]{:S(2)}) collective-permute-start(bf16[2,256,512]{2,1,0:T(8,128)(2,1)S(1)} %collective-permute-done.b1), channel_id=1, source_target_pairs={{4,0},{8,4},{12,8},{16,12},{20,16},{24,20},{28,24},{32,28},{36,32}... | collective-permute-start | bytes 1572872 | tf_op jit(solution)/shard_map/ppermute | solution.py:18
  32.6 11.8 %collective-permute-start.10 = (bf16[2,256,512]{2,1,0:T(8,128)(2,1)S(1)}, bf16[2,256,512]{2,1,0:T(8,128)(2,1)S(1)}, u32[]{:S(2)}, u32[]{:S(2)}) collective-permute-start(bf16[2,256,512]{2,1,0:T(8,128)(2,1)S(1)} %collective-permute-done.3.b3), channel_id=1, source_target_pairs={{4,0},{12,8},{20,16},{28,24},{36,32},{44,40},{52,48},{60,56},{68,6... | collective-permute-start | bytes 1572872 | tf_op jit(solution)/shard_map/ppermute | solution.py:34
  37.4 9.9 %collective-permute-start.9 = (bf16[2,256,512]{2,1,0:T(8,128)(2,1)S(1)}, bf16[2,256,512]{2,1,0:T(8,128)(2,1)S(1)}, u32[]{:S(2)}, u32[]{:S(2)}) collective-permute-start(bf16[2,256,512]{2,1,0:T(8,128)(2,1)S(1)} %collective-permute-done.4.n2x), channel_id=1, source_target_pairs={{4,7},{5,4},{6,5},{7,6},{12,15},{13,12},{14,13},{15,14},{20,23},{2... | collective-permute-start | bytes 1572872 | tf_op jit(solution)/shard_map/ppermute | solution.py:29
  39.4 1.0 %copy-start.1 = (bf16[2,256,512]{2,1,0:T(8,128)(2,1)S(1)}, bf16[2,256,512]{2,1,0:T(8,128)(2,1)}, u32[]{:S(2)}) copy-start(bf16[2,256,512]{2,1,0:T(8,128)(2,1)} %b0.1) | copy-start | bytes 1572868
  40.4 0.8 %copy-start.2 = (s32[8,2]{0,1:T(2,128)S(1)}, s32[8,2]{0,1:T(2,128)}, u32[]{:S(2)}) copy-start(s32[8,2]{0,1:T(2,128)} %param.9) | copy-start | bytes 196
  40.4 0.8 %copy-start.3 = (s32[8,4]{0,1:T(4,128)S(1)}, s32[8,4]{0,1:T(4,128)}, u32[]{:S(2)}) copy-start(s32[8,4]{0,1:T(4,128)} %param.10) | copy-start | bytes 388
  40.4 0.8 %copy-start.4 = (f32[512]{0:T(512)S(1)}, f32[512]{0:T(512)}, u32[]{:S(2)}) copy-start(f32[512]{0:T(512)} %param.12) | copy-start | bytes 6148
  40.4 0.8 %copy-start.5 = (bf16[8,4]{0,1:T(4,128)(2,1)S(1)}, bf16[8,4]{0,1:T(4,128)(2,1)}, u32[]{:S(2)}) copy-start(bf16[8,4]{0,1:T(4,128)(2,1)} %param.11) | copy-start | bytes 196
  40.4 0.8 %copy-start.6 = (f32[128]{0:T(128)S(1)}, f32[128]{0:T(128)}, u32[]{:S(2)}) copy-start(f32[128]{0:T(128)} %occ.1) | copy-start | bytes 1540

commit v12 on v11

--- a/solution.py
+++ b/solution.py
@@ -167,36 +167,27 @@
 def last_update(ints, part, wgt, b1, b3, n1, n3x, n3c):
     def body(ints, part, wgt, b1, b3, n1, n3x, n3c, out, acc, done, sem):
         orbitals = acc.shape[0]
-        write = lambda p: pltpu.make_async_copy(done.at[p], out.at[p], sem.at[p])
-
-        def settled(p, carry):
-            _, j = pair_slot(ints, p, orbitals)
+        products((b1, b3), [whole(n1), either(n3x, n3c)], acc)
+
+        def pair(p, carry):
+            i, j = pair_slot(ints, p, orbitals)
+
+            @pl.when(j >= orbitals)
+            def _():
+                done[p] = (part[p] - wgt[p] * acc[i, j - orbitals]).astype(done.dtype)
 
             @pl.when(j < orbitals)
             def _():
                 done[p] = part[p].astype(done.dtype)
-                write(p).start()
-
-            return carry
-
-        lax.fori_loop(0, done.shape[0], settled, 0)
-        products((b1, b3), [whole(n1), either(n3x, n3c)], acc)
-
-        def pair(p, carry):
-            i, j = pair_slot(ints, p, orbitals)
-
-            @pl.when(j >= orbitals)
-            def _():
-                done[p] = (part[p] - wgt[p] * acc[i, j - orbitals]).astype(done.dtype)
-                write(p).start()
-
+
+            pltpu.make_async_copy(done.at[p], out.at[p], sem.at[p]).start()
             return carry
 
         def wait(p, carry):
             pltpu.make_async_copy(done.at[p], out.at[p], sem.at[p]).wait()
             return carry
 
-        lax.fori_loop(0, done.shape[0], pair, 0)
+        lax.fori_loop(0, done.shape[0], pair, 0, unroll=4)
         lax.fori_loop(0, done.shape[0], wait, 0)
 
     acc = acc_shape(b3)

time: 49.9 us -> 49.7 us (level)
  no operation moved by 1% of the time
where the time goes in v12:
time: 49.7 us; the launch traced here: 49.4 us
  starting transfers between devices  35.1 us (71%)
  waiting for transfers between devices  7.15 us (14%)
  Pallas kernels  5.94 us (12%)
  local copies, waits for them, and re-layouts  1.06 us (2%)
    ppermute x4, starting transfers between devices, along_orb(): lax.ppermute(x, 'orb', [(i - distance, i) for i in range(n) if 0 <= i - d...  18.9 us
    ppermute x2, starting transfers between devices, odd_to_even(): return lax.ppermute(x, 'orb', [(o, o - 1) for o in range(1, n, 2)])  6.83 us
    ppermute x2, starting transfers between devices, along_rep_odd(): return lax.ppermute(x, ('orb', 'rep'), route)  6.52 us
    ppermute x3, waiting for transfers between devices, along_rep(): return lax.ppermute(x, 'rep', [(i, (i + distance) % n) for i in range(n)])  4.21 us
    pallas_call x1, Pallas kernels, middle(): return call(middle_kernel, (shape, shape), specs, scratch)(*args)  3.1 us
    ppermute x2, waiting for transfers between devices, along_rep_odd(): return lax.ppermute(x, ('orb', 'rep'), route)  2.93 us
    ppermute x3, starting transfers between devices, along_rep(): return lax.ppermute(x, 'rep', [(i, (i + distance) % n) for i in range(n)])  2.84 us
    pallas_call x1, Pallas kernels, last_update(): call(body, jax.ShapeDtypeStruct(part.shape, jnp.bfloat16), [SMEM] + [VMEM...  2.09 us
  transfers between devices with their start and end apart: 11, of which 2 were waited for; matrix products, arithmetic and copies ran while one was open for 0% of the time, Pallas kernels for 8%

profile of v12, /device:TPU:25, one launch (start us, length us, event | category | flops | bytes accessed | tf_op | source)
XLA Modules:
  0.0 49.4 jit_solution(7353669192304050267)
XLA Ops:
  0.0 0.0 copy-start
  0.0 1.2 %collective-permute-start = (bf16[2,256,512]{2,1,0:T(8,128)(2,1)}, bf16[2,256,512]{2,1,0:T(8,128)(2,1)S(1)}, u32[]{:S(2)}, u32[]{:S(2)}) collective-permute-start(bf16[2,256,512]{2,1,0:T(8,128)(2,1)} %b0.1), channel_id=1, source_target_pairs={{0,1},{1,2},{2,3},{3,0},{4,5},{5,6},{6,7},{7,4},{8,9},{9,10},{10,1... | collective-permute-start | bytes 1572872 | tf_op jit(solution)/shard_map/ppermute | solution.py:23
  1.2 2.9 %collective-permute-start.2 = (bf16[2,256,512]{2,1,0:T(8,128)(2,1)}, bf16[2,256,512]{2,1,0:T(8,128)(2,1)S(1)}, u32[]{:S(2)}, u32[]{:S(2)}) collective-permute-start(bf16[2,256,512]{2,1,0:T(8,128)(2,1)} %b0.1), channel_id=1, source_target_pairs={{4,0},{8,4},{12,8},{16,12},{20,16},{24,20},{28,24},{32,28},{36,32}... | collective-permute-start | bytes 1572872 | tf_op jit(solution)/shard_map/ppermute | solution.py:18
  4.1 1.5 %collective-permute-start.1 = (bf16[2,256,512]{2,1,0:T(8,128)(2,1)}, bf16[2,256,512]{2,1,0:T(8,128)(2,1)S(1)}, u32[]{:S(2)}, u32[]{:S(2)}) collective-permute-start(bf16[2,256,512]{2,1,0:T(8,128)(2,1)} %b0.1), channel_id=1, source_target_pairs={{0,3},{1,0},{2,1},{3,2},{4,7},{5,4},{6,5},{7,6},{8,11},{9,8},{10,9... | collective-permute-start | bytes 1572872 | tf_op jit(solution)/shard_map/ppermute | solution.py:23
  5.6 3.7 %collective-permute-start.6 = (bf16[8,128,512]{2,1,0:T(8,128)(2,1)}, bf16[8,128,512]{2,1,0:T(8,128)(2,1)S(1)}, u32[]{:S(2)}, u32[]{:S(2)}) collective-permute-start(bf16[8,128,512]{2,1,0:T(8,128)(2,1)} %own.1), channel_id=1, source_target_pairs={{0,4},{4,8},{8,12},{12,16},{16,20},{20,24},{24,28},{28,32},{32,36}... | collective-permute-start | bytes 3145736 | tf_op jit(solution)/shard_map/ppermute | solution.py:18
  9.3 5.7 %collective-permute-start.7 = (bf16[8,128,512]{2,1,0:T(8,128)(2,1)}, bf16[8,128,512]{2,1,0:T(8,128)(2,1)S(1)}, u32[]{:S(2)}, u32[]{:S(2)}) collective-permute-start(bf16[8,128,512]{2,1,0:T(8,128)(2,1)} %own.1), channel_id=1, source_target_pairs={{4,0},{8,4},{12,8},{16,12},{20,16},{24,20},{28,24},{32,28},{36,32}... | collective-permute-start | bytes 3145736 | tf_op jit(solution)/shard_map/ppermute | solution.py:18
  15.1 0.0 collective-permute-done.b1
  15.1 0.1 collective-permute-start.3
  15.2 0.0 collective-permute-done.2.n0
  15.2 4.6 %collective-permute-start.4 = (bf16[2,256,512]{2,1,0:T(8,128)(2,1)S(1)}, bf16[2,256,512]{2,1,0:T(8,128)(2,1)S(1)}, u32[]{:S(2)}, u32[]{:S(2)}) collective-permute-start(bf16[2,256,512]{2,1,0:T(8,128)(2,1)S(1)} %collective-permute-done.2.n0), channel_id=1, source_target_pairs={{4,7},{5,4},{6,5},{7,6},{12,15},{13,12},{14,13},{15,14},{20,23},{2... | collective-permute-start | bytes 1572872 | tf_op jit(solution)/shard_map/ppermute | solution.py:29
  19.7 0.0 collective-permute-done.1.b2
  19.7 2.0 %collective-permute-start.5 = (bf16[2,256,512]{2,1,0:T(8,128)(2,1)S(1)}, bf16[2,256,512]{2,1,0:T(8,128)(2,1)S(1)}, u32[]{:S(2)}, u32[]{:S(2)}) collective-permute-start(bf16[2,256,512]{2,1,0:T(8,128)(2,1)S(1)} %collective-permute-done.1.b2), channel_id=1, source_target_pairs={{4,0},{12,8},{20,16},{28,24},{36,32},{44,40},{52,48},{60,56},{68,6... | collective-permute-start | bytes 1572872 | tf_op jit(solution)/shard_map/ppermute | solution.py:34
  21.8 4.2 %collective-permute-done.3.b3 = bf16[2,256,512]{2,1,0:T(8,128)(2,1)S(1)} collective-permute-done((bf16[2,256,512]{2,1,0:T(8,128)(2,1)S(1)}, bf16[2,256,512]{2,1,0:T(8,128)(2,1)S(1)}, u32[]{:S(2)}, u32[]{:S(2)}) %collective-permute-start.3) | collective-permute-done | bytes 524320 | tf_op jit(solution)/shard_map/ppermute | solution.py:23
  26.0 6.6 %collective-permute-start.8 = (bf16[2,256,512]{2,1,0:T(8,128)(2,1)S(1)}, bf16[2,256,512]{2,1,0:T(8,128)(2,1)S(1)}, u32[]{:S(2)}, u32[]{:S(2)}) collective-permute-start(bf16[2,256,512]{2,1,0:T(8,128)(2,1)S(1)} %collective-permute-done.b1), channel_id=1, source_target_pairs={{4,0},{8,4},{12,8},{16,12},{20,16},{24,20},{28,24},{32,28},{36,32}... | collective-permute-start | bytes 1572872 | tf_op jit(solution)/shard_map/ppermute | solution.py:18
  32.6 0.0 collective-permute-done.4.n2x
  32.6 4.8 %collective-permute-start.10 = (bf16[2,256,512]{2,1,0:T(8,128)(2,1)S(1)}, bf16[2,256,512]{2,1,0:T(8,128)(2,1)S(1)}, u32[]{:S(2)}, u32[]{:S(2)}) collective-permute-start(bf16[2,256,512]{2,1,0:T(8,128)(2,1)S(1)} %collective-permute-done.3.b3), channel_id=1, source_target_pairs={{4,0},{12,8},{20,16},{28,24},{36,32},{44,40},{52,48},{60,56},{68,6... | collective-permute-start | bytes 1572872 | tf_op jit(solution)/shard_map/ppermute | solution.py:34
  37.4 0.0 collective-permute-done.5.n2c
  37.4 2.0 %collective-permute-start.9 = (bf16[2,256,512]{2,1,0:T(8,128)(2,1)S(1)}, bf16[2,256,512]{2,1,0:T(8,128)(2,1)S(1)}, u32[]{:S(2)}, u32[]{:S(2)}) collective-permute-start(bf16[2,256,512]{2,1,0:T(8,128)(2,1)S(1)} %collective-permute-done.4.n2x), channel_id=1, source_target_pairs={{4,7},{5,4},{6,5},{7,6},{12,15},{13,12},{14,13},{15,14},{20,23},{2... | collective-permute-start | bytes 1572872 | tf_op jit(solution)/shard_map/ppermute | solution.py:29
  39.4 0.0 copy-start.1
  39.4 1.0 %copy-done.1 = bf16[2,256,512]{2,1,0:T(8,128)(2,1)S(1)} copy-done((bf16[2,256,512]{2,1,0:T(8,128)(2,1)S(1)}, bf16[2,256,512]{2,1,0:T(8,128)(2,1)}, u32[]{:S(2)}) %copy-start.1) | copy-done | bytes 524312
  40.4 0.0 copy-start.2
  40.4 0.0 copy-start.3
  40.4 0.0 copy-start.4
  40.4 0.0 copy-start.5
  40.4 0.0 copy-start.6
  40.5 0.8 %shard_map.73.base = f32[2,4,128,512]{3,2,1,0:T(8,128)S(1)} custom-call(bf16[2,256,512]{2,1,0:T(8,128)(2,1)S(1)} %copy-done.1, bf16[2,256,512]{2,1,0:T(8,128)(2,1)S(1)} %collective-permute-done.b1, bf16[2,256,512]{2,1,0:T(8,128)(2,1)S(1)} %collective-permute-done.1.b2, bf16[2,256,512]{2,1,0:T(8,128)(2,1)S(1)} %collective-permute-done.2.n0), custom_call_target="tpu_custom_call" | custom-call | flops 100000000 | bytes 4194304 | tf_op jit(solution)/shard_map/pallas_call | solution.py:94
  41.2 0.0 collective-permute-done.6.prev
  41.2 0.0 collective-permute-done.7.nxt
  41.2 0.0 copy-done
  41.2 0.0 copy-done.2
  41.3 0.0 copy-done.3
  41.3 0.0 copy-done.4
  41.3 0.0 copy-done.5
  41.3 0.0 copy-done.6
  41.3 3.1 %shard_map.74 = (f32[8,128,512]{2,1,0:T(8,128)S(1)}, f32[8,128,512]{2,1,0:T(8,128)S(1)}) custom-call(s32[2,8]{1,0:T(2,128)S(1)} %bitcast.4, s32[4,8]{1,0:T(4,128)S(1)} %bitcast.6, bf16[4,8]{1,0:T(4,128)(2,1)S(1)} %bitcast.8, f32[128]{0:T(128)S(1)} %copy-done.6, f32[1,512]{1,0:T(1,128)S(1)} %bitcast.7, f32[2,4,128,512]{3,2,1,0:T(8,128)S(1)} %shard_map.73.base, ...), custom_call_target="tpu_custom_call" | custom-call | flops 100000000 | bytes 4194304 | tf_op jit(solution)/shard_map/pallas_call | solution.py:164
  44.4 0.0 collective-permute-done.8.n1
  44.4 0.0 collective-permute-done.10.n3c
  44.4 2.9 %collective-permute-done.9.n3x = bf16[2,256,512]{2,1,0:T(8,128)(2,1)S(1)} collective-permute-done((bf16[2,256,512]{2,1,0:T(8,128)(2,1)S(1)}, bf16[2,256,512]{2,1,0:T(8,128)(2,1)S(1)}, u32[]{:S(2)}, u32[]{:S(2)}) %collective-permute-start.9) | collective-permute-done | bytes 524320 | tf_op jit(solution)/shard_map/ppermute | solution.py:29
  47.3 2.1 %shard_map.75 = bf16[8,128,512]{2,1,0:T(8,128)(2,1)} custom-call(s32[2,8]{1,0:T(2,128)S(1)} %bitcast.5, f32[8,128,512]{2,1,0:T(8,128)S(1)} %get-tuple-element.7.part, f32[8,128,512]{2,1,0:T(8,128)S(1)} %get-tuple-element.8.wgt, bf16[2,256,512]{2,1,0:T(8,128)(2,1)S(1)} %collective-permute-done.b1, bf16[2,256,512]{2,1,0:T(8,128)(2,1)S(1)} %collective-permute-done.3.b3, ...), custom_call_target="tpu_custom_call" | custom-call | flops 100000000 | bytes 4194304 | tf_op jit(solution)/shard_map/pallas_call | solution.py:199
Async XLA Ops:
  0.0 41.2 %copy-start = (bf16[8,128,512]{2,1,0:T(8,128)(2,1)S(1)}, bf16[8,128,512]{2,1,0:T(8,128)(2,1)}, u32[]{:S(2)}) copy-start(bf16[8,128,512]{2,1,0:T(8,128)(2,1)} %own.1) | copy-start | bytes 3145732
  0.0 15.1 %collective-permute-start = (bf16[2,256,512]{2,1,0:T(8,128)(2,1)}, bf16[2,256,512]{2,1,0:T(8,128)(2,1)S(1)}, u32[]{:S(2)}, u32[]{:S(2)}) collective-permute-start(bf16[2,256,512]{2,1,0:T(8,128)(2,1)} %b0.1), channel_id=1, source_target_pairs={{0,1},{1,2},{2,3},{3,0},{4,5},{5,6},{6,7},{7,4},{8,9},{9,10},{10,1... | collective-permute-start | bytes 1572872 | tf_op jit(solution)/shard_map/ppermute | solution.py:23
  1.2 13.9 %collective-permute-start.2 = (bf16[2,256,512]{2,1,0:T(8,128)(2,1)}, bf16[2,256,512]{2,1,0:T(8,128)(2,1)S(1)}, u32[]{:S(2)}, u32[]{:S(2)}) collective-permute-start(bf16[2,256,512]{2,1,0:T(8,128)(2,1)} %b0.1), channel_id=1, source_target_pairs={{4,0},{8,4},{12,8},{16,12},{20,16},{24,20},{28,24},{32,28},{36,32}... | collective-permute-start | bytes 1572872 | tf_op jit(solution)/shard_map/ppermute | solution.py:18
  4.1 15.7 %collective-permute-start.1 = (bf16[2,256,512]{2,1,0:T(8,128)(2,1)}, bf16[2,256,512]{2,1,0:T(8,128)(2,1)S(1)}, u32[]{:S(2)}, u32[]{:S(2)}) collective-permute-start(bf16[2,256,512]{2,1,0:T(8,128)(2,1)} %b0.1), channel_id=1, source_target_pairs={{0,3},{1,0},{2,1},{3,2},{4,7},{5,4},{6,5},{7,6},{8,11},{9,8},{10,9... | collective-permute-start | bytes 1572872 | tf_op jit(solution)/shard_map/ppermute | solution.py:23
  5.6 35.6 %collective-permute-start.6 = (bf16[8,128,512]{2,1,0:T(8,128)(2,1)}, bf16[8,128,512]{2,1,0:T(8,128)(2,1)S(1)}, u32[]{:S(2)}, u32[]{:S(2)}) collective-permute-start(bf16[8,128,512]{2,1,0:T(8,128)(2,1)} %own.1), channel_id=1, source_target_pairs={{0,4},{4,8},{8,12},{12,16},{16,20},{20,24},{24,28},{28,32},{32,36}... | collective-permute-start | bytes 3145736 | tf_op jit(solution)/shard_map/ppermute | solution.py:18
  9.3 31.9 %collective-permute-start.7 = (bf16[8,128,512]{2,1,0:T(8,128)(2,1)}, bf16[8,128,512]{2,1,0:T(8,128)(2,1)S(1)}, u32[]{:S(2)}, u32[]{:S(2)}) collective-permute-start(bf16[8,128,512]{2,1,0:T(8,128)(2,1)} %own.1), channel_id=1, source_target_pairs={{4,0},{8,4},{12,8},{16,12},{20,16},{24,20},{28,24},{32,28},{36,32}... | collective-permute-start | bytes 3145736 | tf_op jit(solution)/shard_map/ppermute | solution.py:18
  15.1 10.9 %collective-permute-start.3 = (bf16[2,256,512]{2,1,0:T(8,128)(2,1)S(1)}, bf16[2,256,512]{2,1,0:T(8,128)(2,1)S(1)}, u32[]{:S(2)}, u32[]{:S(2)}) collective-permute-start(bf16[2,256,512]{2,1,0:T(8,128)(2,1)S(1)} %collective-permute-done.b1), channel_id=1, source_target_pairs={{0,1},{1,2},{2,3},{3,0},{4,5},{5,6},{6,7},{7,4},{8,9},{9,10},{10,1... | collective-permute-start | bytes 1572872 | tf_op jit(solution)/shard_map/ppermute | solution.py:23
  15.2 17.4 %collective-permute-start.4 = (bf16[2,256,512]{2,1,0:T(8,128)(2,1)S(1)}, bf16[2,256,512]{2,1,0:T(8,128)(2,1)S(1)}, u32[]{:S(2)}, u32[]{:S(2)}) collective-permute-start(bf16[2,256,512]{2,1,0:T(8,128)(2,1)S(1)} %collective-permute-done.2.n0), channel_id=1, source_target_pairs={{4,7},{5,4},{6,5},{7,6},{12,15},{13,12},{14,13},{15,14},{20,23},{2... | collective-permute-start | bytes 1572872 | tf_op jit(solution)/shard_map/ppermute | solution.py:29
  19.7 17.7 %collective-permute-start.5 = (bf16[2,256,512]{2,1,0:T(8,128)(2,1)S(1)}, bf16[2,256,512]{2,1,0:T(8,128)(2,1)S(1)}, u32[]{:S(2)}, u32[]{:S(2)}) collective-permute-start(bf16[2,256,512]{2,1,0:T(8,128)(2,1)S(1)} %collective-permute-done.1.b2), channel_id=1, source_target_pairs={{4,0},{12,8},{20,16},{28,24},{36,32},{44,40},{52,48},{60,56},{68,6... | collective-permute-start | bytes 1572872 | tf_op jit(solution)/shard_map/ppermute | solution.py:34
  26.0 18.4 %collective-permute-start.8 = (bf16[2,256,512]{2,1,0:T(8,128)(2,1)S(1)}, bf16[2,256,512]{2,1,0:T(8,128)(2,1)S(1)}, u32[]{:S(2)}, u32[]{:S(2)}) collective-permute-start(bf16[2,256,512]{2,1,0:T(8,128)(2,1)S(1)} %collective-permute-done.b1), channel_id=1, source_target_pairs={{4,0},{8,4},{12,8},{16,12},{20,16},{24,20},{28,24},{32,28},{36,32}... | collective-permute-start | bytes 1572872 | tf_op jit(solution)/shard_map/ppermute | solution.py:18
  32.6 11.8 %collective-permute-start.10 = (bf16[2,256,512]{2,1,0:T(8,128)(2,1)S(1)}, bf16[2,256,512]{2,1,0:T(8,128)(2,1)S(1)}, u32[]{:S(2)}, u32[]{:S(2)}) collective-permute-start(bf16[2,256,512]{2,1,0:T(8,128)(2,1)S(1)} %collective-permute-done.3.b3), channel_id=1, source_target_pairs={{4,0},{12,8},{20,16},{28,24},{36,32},{44,40},{52,48},{60,56},{68,6... | collective-permute-start | bytes 1572872 | tf_op jit(solution)/shard_map/ppermute | solution.py:34
  37.4 9.9 %collective-permute-start.9 = (bf16[2,256,512]{2,1,0:T(8,128)(2,1)S(1)}, bf16[2,256,512]{2,1,0:T(8,128)(2,1)S(1)}, u32[]{:S(2)}, u32[]{:S(2)}) collective-permute-start(bf16[2,256,512]{2,1,0:T(8,128)(2,1)S(1)} %collective-permute-done.4.n2x), channel_id=1, source_target_pairs={{4,7},{5,4},{6,5},{7,6},{12,15},{13,12},{14,13},{15,14},{20,23},{2... | collective-permute-start | bytes 1572872 | tf_op jit(solution)/shard_map/ppermute | solution.py:29
  39.4 1.0 %copy-start.1 = (bf16[2,256,512]{2,1,0:T(8,128)(2,1)S(1)}, bf16[2,256,512]{2,1,0:T(8,128)(2,1)}, u32[]{:S(2)}) copy-start(bf16[2,256,512]{2,1,0:T(8,128)(2,1)} %b0.1) | copy-start | bytes 1572868
  40.4 0.8 %copy-start.2 = (s32[8,2]{0,1:T(2,128)S(1)}, s32[8,2]{0,1:T(2,128)}, u32[]{:S(2)}) copy-start(s32[8,2]{0,1:T(2,128)} %param.9) | copy-start | bytes 196
  40.4 0.8 %copy-start.3 = (s32[8,4]{0,1:T(4,128)S(1)}, s32[8,4]{0,1:T(4,128)}, u32[]{:S(2)}) copy-start(s32[8,4]{0,1:T(4,128)} %param.10) | copy-start | bytes 388
  40.4 0.8 %copy-start.4 = (f32[512]{0:T(512)S(1)}, f32[512]{0:T(512)}, u32[]{:S(2)}) copy-start(f32[512]{0:T(512)} %param.12) | copy-start | bytes 6148
  40.4 0.8 %copy-start.5 = (bf16[8,4]{0,1:T(4,128)(2,1)S(1)}, bf16[8,4]{0,1:T(4,128)(2,1)}, u32[]{:S(2)}) copy-start(bf16[8,4]{0,1:T(4,128)(2,1)} %param.11) | copy-start | bytes 196
  40.4 0.8 %copy-start.6 = (f32[128]{0:T(128)S(1)}, f32[128]{0:T(128)}, u32[]{:S(2)}) copy-start(f32[128]{0:T(128)} %occ.1) | copy-start | bytes 1540
